TPU v7x, 32 devices: a whole 2x2x4 slice. The times are simulated.
32 devices in a mesh: gx: 8 (over z, x), gy: 4 (over y, core).
Axes of the slice: x: 2, y: 2, z: 4, core: 2. Of those that a mesh axis runs over, the one named last changes fastest.
Arguments:
- positions: float32 [3, 1048576], P(None, ('gx', 'gy')), may hold values from -5 to 5, as said below
- noise: float32 [3, 1048576], P(None, ('gx', 'gy')), may hold values from -0.6 to 0.6
- route: int32 [1048576], P(('gx', 'gy')), may hold values from 0 to 65535, as said below
- node_perm: int32 [8, 4, 65536], P(None, 'gy'), may hold values from 0 to 65535, each once within a row
- pair_first: int32 [32, 1024], P(('gx', 'gy')), may hold values from 0 to 1023
- pair_second: int32 [32, 1024], P(('gx', 'gy')), may hold values from 0 to 2047
- pair_count: int32 [32], P(('gx', 'gy')), may hold values from 512 to 1024, as said below
Outputs:
- moved: float32 [3, 1048576], P(None, ('gx', 'gy'))
- drift: float32 [3, 1048576], P(None, ('gx', 'gy'))
Inputs may be any that keep to these rules, and one draw needn't show every extreme that they name: `positions`: consecutive beads of a chain lie between 0.25 and 0.95 apart. `route`: within one device the values are distinct and rise along its beads; at most 2048 beads of one device go to one device, and every device sends exactly 2048 beads to some device. `pair_count`: some device's count is 1024.
All inputs are finite; a program needn't handle non-finite values.
Results may differ from a plain program's by a relative error of at most 0.015.
Values sent between devices are 32-bit elements; how exact they have to be, the bound alone decides.
No kernel may reach another device: no remote copies, remote signals or barrier semaphores. Data moves between devices by JAX's collectives and lax.ppermute only.
A program may use at most 192 MiB of HBM per device.

v0:
```python
from functools import partial
import math

import jax
import jax.numpy as jnp
from jax import lax
from jax.sharding import PartitionSpec as P

G = 128
BEAD_CH = 64
CELL = 64


bead_radius = 0.5
split_xi = 0.5
time_step = 0.01
fene_k = 30.0
fene_reach = 1.5
bend_k = 2.0
grid_spacing = 4.0
pair_block = 64


def shifted(value, axis, by):
    devices = lax.axis_size(axis)
    return lax.ppermute(value, axis, [(i, (i + by) % devices) for i in range(devices)])


def bonded_forces(positions):
    chains = positions.reshape(3, -1, BEAD_CH)

    def energy(coords):
        bond = coords[:, :, 1:] - coords[:, :, :-1]
        square = jnp.sum(bond * bond, axis=0)
        stretch = -0.5 * fene_k * fene_reach**2 * jnp.sum(jnp.log(1.0 - square / fene_reach**2))
        length = jnp.sqrt(square)
        cosine = jnp.sum(bond[:, :, 1:] * bond[:, :, :-1], axis=0) / (
            length[:, 1:] * length[:, :-1]
        )
        return stretch + bend_k * jnp.sum(1.0 - cosine)

    return (-jax.grad(energy)(chains)).reshape(3, -1)


def tile_pairs(near_pos, near_force, far_pos, far_force):
    offsets = [near_pos[channel][:, :, None] - far_pos[channel][:, None, :] for channel in range(3)]
    square = (
        offsets[0] * offsets[0] + offsets[1] * offsets[1] + offsets[2] * offsets[2] + bead_radius**2
    )
    distance = jnp.sqrt(square)
    scaled = bead_radius / distance
    scaled_cube = scaled * scaled * scaled
    screen = jax.scipy.special.erfc(split_xi * distance)
    gauss_part = 0.5 * split_xi * bead_radius * jnp.exp(-(split_xi**2) * square)
    along_part = screen * (0.75 * scaled + 0.5 * scaled_cube) + gauss_part
    across = (screen * (0.75 * scaled - 1.5 * scaled_cube) - gauss_part) / square
    onto_far = across * sum(
        (offsets[channel] * far_force[channel][:, None, :] for channel in range(3))
    )
    onto_near = across * sum(
        (offsets[channel] * near_force[channel][:, :, None] for channel in range(3))
    )
    near_vel = jnp.stack(
        [
            jnp.sum(
                along_part * far_force[channel][:, None, :] + onto_far * offsets[channel], axis=2
            )
            for channel in range(3)
        ]
    )
    far_vel = jnp.stack(
        [
            jnp.sum(
                along_part * near_force[channel][:, :, None] + onto_near * offsets[channel], axis=1
            )
            for channel in range(3)
        ]
    )
    return (near_vel, far_vel)


def pair_sums(cells, first_list, second_list, pair_total):

    def turn(turn_index, velocity_sum):
        offset_at = turn_index * pair_block
        near_idx = lax.dynamic_slice_in_dim(first_list, offset_at, pair_block)
        far_idx = lax.dynamic_slice_in_dim(second_list, offset_at, pair_block)
        live_mask = (offset_at + jnp.arange(pair_block, dtype=jnp.int32) < pair_total).astype(
            jnp.float32
        )
        near_cells = jnp.take(cells, near_idx, axis=1)
        far_cells = jnp.take(cells, far_idx, axis=1)
        near_vel, far_vel = tile_pairs(near_cells[:3], near_cells[3:], far_cells[:3], far_cells[3:])
        cross_mask = live_mask * (near_idx != far_idx).astype(jnp.float32)
        velocity_sum = velocity_sum.at[:, near_idx].add(near_vel * live_mask[None, :, None])
        return velocity_sum.at[:, far_idx].add(far_vel * cross_mask[None, :, None])

    turn_total = (pair_total + pair_block - 1) // pair_block
    start_sum = jnp.zeros((3, cells.shape[1], CELL), jnp.float32)
    return lax.fori_loop(0, turn_total, turn, start_sum)


def signed_wave(grid_index):
    return jnp.where(grid_index < G // 2, grid_index, grid_index - G).astype(jnp.float32) * (
        2.0 * math.pi / (G * grid_spacing)
    )


def forward_pass(real_in, imag_in, form, cos_part, sin_part):
    contract = partial(jnp.einsum, precision=lax.Precision.HIGHEST)
    real_out = contract(form, real_in, cos_part) + contract(form, imag_in, sin_part)
    imag_out = contract(form, imag_in, cos_part) - contract(form, real_in, sin_part)
    return (real_out, imag_out)


def inverse_pass(real_in, imag_in, form, cos_part, sin_part):
    contract = partial(jnp.einsum, precision=lax.Precision.HIGHEST)
    real_out = contract(form, real_in, cos_part) - contract(form, imag_in, sin_part)
    imag_out = contract(form, imag_in, cos_part) + contract(form, real_in, sin_part)
    return (real_out, imag_out)


def project_flow(spectrum, wave_x, wave_y, wave_z):
    wave_sq = wave_x * wave_x + wave_y * wave_y + wave_z * wave_z
    wave_safe = jnp.where(wave_sq > 0, wave_sq, 1.0)
    spread_sq = wave_sq / (4.0 * split_xi**2)
    green_fn = jnp.where(
        wave_sq > 0,
        (1.0 - bead_radius**2 * wave_sq / 3.0)
        * (1.0 + spread_sq)
        * jnp.exp(-spread_sq)
        / wave_safe,
        0.0,
    )
    along_wave = (wave_x * spectrum[0] + wave_y * spectrum[1] + wave_z * spectrum[2]) / wave_safe
    return jnp.stack(
        [
            green_fn * (spectrum[0] - wave_x * along_wave),
            green_fn * (spectrum[1] - wave_y * along_wave),
            green_fn * (spectrum[2] - wave_z * along_wave),
        ]
    )


def kspace_part(force_rows, n_gx, n_gy):
    local_x = G // n_gx
    local_y = G // n_gy
    grid_index = jnp.arange(G, dtype=jnp.int32)
    phase_grid = (grid_index[:, None] * grid_index[None, :] % G).astype(jnp.float32) * (
        2.0 * math.pi / G
    )
    cosine_table = jnp.cos(phase_grid)
    sine_table = jnp.sin(phase_grid)
    contract = partial(jnp.einsum, precision=lax.Precision.HIGHEST)
    force_field = force_rows.reshape(3, local_x, local_y, G)
    wave_full = signed_wave(grid_index)
    row_gx = lax.axis_index("gx")
    row_gy = lax.axis_index("gy")
    freq_count = G
    spec_z = jnp.stack(
        [
            contract("cabz,zk->cabk", force_field, cosine_table),
            -contract("cabz,zk->cabk", force_field, sine_table),
        ]
    )
    cos_x = cosine_table.reshape(n_gx, local_x, G)
    sin_x = sine_table.reshape(n_gx, local_x, G)
    cos_y = cosine_table.reshape(n_gy, local_y, G)
    sin_y = sine_table.reshape(n_gy, local_y, G)
    depth_part = freq_count // n_gx
    width_part = G // n_gy
    slabs = lax.all_to_all(spec_z[:, :, None], "gx", split_axis=5, concat_axis=2, tiled=True)
    xr_part, xi_part = forward_pass(slabs[0], slabs[1], "ciabl,iak->cbkl", cos_x, sin_x)
    pencils = lax.all_to_all(
        jnp.stack([xr_part, xi_part])[:, :, None], "gy", split_axis=4, concat_axis=2, tiled=True
    )
    yr_part, yi_part = forward_pass(pencils[0], pencils[1], "cjbkl,jbm->ckml", cos_y, sin_y)
    wave_x = signed_wave(row_gy * width_part + jnp.arange(width_part, dtype=jnp.int32))[
        :, None, None
    ]
    wave_y = wave_full[None, :, None]
    wave_z = signed_wave(row_gx * depth_part + jnp.arange(depth_part, dtype=jnp.int32))[
        None, None, :
    ]
    flow_real = project_flow(yr_part, wave_x, wave_y, wave_z)
    flow_imag = project_flow(yi_part, wave_x, wave_y, wave_z)
    br_part, bi_part = inverse_pass(flow_real, flow_imag, "ckml,jbm->cjbkl", cos_y, sin_y)
    back = lax.all_to_all(
        jnp.stack([br_part, bi_part]), "gy", split_axis=2, concat_axis=4, tiled=True
    )[:, :, 0]
    ar_part, ai_part = inverse_pass(back[0], back[1], "cbkl,iak->ciabl", cos_x, sin_x)
    gathered = lax.all_to_all(
        jnp.stack([ar_part, ai_part]), "gx", split_axis=2, concat_axis=5, tiled=True
    )[:, :, 0]
    result = contract("cabk,zk->cabz", gathered[0], cosine_table) - contract(
        "cabk,zk->cabz", gathered[1], sine_table
    )
    return (result / float(G**3)).reshape(3, local_x * local_y * G)


def shards(positions, noise, route, node_perm, pair_first, pair_second, pair_count):
    forces = bonded_forces(positions)
    n_gx = lax.axis_size("gx")
    n_gy = lax.axis_size("gy")
    devices = n_gx * n_gy
    slots = node_perm.shape[2]
    per_peer = slots // devices
    blocks = slots // CELL
    row_gx = lax.axis_index("gx")
    own_order = node_perm[row_gx, 0]
    stacked = jnp.concatenate([positions, forces], axis=0)
    outgoing = (
        jnp.zeros((6, slots), jnp.float32).at[:, route].set(stacked).reshape(6, devices, per_peer)
    )
    incoming = lax.all_to_all(outgoing, ("gx", "gy"), split_axis=1, concat_axis=1, tiled=True)
    grid_data = jnp.zeros((6, slots), jnp.float32).at[:, own_order].set(incoming.reshape(6, slots))
    beside_data = shifted(grid_data, "gx", -1)
    cells = jnp.concatenate(
        [grid_data.reshape(6, blocks, CELL), beside_data.reshape(6, blocks, CELL)], axis=1
    )
    real_vel = pair_sums(cells, pair_first[0], pair_second[0], pair_count[0])
    wave_vel = kspace_part(grid_data[3:], n_gx, n_gy)
    own_vel = real_vel[:, :blocks].reshape(3, slots) + wave_vel
    far_part = real_vel[:, blocks:].reshape(3, slots)
    own_vel = own_vel + shifted(far_part, "gx", 1)
    back_msg = own_vel[:, own_order].reshape(3, devices, per_peer)
    arrived = lax.all_to_all(
        back_msg, ("gx", "gy"), split_axis=1, concat_axis=1, tiled=True
    ).reshape(3, slots)
    velocity = arrived[:, route]
    drift = time_step * velocity
    moved = positions + drift + noise
    return (moved, drift)


def solution(mesh):
    in_specs = (
        P(None, ("gx", "gy")),
        P(None, ("gx", "gy")),
        P(("gx", "gy")),
        P(None, "gy", None),
        P(("gx", "gy"), None),
        P(("gx", "gy"), None),
        P(("gx", "gy")),
    )
    out_specs = (P(None, ("gx", "gy")), P(None, ("gx", "gy")))
    return jax.shard_map(shards, mesh=mesh, in_specs=in_specs, out_specs=out_specs, check_vma=False)
```

profile of v0, /device:TPU:0, one launch (start us, length us, event | category | flops | bytes accessed | tf_op | source)
XLA Modules:
  0.0 1835.9 jit_solution(16135016490400526492)
XLA Ops:
  14.4 93.5 %scatter_custom_fusion.2 = f32[6,65536]{0,1:T(8,128)} fusion(s32[32768]{0:T(1024)S(1)} %get-tuple-element.158, f32[32768,6]{1,0:T(8,128)} %copy.190, f32[]{:T(128)} %constant.138.clone.1), kind=kCustom, calls=%fused_computation.82 | custom fusion | bytes 1573376 | tf_op jit(solution)/shard_map/scatter | solution.py:213
  107.9 18.6 %copy.191 = f32[6,32,2048]{2,0,1:T(8,128)} copy(f32[6,32,2048]{0,2,1:T(8,128)} %bitcast.353) | data formatting | bytes 3145728 | tf_op jit(solution)/shard_map/reshape | solution.py:213
  135.2 47.4 %all-to-all-done = f32[6,32,2048]{2,0,1:T(8,128)S(1)} async-done(((f32[6,32,2048]{2,0,1:T(8,128)}), f32[6,32,2048]{2,0,1:T(8,128)S(1)}, u32[]{:S(2)}, u32[]{:S(2)}) %all-to-all-start) | async-done | bytes 1572896 | tf_op jit(solution)/shard_map/all_to_all | solution.py:215
  182.7 16.7 copy.192
  199.4 172.8 %scatter_custom_fusion.3 = f32[6,65536]{0,1:T(8,128)} fusion(s32[65536]{0:T(1024)S(1)} %bitcast.373, f32[65536,6]{1,0:T(8,128)} %copy.192, f32[]{:T(128)} %constant.138.clone.1), kind=kCustom, calls=%fused_computation.80 | custom fusion | bytes 1573376 | tf_op jit(solution)/shard_map/scatter | solution.py:216
  372.1 25.1 %slice.190 = f32[3,65536]{0,1:T(8,128)} slice(f32[6,65536]{0,1:T(8,128)} %scatter_custom_fusion.3), slice={[3:6], [0:65536]} | slice | bytes 1572864 | tf_op jit(solution)/shard_map/slice | solution.py:222
  397.2 19.5 %copy.244 = f32[3,16,32,128]{3,2,1,0:T(8,128)S(1)} copy(f32[3,16,32,128]{0,3,2,1:T(8,128)} %bitcast.354) | data formatting | bytes 1572864 | tf_op jit(solution)/shard_map/reshape | solution.py:155
  436.7 36.8 %all-to-all-done.1 = f32[8,1,49152]{2,1,0:T(1,128)S(1)} async-done(((f32[8,1,49152]{2,1,0:T(1,128)}), f32[8,1,49152]{2,1,0:T(1,128)S(1)}, u32[]{:S(2)}, u32[]{:S(2)}) %all-to-all-start.1) | async-done | bytes 1572896 | tf_op jit(solution)/shard_map/all_to_all | solution.py:172
  523.8 18.5 %copy.193 = f32[6,65536]{1,0:T(8,128)} copy(f32[6,65536]{0,1:T(8,128)} %scatter_custom_fusion.3) | data formatting | bytes 3145728 | tf_op jit(solution)/shard_map/scatter | solution.py:216
  610.2 20.6 %copy.194 = f32[6,1024,64]{1,2,0:T(8,128)} copy(f32[6,1024,64]{0,2,1:T(8,128)} %bitcast.352) | data formatting | bytes 3145728 | tf_op jit(solution)/shard_map/reshape | solution.py:219
  710.2 604.5 %while.10 = (s32[]{:T(128)}, f32[3,2048,64]{2,0,1:T(4,128)}, s32[]{:T(128)}, s32[1024]{0:T(1024)}, f32[6,2048,64]{2,0,1:T(8,128)}, /*index=5*/s32[1024]{0:T(1024...) while((s32[]{:T(128)}, f32[3,2048,64]{2,0,1:T(4,128)}, s32[]{:T(128)}, ...), condition=%wide.region_13.15_spmd, body=%wide.region_4.14_spmd.sunk | while | flops 31845444 | bytes 2175403 | solution.py:100
  719.5 13.2 fusion.263
  757.3 13.2 fusion.263
  795.0 13.2 fusion.263
  832.8 13.2 fusion.263
  870.5 13.2 fusion.263
  908.3 13.2 fusion.263
  946.1 13.2 fusion.263
  983.8 13.2 fusion.263
  1021.6 13.2 fusion.263
  1059.4 13.2 fusion.263
  1097.2 13.2 fusion.263
  1134.9 13.2 fusion.263
  1172.7 13.2 fusion.263
  1210.6 13.2 fusion.263
  1356.3 15.9 copy.217
  1372.2 226.0 %gather_fusion.2 = f32[65536,3]{1,0:T(8,128)} fusion(f32[3,65536]{0,1:T(8,128)} %copy.217, s32[65536]{0:T(1024)S(1)} %broadcast_clamp_fusion), kind=kCustom, calls=%fused_computation.2 | custom fusion | bytes 1835008 | tf_op jit(solution)/shard_map/gather | solution.py:226
  1598.2 18.4 copy.218
  1647.6 15.4 copy.219
  1663.0 118.9 %gather_fusion.3 = f32[32768,3]{1,0:T(8,128)} fusion(f32[3,65536]{0,1:T(8,128)} %bitcast.363, s32[32768]{0:T(1024)S(1)} %copy-done.9), kind=kCustom, calls=%fused_computation.3 | custom fusion | bytes 917504 | tf_op jit(solution)/shard_map/gather | solution.py:230
  1781.9 13.2 multiply_bitcast_fusion
  1798.3 17.7 add_add_fusion
  (384 shorter events, 752.5 us)
Async XLA Ops:
  3.5 1.0 copy-start.4
  4.8 9.0 copy-start.10
  126.5 56.2 %all-to-all-start = ((f32[6,32,2048]{2,0,1:T(8,128)}), f32[6,32,2048]{2,0,1:T(8,128)S(1)}, u32[]{:S(2)}, u32[]{:S(2)}) async-start(f32[6,32,2048]{2,0,1:T(8,128)} %copy.191), calls=%async_computation | async-start | bytes 4194304 | tf_op jit(solution)/shard_map/all_to_all | solution.py:215
  135.2 64.1 %copy-start.6 = (s32[65536,1]{0,1:T(1,128)}, s32[65536,1]{0,1:T(1,128)S(1)}, u32[]{:S(2)}) copy-start(s32[65536,1]{0,1:T(1,128)S(1)} %compare_select_fusion.3) | copy-start | bytes 786436
  432.6 40.9 %all-to-all-start.1 = ((f32[8,1,49152]{2,1,0:T(1,128)}), f32[8,1,49152]{2,1,0:T(1,128)S(1)}, u32[]{:S(2)}, u32[]{:S(2)}) async-start(f32[8,1,49152]{2,1,0:T(1,128)} %reshape.447), calls=%async_computation.1 | async-start | bytes 3145728 | tf_op jit(solution)/shard_map/all_to_all | solution.py:172
  520.1 25.0 %all-to-all-start.2 = ((f32[4,1,98304]{2,1,0:T(1,128)}), f32[4,1,98304]{2,1,0:T(1,128)S(1)}, u32[]{:S(2)}, u32[]{:S(2)}) async-start(f32[4,1,98304]{2,1,0:T(1,128)} %reshape.449), calls=%async_computation.2 | async-start | bytes 3145728 | tf_op jit(solution)/shard_map/all_to_all | solution.py:174
  542.3 88.4 %collective-permute-start = (f32[6,65536]{1,0:T(8,128)}, f32[6,65536]{1,0:T(8,128)}, u32[]{:S(2)}, u32[]{:S(2)}) collective-permute-start(f32[6,65536]{1,0:T(8,128)} %copy.193), channel_id=1, source_target_pairs={{0,28},{4,0},{8,4},{12,8},{16,12},{20,16},{24,20},{28,24},{1,29},{... | collective-permute-start | bytes 4718600 | tf_op jit(solution)/shard_map/ppermute | solution.py:26
  605.0 4.5 copy-start.7
  605.0 37.6 %all-to-all-start.3 = ((f32[4,1,98304]{2,1,0:T(1,128)}), f32[4,1,98304]{2,1,0:T(1,128)}, u32[]{:S(2)}, u32[]{:S(2)}) async-start(f32[4,1,98304]{2,1,0:T(1,128)} %reshape.451), calls=%async_computation.3 | async-start | bytes 3145728 | tf_op jit(solution)/shard_map/all_to_all | solution.py:188
  665.0 5.3 copy-start.1
  679.0 5.2 copy-start.3
  684.2 4.1 copy-start.2
  703.6 623.4 %all-to-all-start.4 = ((f32[8,1,49152]{2,1,0:T(1,128)}), f32[8,1,49152]{2,1,0:T(1,128)}, u32[]{:S(2)}, u32[]{:S(2)}) async-start(f32[8,1,49152]{2,1,0:T(1,128)} %reshape.453), calls=%async_computation.4 | async-start | bytes 3145728 | tf_op jit(solution)/shard_map/all_to_all | solution.py:192
  1322.0 32.2 %collective-permute-start.1 = (f32[3,65536]{1,0:T(4,128)}, f32[3,65536]{1,0:T(4,128)}, u32[]{:S(2)}, u32[]{:S(2)}) collective-permute-start(f32[3,65536]{1,0:T(4,128)} %reshape.342), channel_id=1, source_target_pairs={{0,4},{4,8},{8,12},{12,16},{16,20},{20,24},{24,28},{28,0},{1,5},{5... | collective-permute-start | bytes 2359304 | tf_op jit(solution)/shard_map/ppermute | solution.py:26
  1616.6 4.8 copy-start.5
  1616.6 31.0 %all-to-all-start.5 = ((f32[3,32,2048]{2,0,1:T(4,128)}), f32[3,32,2048]{2,0,1:T(4,128)S(1)}, u32[]{:S(2)}, u32[]{:S(2)}) async-start(f32[3,32,2048]{2,0,1:T(4,128)} %copy.218), calls=%async_computation.5 | async-start | bytes 2097152 | tf_op jit(solution)/shard_map/all_to_all | solution.py:227
  1621.4 8.5 copy-start.8
  1638.3 24.7 %copy-start.9 = (s32[32768]{0:T(1024)S(1)}, s32[32768]{0:T(1024)}, u32[]{:S(2)}) copy-start(s32[32768]{0:T(1024)} %get-tuple-element.157) | copy-start | bytes 393220
  1781.9 16.4 copy-start
where the time goes:
time: 1850 us; the launch traced here: 1840 us
  local copies, waits for them, and re-layouts  1080 us (58%)
  other arithmetic  538 us (29%)
  waiting for transfers between devices  93.5 us (5%)
  matrix products  85.6 us (5%)
  starting transfers between devices  33.1 us (2%)
    gather x1, local copies, waits for them, and re-layouts, shards(): back_msg = own_vel[:, own_order].reshape(3, devices, per_peer)  226 us
    reduce_sum x16, other arithmetic, tile_pairs(): jnp.sum(along_part * near_force[channel][:, :, None] + onto_near * offset...  211 us
    scatter x2, local copies, waits for them, and re-layouts, shards(): jnp.zeros((6, slots), jnp.float32).at[:, own_order]  191 us
    gather x1, local copies, waits for them, and re-layouts, shards(): velocity = arrived[:, route]  119 us
    scatter-add x16, other arithmetic, turn(): velocity_sum.at[:, near_idx].add(near_vel * live_mask[None, :, None])  108 us
    scatter-add x16, other arithmetic, turn(): return velocity_sum.at[:, far_idx].add(far_vel * cross_mask[None, :, None])  108 us
    scatter x1, local copies, waits for them, and re-layouts, shards(): jnp.zeros((6, slots), jnp.float32).at[:, route].set(stacked)  93.5 us
    unnamed x34, local copies, waits for them, and re-layouts  86.4 us
  transfers between devices with their start and end apart: 8, of which 3 were waited for; matrix products, arithmetic and copies ran while one was open for 42% of the time, Pallas kernels for 0%

commit v1 on v0

--- a/solution.py
+++ b/solution.py
@@ -1,9 +1,12 @@
+import functools
 from functools import partial
 import math
 
 import jax
 import jax.numpy as jnp
 from jax import lax
+from jax.experimental import pallas as pl
+from jax.experimental.pallas import tpu as pltpu
 from jax.sharding import PartitionSpec as P
 
 G = 128
@@ -42,62 +45,141 @@
     return (-jax.grad(energy)(chains)).reshape(3, -1)
 
 
-def tile_pairs(near_pos, near_force, far_pos, far_force):
-    offsets = [near_pos[channel][:, :, None] - far_pos[channel][:, None, :] for channel in range(3)]
-    square = (
-        offsets[0] * offsets[0] + offsets[1] * offsets[1] + offsets[2] * offsets[2] + bead_radius**2
-    )
-    distance = jnp.sqrt(square)
-    scaled = bead_radius / distance
-    scaled_cube = scaled * scaled * scaled
-    screen = jax.scipy.special.erfc(split_xi * distance)
-    gauss_part = 0.5 * split_xi * bead_radius * jnp.exp(-(split_xi**2) * square)
-    along_part = screen * (0.75 * scaled + 0.5 * scaled_cube) + gauss_part
-    across = (screen * (0.75 * scaled - 1.5 * scaled_cube) - gauss_part) / square
-    onto_far = across * sum(
-        (offsets[channel] * far_force[channel][:, None, :] for channel in range(3))
-    )
-    onto_near = across * sum(
-        (offsets[channel] * near_force[channel][:, :, None] for channel in range(3))
-    )
-    near_vel = jnp.stack(
-        [
-            jnp.sum(
-                along_part * far_force[channel][:, None, :] + onto_far * offsets[channel], axis=2
-            )
-            for channel in range(3)
-        ]
-    )
-    far_vel = jnp.stack(
-        [
-            jnp.sum(
-                along_part * near_force[channel][:, :, None] + onto_near * offsets[channel], axis=1
-            )
-            for channel in range(3)
-        ]
-    )
-    return (near_vel, far_vel)
-
-
-def pair_sums(cells, first_list, second_list, pair_total):
-
-    def turn(turn_index, velocity_sum):
-        offset_at = turn_index * pair_block
-        near_idx = lax.dynamic_slice_in_dim(first_list, offset_at, pair_block)
-        far_idx = lax.dynamic_slice_in_dim(second_list, offset_at, pair_block)
-        live_mask = (offset_at + jnp.arange(pair_block, dtype=jnp.int32) < pair_total).astype(
-            jnp.float32
-        )
-        near_cells = jnp.take(cells, near_idx, axis=1)
-        far_cells = jnp.take(cells, far_idx, axis=1)
-        near_vel, far_vel = tile_pairs(near_cells[:3], near_cells[3:], far_cells[:3], far_cells[3:])
-        cross_mask = live_mask * (near_idx != far_idx).astype(jnp.float32)
-        velocity_sum = velocity_sum.at[:, near_idx].add(near_vel * live_mask[None, :, None])
-        return velocity_sum.at[:, far_idx].add(far_vel * cross_mask[None, :, None])
-
-    turn_total = (pair_total + pair_block - 1) // pair_block
-    start_sum = jnp.zeros((3, cells.shape[1], CELL), jnp.float32)
-    return lax.fori_loop(0, turn_total, turn, start_sum)
+ERFCX_COEF = (0.06548172872398669,
+    -0.3609186250151195,
+    0.6338942267842493,
+    -0.3384301108125971,
+    0.4003704641202259,
+    0.13581047899030682,
+    0.2395463173952274,
+    0.22417089752024144,
+    7.010614160106155e-05)
+
+
+def pair_math(dx, dy, dz, coef):
+    s2 = dx*dx + dy*dy + dz*dz + 0.25
+    u = lax.rsqrt(s2)
+    r = s2*u
+    t = pl.reciprocal(1.0 + 0.2*r)
+    w = coef[0]*t + coef[1]
+    for k in coef[2:]:
+        w = w*t + k
+    ex = jnp.exp(-0.25*s2)
+    u2 = u*u
+    a = w*u
+    f = ex*(a*(0.375 + 0.0625*u2) + 0.125)
+    h = ex*u2*(a*(0.375 - 0.1875*u2) - 0.125)
+    return f, h
+
+def pair_kernel(first, second, count, own_ref, far_ref, vown_ref, vfar_ref, pc, xr, vc, vr, *, rp, coef, unroll):
+    lane = lax.broadcasted_iota(jnp.int32, (8, 128), 1)
+    sub = lax.broadcasted_iota(jnp.int32, (8, 128), 0)
+    left = lane < 64
+    groups = rp // 4
+
+    @pl.loop(0, rp // 8)
+    def _(i):
+        for src, off in ((own_ref, 0), (far_ref, rp)):
+            for c in range(6):
+                pc[pl.ds((off + i*8)*8 + c, 8, stride=8), :] = src[c, pl.ds(pl.multiple_of(i*8, 8), 8), :]
+            for c in (6, 7):
+                pc[pl.ds((off + i*8)*8 + c, 8, stride=8), :] = jnp.zeros((8, 128), jnp.float32)
+            vc[pl.ds(pl.multiple_of((off + i*8)*8, 64), 64), :] = jnp.zeros((64, 128), jnp.float32)
+
+    lane32 = lax.broadcasted_iota(jnp.int32, (32, 128), 1)
+
+    @pl.loop(0, groups)
+    def _(g):
+        blk = pc[pl.ds(pl.multiple_of(g*32, 32), 32), :]
+        tr = jnp.transpose(blk)
+        tr = jnp.concatenate([tr[32*b:32*b + 32, :] for b in range(4)], axis=1)
+        xr[pl.ds(pl.multiple_of(g*32, 32), 32), :] = tr
+        vr[pl.ds(pl.multiple_of(g*32, 32), 32), :] = jnp.zeros((32, 128), jnp.float32)
+
+    total = count[0]
+
+    def one(p):
+        ka = first[p]
+        kb = second[p]
+        jv = pc[pl.ds(pl.multiple_of((kb >> 1)*8, 8), 8), :]
+        dup = jnp.where(left == ((kb & 1) == 0), jv, pltpu.roll(jv, 64, 1))
+        xj = [jnp.broadcast_to(dup[c:c+1, :], (8, 128)) for c in range(6)]
+        base = (ka & 1)*64 + ((ka >> 1) & 3)*8
+        idx0 = base + jnp.where(left, 0, 32)
+        row0 = pl.multiple_of((ka >> 3)*32, 32)
+        facc = [jnp.zeros((8, 128), jnp.float32) for _ in range(3)]
+        near = []
+        for q in range(4):
+            row = xr[pl.ds(row0 + 8*q, 8), :]
+            xi = [jnp.take_along_axis(row, idx0 + c, axis=1) for c in range(6)]
+            d = [xi[c] - xj[c] for c in range(3)]
+            f, h = pair_math(d[0], d[1], d[2], coef)
+            dj = d[0]*xj[3] + d[1]*xj[4] + d[2]*xj[5]
+            di = d[0]*xi[3] + d[1]*xi[4] + d[2]*xi[5]
+            hj = h*dj
+            hi = h*di
+            val = jnp.zeros((8, 128), jnp.float32)
+            for c in range(3):
+                nv = f*xj[3+c] + hj*d[c]
+                lo = jnp.sum(jnp.where(left, nv, 0.0), axis=1, keepdims=True)
+                hi_ = jnp.sum(jnp.where(left, 0.0, nv), axis=1, keepdims=True)
+                val = jnp.where(lane == base + c, lo, val)
+                val = jnp.where(lane == base + 32 + c, hi_, val)
+                facc[c] = facc[c] + (f*xi[3+c] + hi*d[c])
+            near.append(val)
+        fv = jnp.zeros((8, 128), jnp.float32)
+        for c in range(3):
+            s = jnp.sum(facc[c], axis=0, keepdims=True)
+            fv = jnp.where(sub == c, s, fv)
+        fv = fv + pltpu.roll(fv, 64, 1)
+        keep = (left == ((kb & 1) == 0)) & (ka != kb)
+        fv = jnp.where(keep, fv, 0.0)
+        return row0, near, kb, fv
+
+    def turn(i, carry):
+        outs = []
+        for k in range(unroll):
+            outs.append((i*unroll + k, one(i*unroll + k)))
+        for p, (row0, near, kb, fv) in outs:
+            alive = (p < total).astype(jnp.float32) if unroll > 1 else None
+            if unroll > 1:
+                near = [n*alive for n in near]
+                fv = fv*alive
+            for q in range(4):
+                at = pl.ds(row0 + 8*q, 8)
+                vr[at, :] = vr[at, :] + near[q]
+            at = pl.ds(pl.multiple_of((kb >> 1)*8, 8), 8)
+            vc[at, :] = vc[at, :] + fv
+        return carry
+
+    lax.fori_loop(0, lax.div(total + (unroll - 1), jnp.int32(unroll)), turn, 0)
+
+    @pl.loop(0, groups)
+    def _(g):
+        m = vr[pl.ds(pl.multiple_of(g*32, 32), 32), :]
+        st = jnp.concatenate([m[:, 32*b:32*b + 32] for b in range(4)], axis=0)
+        at = pl.ds(pl.multiple_of(g*32, 32), 32)
+        vc[at, :] = vc[at, :] + jnp.transpose(st)
+
+    @pl.loop(0, rp // 8)
+    def _(i):
+        for dst, off in ((vown_ref, 0), (vfar_ref, rp)):
+            for c in range(3):
+                dst[c, pl.ds(pl.multiple_of(i*8, 8), 8), :] = vc[pl.ds((off + i*8)*8 + c, 8, stride=8), :]
+
+def pair_call(first, second, count, own, far, coef=ERFCX_COEF, unroll=1):
+    rp = own.shape[1]
+    f32 = jnp.float32
+    return pl.pallas_call(
+        functools.partial(pair_kernel, rp=rp, coef=coef, unroll=unroll),
+        out_shape=(jax.ShapeDtypeStruct((3, rp, 128), f32),)*2,
+        in_specs=[pl.BlockSpec(memory_space=pltpu.SMEM)]*3 + [pl.BlockSpec(memory_space=pltpu.VMEM)]*2,
+        out_specs=(pl.BlockSpec(memory_space=pltpu.VMEM),)*2,
+        scratch_shapes=[pltpu.VMEM((2*rp*8, 128), f32), pltpu.VMEM((rp*8, 128), f32),
+                        pltpu.VMEM((2*rp*8, 128), f32), pltpu.VMEM((rp*8, 128), f32)],
+        compiler_params=pltpu.CompilerParams(vmem_limit_bytes=48*1024*1024),
+        name="pairs",
+    )(first, second, count, own, far)
 
 
 def signed_wave(grid_index):
@@ -205,7 +287,6 @@
     devices = n_gx * n_gy
     slots = node_perm.shape[2]
     per_peer = slots // devices
-    blocks = slots // CELL
     row_gx = lax.axis_index("gx")
     own_order = node_perm[row_gx, 0]
     stacked = jnp.concatenate([positions, forces], axis=0)
@@ -215,14 +296,16 @@
     incoming = lax.all_to_all(outgoing, ("gx", "gy"), split_axis=1, concat_axis=1, tiled=True)
     grid_data = jnp.zeros((6, slots), jnp.float32).at[:, own_order].set(incoming.reshape(6, slots))
     beside_data = shifted(grid_data, "gx", -1)
-    cells = jnp.concatenate(
-        [grid_data.reshape(6, blocks, CELL), beside_data.reshape(6, blocks, CELL)], axis=1
-    )
-    real_vel = pair_sums(cells, pair_first[0], pair_second[0], pair_count[0])
+    near_vel, far_vel = pair_call(
+        pair_first[0],
+        pair_second[0],
+        pair_count,
+        grid_data.reshape(6, slots // 128, 128),
+        beside_data.reshape(6, slots // 128, 128),
+    )
     wave_vel = kspace_part(grid_data[3:], n_gx, n_gy)
-    own_vel = real_vel[:, :blocks].reshape(3, slots) + wave_vel
-    far_part = real_vel[:, blocks:].reshape(3, slots)
-    own_vel = own_vel + shifted(far_part, "gx", 1)
+    own_vel = near_vel.reshape(3, slots) + wave_vel
+    own_vel = own_vel + shifted(far_vel.reshape(3, slots), "gx", 1)
     back_msg = own_vel[:, own_order].reshape(3, devices, per_peer)
     arrived = lax.all_to_all(
         back_msg, ("gx", "gy"), split_axis=1, concat_axis=1, tiled=True

time: 1850 us -> 1580 us (0.85)
  other arithmetic: 538 us -> 65.2 us
  Pallas kernels: 0 us -> 291 us
  local copies, waits for them, and re-layouts: 1080 us -> 927 us
  waiting for transfers between devices: 93.5 us -> 142 us
  blocking collectives: 0 us -> 22.5 us
    pallas_call x0 -> x1, Pallas kernels: none -> 291 us  [pair_call(): pl.pallas_call(functools.partial(pair_kernel, rp=rp, coef=coef, unroll=un...]
    scatter-add x32 -> x0, other arithmetic: 216 us -> none  [the longest x16 108 us: turn(): velocity_sum.at[:, near_idx].add(near_vel * live_mask[None, :, None])]
    reduce_sum x16 -> x0, other arithmetic: 211 us -> none  [tile_pairs(): jnp.sum(along_part * near_force[channel][:, :, None] + onto_near * offset...]
    gather x32 -> x0, local copies, waits for them, and re-layouts: 127 us -> none  [the longest x16 63.6 us: turn(): far_cells = jnp.take(cells, far_idx, axis=1)]
    ppermute x2, waiting for transfers between devices: 0.01 us -> 28.7 us  [shifted(): lax.ppermute(value, axis, [(i, (i + by) % devices) for i in range(devices)])]
    mul x48 -> x0, other arithmetic: 25.3 us -> none  [the longest x16 22.8 us: turn(): cross_mask = live_mask * (near_idx != far_idx).astype(jnp.float32)]
    all_to_all x0 -> x1, blocking collectives: none -> 22.5 us  [kspace_part(): lax.all_to_all(jnp.stack([br_part, bi_part]), 'gy', split_axis=2, concat_...]
    all_to_all x1, waiting for transfers between devices: 0.01 us -> 19.5 us  [kspace_part(): lax.all_to_all(jnp.stack([xr_part, xi_part])[:, :, None], 'gy', split_axi...]
  transfers between devices with their start and end apart: 8 -> 7, of which waited for: 3 -> 6; matrix products, arithmetic and copies ran while one was open for 42% -> 5% of each run, Pallas kernels for 0% -> 18%
where the time goes in v1:
time: 1580 us; the launch traced here: 1570 us
  local copies, waits for them, and re-layouts  927 us (59%)
  Pallas kernels  291 us (18%)
  waiting for transfers between devices  142 us (9%)
  matrix products  85.6 us (5%)
  other arithmetic  65.2 us (4%)
  starting transfers between devices  37.4 us (2%)
  blocking collectives  22.5 us (1%)
    pallas_call x1, Pallas kernels, pair_call(): pl.pallas_call(functools.partial(pair_kernel, rp=rp, coef=coef, unroll=un...  291 us
    gather x1, local copies, waits for them, and re-layouts, shards(): back_msg = own_vel[:, own_order].reshape(3, devices, per_peer)  228 us
    scatter x2, local copies, waits for them, and re-layouts, shards(): jnp.zeros((6, slots), jnp.float32).at[:, own_order]  191 us
    gather x1, local copies, waits for them, and re-layouts, shards(): velocity = arrived[:, route]  120 us
    scatter x1, local copies, waits for them, and re-layouts, shards(): jnp.zeros((6, slots), jnp.float32).at[:, route].set(stacked)  93.5 us
    unnamed x38, local copies, waits for them, and re-layouts  88.3 us
    all_to_all x1, waiting for transfers between devices, shards(): lax.all_to_all(outgoing, ('gx', 'gy'), split_axis=1, concat_axis=1, tiled...  47.5 us
    all_to_all x1, waiting for transfers between devices, kspace_part(): lax.all_to_all(spec_z[:, :, None], 'gx', split_axis=5, concat_axis=2, til...  36.8 us
  transfers between devices with their start and end apart: 7, of which 6 were waited for; matrix products, arithmetic and copies ran while one was open for 5% of the time, Pallas kernels for 18%

profile of v1, /device:TPU:0, one launch (start us, length us, event | category | flops | bytes accessed | tf_op | source)
XLA Modules:
  0.0 1572.5 jit_solution(938358039896782832)
XLA Ops:
  4.5 8.9 copy.109
  14.1 93.5 %scatter_custom_fusion = f32[6,65536]{0,1:T(8,128)} fusion(s32[32768]{0:T(1024)S(1)} %get-tuple-element.38, f32[32768,6]{1,0:T(8,128)} %copy.109, f32[]{:T(128)} %constant.34.clone.1), kind=kCustom, calls=%fused_computation.8 | custom fusion | bytes 1573376 | tf_op jit(solution)/shard_map/scatter | solution.py:294
  107.5 18.6 %copy.110 = f32[6,32,2048]{2,0,1:T(8,128)} copy(f32[6,32,2048]{0,2,1:T(8,128)} %bitcast.297) | data formatting | bytes 3145728 | tf_op jit(solution)/shard_map/reshape | solution.py:294
  126.1 7.5 all-to-all-start
  134.9 47.5 %all-to-all-done = f32[6,32,2048]{2,0,1:T(8,128)S(1)} async-done(((f32[6,32,2048]{2,0,1:T(8,128)}), f32[6,32,2048]{2,0,1:T(8,128)S(1)}, u32[]{:S(2)}, u32[]{:S(2)}) %all-to-all-start) | async-done | bytes 1572896 | tf_op jit(solution)/shard_map/all_to_all | solution.py:296
  182.3 16.6 %copy.111 = f32[65536,6]{1,0:T(8,128)} copy(f32[65536,6]{0,1:T(8,128)S(1)} %bitcast.315) | data formatting | bytes 3145728 | tf_op jit(solution)/shard_map/reshape | solution.py:297
  198.9 172.8 %scatter_custom_fusion.1 = f32[6,65536]{0,1:T(8,128)} fusion(s32[65536]{0:T(1024)S(1)} %bitcast.317, f32[65536,6]{1,0:T(8,128)} %copy.111, f32[]{:T(128)} %constant.34.clone.1), kind=kCustom, calls=%fused_computation.6 | custom fusion | bytes 1573376 | tf_op jit(solution)/shard_map/scatter | solution.py:297
  371.7 25.2 %slice.108 = f32[3,65536]{0,1:T(8,128)} slice(f32[6,65536]{0,1:T(8,128)} %scatter_custom_fusion.1), slice={[3:6], [0:65536]} | slice | bytes 1572864 | tf_op jit(solution)/shard_map/slice | solution.py:306
  396.8 19.5 %copy.160 = f32[3,16,32,128]{3,2,1,0:T(8,128)S(1)} copy(f32[3,16,32,128]{0,3,2,1:T(8,128)} %bitcast.298) | data formatting | bytes 1572864 | tf_op jit(solution)/shard_map/reshape | solution.py:237
  424.6 7.6 reshape.383
  436.2 36.8 %all-to-all-done.1 = f32[8,1,49152]{2,1,0:T(1,128)S(1)} async-done(((f32[8,1,49152]{2,1,0:T(1,128)}), f32[8,1,49152]{2,1,0:T(1,128)S(1)}, u32[]{:S(2)}, u32[]{:S(2)}) %all-to-all-start.1) | async-done | bytes 1572896 | tf_op jit(solution)/shard_map/all_to_all | solution.py:254
  523.8 19.5 %all-to-all-done.2 = f32[4,1,98304]{2,1,0:T(1,128)S(1)} async-done(((f32[4,1,98304]{2,1,0:T(1,128)}), f32[4,1,98304]{2,1,0:T(1,128)S(1)}, u32[]{:S(2)}, u32[]{:S(2)}) %all-to-all-start.2) | async-done | bytes 1572896 | tf_op jit(solution)/shard_map/all_to_all | solution.py:256
  553.3 6.4 copy.119
  602.3 22.5 %all_to_all.70 = f32[4,1,98304]{2,1,0:T(1,128)S(1)} all-to-all(f32[4,1,98304]{2,1,0:T(1,128)S(1)} %reshape.387), channel_id=1, replica_groups=mesh['gx'=8,'gy'=4] {'gy'}, dimensions={0} | all-to-all | bytes 3145728 | tf_op jit(solution)/shard_map/all_to_all | solution.py:270
  676.7 7.6 reshape.389
  689.3 18.5 %copy.113 = f32[6,65536]{1,0:T(8,128)} copy(f32[6,65536]{0,1:T(8,128)} %scatter_custom_fusion.1) | data formatting | bytes 3145728 | tf_op jit(solution)/shard_map/scatter | solution.py:297
  713.2 18.1 %copy.159.own_ref = f32[6,512,128]{2,1,0:T(8,128)S(1)} copy(f32[6,512,128]{0,2,1:T(8,128)} %bitcast.296) | data formatting | bytes 3145728 | tf_op jit(solution)/shard_map/reshape | solution.py:303
  731.4 28.3 %collective-permute-done = f32[6,65536]{1,0:T(8,128)} collective-permute-done((f32[6,65536]{1,0:T(8,128)}, f32[6,65536]{1,0:T(8,128)}, u32[]{:S(2)}, u32[]{:S(2)}) %collective-permute-start) | collective-permute-done | bytes 1572896 | tf_op jit(solution)/shard_map/ppermute | solution.py:29
  761.7 290.6 %pairs.1 = (f32[3,512,128]{2,1,0:T(8,128)S(1)}, f32[3,512,128]{2,1,0:T(8,128)S(1)}) custom-call(s32[1024]{0:T(1024)S(1)} %bitcast.294, s32[1024]{0:T(1024)S(1)} %bitcast.295, s32[1]{0:T(128)S(6)} %copy.181.count, f32[6,512,128]{2,1,0:T(8,128)S(1)} %copy.159.own_ref, f32[6,512,128]{2,1,0:T(8,128)S(1)} %bitcast.291), custom_call_target="tpu_custom_call" | custom-call | tf_op jit(solution)/shard_map/pairs/pallas_call | solution.py:173
  1082.7 15.8 %copy.132 = f32[3,65536]{0,1:T(8,128)} copy(f32[3,65536]{1,0:T(4,128)S(1)} %fusion.30) | data formatting | bytes 1572864 | tf_op jit(solution)/shard_map/add | solution.py:308
  1098.5 227.6 %gather_fusion = f32[65536,3]{1,0:T(8,128)} fusion(f32[3,65536]{0,1:T(8,128)} %copy.132, s32[65536]{0:T(1024)S(1)} %copy-done.8), kind=kCustom, calls=%fused_computation | custom fusion | bytes 1835008 | tf_op jit(solution)/shard_map/gather | solution.py:309
  1326.1 18.4 %copy.133 = f32[3,32,2048]{2,0,1:T(4,128)} copy(f32[3,32,2048]{0,2,1:T(8,128)} %bitcast.308) | data formatting | bytes 1572864 | tf_op jit(solution)/shard_map/reshape | solution.py:309
  1344.5 12.9 all-to-all-start.5
  1357.4 8.4 copy.135
  1365.8 8.4 copy.136
  1374.2 9.4 all-to-all-done.5
  1383.6 15.4 copy.134
  1399.0 119.5 %gather_fusion.1 = f32[32768,3]{1,0:T(8,128)} fusion(f32[3,65536]{0,1:T(8,128)} %bitcast.307, s32[32768]{0:T(1024)S(1)} %copy-done.10), kind=kCustom, calls=%fused_computation.1 | custom fusion | bytes 917504 | tf_op jit(solution)/shard_map/gather | solution.py:313
  1518.5 13.3 multiply_bitcast_fusion
  1535.0 17.7 %add_add_fusion = f32[3,32768]{0,1:T(8,128)} fusion(f32[3,32768]{0,1:T(8,128)} %copy.136, f32[3,32768]{0,1:T(8,128)} %copy.135, f32[32768,3]{1,0:T(8,128)S(1)} %copy-done.2), kind=kLoop, calls=%fused_computation.5 | loop fusion | flops 294912 | bytes 1572864 | tf_op jit(solution)/shard_map/add | solution.py:315
  1552.7 9.8 copy.137
  1562.5 9.8 copy.138
  (105 shorter events, 218.0 us)
Async XLA Ops:
  3.2 1.0 copy-start.6
  4.5 8.9 copy-start.11
  126.1 56.2 %all-to-all-start = ((f32[6,32,2048]{2,0,1:T(8,128)}), f32[6,32,2048]{2,0,1:T(8,128)S(1)}, u32[]{:S(2)}, u32[]{:S(2)}) async-start(f32[6,32,2048]{2,0,1:T(8,128)} %copy.110), calls=%async_computation | async-start | bytes 4194304 | tf_op jit(solution)/shard_map/all_to_all | solution.py:296
  432.2 40.9 %all-to-all-start.1 = ((f32[8,1,49152]{2,1,0:T(1,128)}), f32[8,1,49152]{2,1,0:T(1,128)S(1)}, u32[]{:S(2)}, u32[]{:S(2)}) async-start(f32[8,1,49152]{2,1,0:T(1,128)} %reshape.383), calls=%async_computation.1 | async-start | bytes 3145728 | tf_op jit(solution)/shard_map/all_to_all | solution.py:254
  519.7 23.6 %all-to-all-start.2 = ((f32[4,1,98304]{2,1,0:T(1,128)}), f32[4,1,98304]{2,1,0:T(1,128)S(1)}, u32[]{:S(2)}, u32[]{:S(2)}) async-start(f32[4,1,98304]{2,1,0:T(1,128)} %reshape.385), calls=%async_computation.2 | async-start | bytes 3145728 | tf_op jit(solution)/shard_map/all_to_all | solution.py:256
  646.1 5.3 copy-start.3
  659.8 5.2 copy-start.5
  665.1 4.1 copy-start.4
  684.4 369.6 %all-to-all-start.4 = ((f32[8,1,49152]{2,1,0:T(1,128)}), f32[8,1,49152]{2,1,0:T(1,128)}, u32[]{:S(2)}, u32[]{:S(2)}) async-start(f32[8,1,49152]{2,1,0:T(1,128)} %reshape.389), calls=%async_computation.4 | async-start | bytes 3145728 | tf_op jit(solution)/shard_map/all_to_all | solution.py:274
  707.9 51.9 %collective-permute-start = (f32[6,65536]{1,0:T(8,128)}, f32[6,65536]{1,0:T(8,128)}, u32[]{:S(2)}, u32[]{:S(2)}) collective-permute-start(f32[6,65536]{1,0:T(8,128)} %copy.113), channel_id=1, source_target_pairs={{0,28},{4,0},{8,4},{12,8},{16,12},{20,16},{24,20},{28,24},{1,29},{... | collective-permute-start | bytes 4718600 | tf_op jit(solution)/shard_map/ppermute | solution.py:29
  731.4 30.3 %copy-start = (s32[1,1024]{1,0:T(1,128)S(1)}, s32[1,1024]{1,0:T(1,128)}, u32[]{:S(2)}) copy-start(s32[1,1024]{1,0:T(1,128)} %param.11) | copy-start | bytes 12292
  731.4 30.3 %copy-start.1 = (s32[1,1024]{1,0:T(1,128)S(1)}, s32[1,1024]{1,0:T(1,128)}, u32[]{:S(2)}) copy-start(s32[1,1024]{1,0:T(1,128)} %param.12) | copy-start | bytes 12292
  1053.9 27.8 %collective-permute-start.1 = (f32[3,65536]{1,0:T(4,128)}, f32[3,65536]{1,0:T(4,128)S(1)}, u32[]{:S(2)}, u32[]{:S(2)}) collective-permute-start(f32[3,65536]{1,0:T(4,128)} %bitcast.290), channel_id=1, source_target_pairs={{0,4},{4,8},{8,12},{12,16},{16,20},{20,24},{24,28},{28,0},{1,5},{5... | collective-permute-start | bytes 2359304 | tf_op jit(solution)/shard_map/ppermute | solution.py:29
  1082.7 15.8 %copy-start.8 = (s32[65536]{0:T(1024)S(1)}, s32[65536]{0:T(1024)}, u32[]{:S(2)}) copy-start(s32[65536]{0:T(1024)} %broadcast_clamp_fusion) | copy-start | bytes 786436
  1326.1 31.3 %copy-start.7 = (f32[3,32768]{1,0:T(4,128)S(1)}, f32[3,32768]{1,0:T(4,128)}, u32[]{:S(2)}) copy-start(f32[3,32768]{1,0:T(4,128)} %param.7) | copy-start | bytes 1179652
  1344.5 39.1 %all-to-all-start.5 = ((f32[3,32,2048]{2,0,1:T(4,128)}), f32[3,32,2048]{2,0,1:T(4,128)S(1)}, u32[]{:S(2)}, u32[]{:S(2)}) async-start(f32[3,32,2048]{2,0,1:T(4,128)} %copy.133), calls=%async_computation.5 | async-start | bytes 2097152 | tf_op jit(solution)/shard_map/all_to_all | solution.py:310
  1357.4 8.4 copy-start.9
  1374.2 24.8 %copy-start.10 = (s32[32768]{0:T(1024)S(1)}, s32[32768]{0:T(1024)}, u32[]{:S(2)}) copy-start(s32[32768]{0:T(1024)} %get-tuple-element.37) | copy-start | bytes 393220
  1518.5 16.4 %copy-start.2 = (f32[32768,3]{1,0:T(8,128)S(1)}, f32[32768,3]{1,0:T(8,128)}, u32[]{:S(2)}) copy-start(f32[32768,3]{1,0:T(8,128)} %gather_fusion.1) | copy-start | bytes 1179652

commit v2 on v1

--- a/solution.py
+++ b/solution.py
@@ -29,20 +29,266 @@
     return lax.ppermute(value, axis, [(i, (i + by) % devices) for i in range(devices)])
 
 
-def bonded_forces(positions):
-    chains = positions.reshape(3, -1, BEAD_CH)
-
-    def energy(coords):
-        bond = coords[:, :, 1:] - coords[:, :, :-1]
-        square = jnp.sum(bond * bond, axis=0)
-        stretch = -0.5 * fene_k * fene_reach**2 * jnp.sum(jnp.log(1.0 - square / fene_reach**2))
-        length = jnp.sqrt(square)
-        cosine = jnp.sum(bond[:, :, 1:] * bond[:, :, :-1], axis=0) / (
-            length[:, 1:] * length[:, :-1]
-        )
-        return stretch + bend_k * jnp.sum(1.0 - cosine)
-
-    return (-jax.grad(energy)(chains)).reshape(3, -1)
+UNROLL = 16
+
+SMEM_SPEC = pl.BlockSpec(memory_space=pltpu.SMEM)
+VMEM_SPEC = pl.BlockSpec(memory_space=pltpu.VMEM)
+
+
+def lane_index(rows):
+    return lax.broadcasted_iota(jnp.int32, (rows, 128), 1)
+
+
+def window(table, at, rows):
+    row = lax.shift_right_logical(at, 7)
+    lead = at & 127
+    head = pltpu.roll(table[pl.ds(row, rows), :], (128 - lead) & 127, 1)
+    tail = pltpu.roll(table[pl.ds(row + 1, rows), :], (128 - lead) & 127, 1)
+    return jnp.where(lane_index(rows) < 128 - lead, head, tail)
+
+
+def slots_kernel(starts, route_ref, out_ref, table, *, rows, depth):
+    table[pl.ds(0, rows), :] = route_ref[...]
+    table[pl.ds(rows, depth + 8), :] = jnp.zeros((depth + 8, 128), jnp.int32)
+    place = lane_index(depth) + lax.broadcasted_iota(jnp.int32, (depth, 128), 0) * 128
+
+    @pl.loop(0, out_ref.shape[0])
+    def _(t):
+        at = starts[t]
+        slot = window(table, at, depth) - t * (depth * 128)
+        out_ref[t] = jnp.where(place < starts[t + 1] - at, slot, -1)
+
+
+def slots_call(starts, route, depth):
+    rows = route.shape[0]
+    peers = starts.shape[0] - 1
+    return pl.pallas_call(
+        functools.partial(slots_kernel, rows=rows, depth=depth),
+        out_shape=jax.ShapeDtypeStruct((peers, depth, 128), jnp.int32),
+        in_specs=[SMEM_SPEC, VMEM_SPEC],
+        out_specs=VMEM_SPEC,
+        scratch_shapes=[pltpu.VMEM((rows + depth + 8, 128), jnp.int32)],
+        name="slots",
+    )(starts, route)
+
+
+def chain_forces(pos):
+    rows = pos[0].shape[0]
+    place = lane_index(rows) & (BEAD_CH - 1)
+    bonded = place < BEAD_CH - 1
+    bent = place < BEAD_CH - 2
+    after = (place > 0) & bonded
+    bond = [jnp.where(bonded, pltpu.roll(x, 127, 1) - x, 0.5) for x in pos]
+    square = bond[0] * bond[0] + bond[1] * bond[1] + bond[2] * bond[2]
+    inverse = lax.rsqrt(square)
+    unit = [b * inverse for b in bond]
+    following = [pltpu.roll(u, 127, 1) for u in unit]
+    previous = [pltpu.roll(u, 1, 1) for u in unit]
+    cosine = sum(u * v for u, v in zip(unit, following))
+    cosine_before = pltpu.roll(cosine, 1, 1)
+    pull = fene_k / (1.0 - square / fene_reach**2)
+    out = []
+    for c in range(3):
+        turn = jnp.where(bent, following[c] - cosine * unit[c], 0.0)
+        turn = turn + jnp.where(after, previous[c] - cosine_before * unit[c], 0.0)
+        slope = jnp.where(bonded, pull * bond[c] - bend_k * inverse * turn, 0.0)
+        out.append(slope - pltpu.roll(slope, 1, 1))
+    return out
+
+
+def pack_kernel(starts, pos_ref, out_ref, table, *, rows, depth, stride):
+    step = 8
+
+    @pl.loop(0, rows // step)
+    def _(i):
+        at = pl.multiple_of(i * step, step)
+        pos = [pos_ref[c, pl.ds(at, step), :] for c in range(3)]
+        for c, value in enumerate(pos + chain_forces(pos)):
+            table[pl.ds(c * stride + at, step), :] = value
+
+    for c in range(6):
+        table[pl.ds(c * stride + rows, stride - rows), :] = jnp.zeros((stride - rows, 128), jnp.float32)
+
+    @pl.loop(0, out_ref.shape[0])
+    def _(t):
+        at = starts[t]
+        for c in range(6):
+            out_ref[t, c * depth : (c + 1) * depth, :] = window(table, at + c * stride * 128, depth)
+
+
+def pack_call(starts, pos, depth):
+    rows = pos.shape[1]
+    peers = starts.shape[0] - 1
+    stride = rows + depth + 8
+    stride += -stride % 8
+    return pl.pallas_call(
+        functools.partial(pack_kernel, rows=rows, depth=depth, stride=stride),
+        out_shape=jax.ShapeDtypeStruct((peers, 6 * depth, 128), jnp.float32),
+        in_specs=[SMEM_SPEC, VMEM_SPEC],
+        out_specs=VMEM_SPEC,
+        scratch_shapes=[pltpu.VMEM((6 * stride, 128), jnp.float32)],
+        name="pack",
+    )(starts, pos)
+
+
+def nodes_kernel(slots_ref, perm_ref, out_ref, *, depth, spare):
+    tile = 8 if depth % 8 == 0 else 1
+
+    @pl.loop(0, slots_ref.shape[0])
+    def _(t):
+        rows = [jnp.broadcast_to(perm_ref[t, w : w + 1, :], (8, 128)) for w in range(depth)]
+        for r in range(depth // tile):
+            slot = jnp.broadcast_to(slots_ref[t, r * tile : (r + 1) * tile, :], (8, 128))
+            place = slot & 127
+            which = slot >> 7
+            node = jnp.full((8, 128), spare, jnp.int32)
+            for w in range(depth):
+                node = jnp.where(which == w, jnp.take_along_axis(rows[w], place, axis=1), node)
+            out_ref[t, r * tile : (r + 1) * tile, :] = node[:tile]
+
+
+def nodes_call(slots, perm, spare):
+    return pl.pallas_call(
+        functools.partial(nodes_kernel, depth=slots.shape[1], spare=spare),
+        out_shape=jax.ShapeDtypeStruct(slots.shape, jnp.int32),
+        in_specs=[VMEM_SPEC] * 2,
+        out_specs=VMEM_SPEC,
+        name="nodes",
+    )(slots, perm)
+
+
+def scatter_kernel(nodes, counts, in_ref, out_ref, table, rows_ref, *, depth, rp):
+    t = pl.program_id(0)
+
+    @pl.when(t == 0)
+    def _():
+        @pl.loop(0, rp)
+        def _(k):
+            table[pl.ds(pl.multiple_of(k * 128, 128), 128), :] = jnp.zeros((128, 128), jnp.float32)
+
+    for r in range(depth):
+        piece = in_ref[0, pl.ds(r, 6, stride=depth), :]
+        piece = jnp.concatenate([piece, jnp.zeros((2, 128), jnp.float32)], axis=0)
+        rows_ref[r * 128 : (r + 1) * 128, 0:8] = jnp.transpose(piece)
+
+    base = t * (depth * 128)
+
+    def some(i, carry):
+        at = pl.multiple_of(i * UNROLL, UNROLL)
+        for u in range(UNROLL):
+            table[pl.ds(nodes[base + at + u], 1), :] = rows_ref[pl.ds(at + u, 1), :]
+        return carry
+
+    lax.fori_loop(0, lax.div(counts[t] + (UNROLL - 1), jnp.int32(UNROLL)), some, 0)
+
+    @pl.when(t == pl.num_programs(0) - 1)
+    def _():
+        @pl.loop(0, rp, unroll=4)
+        def _(k):
+            turned = jnp.transpose(table[pl.ds(pl.multiple_of(k * 128, 128), 128), 0:8])
+            out_ref[pl.ds(k, 6, stride=rp), :] = turned[:6]
+
+
+def scatter_call(nodes, counts, data, rp):
+    peers, height, _ = data.shape
+    depth = height // 6
+    return pl.pallas_call(
+        functools.partial(scatter_kernel, depth=depth, rp=rp),
+        out_shape=jax.ShapeDtypeStruct((6 * rp, 128), jnp.float32),
+        grid=(peers,),
+        in_specs=[SMEM_SPEC, SMEM_SPEC, pl.BlockSpec((1, height, 128), lambda t: (t, 0, 0))],
+        out_specs=VMEM_SPEC,
+        scratch_shapes=[pltpu.VMEM((rp * 128 + 8, 128), jnp.float32), pltpu.VMEM((depth * 128, 128), jnp.float32)],
+        compiler_params=pltpu.CompilerParams(vmem_limit_bytes=52 * 1024 * 1024),
+        name="scatter",
+    )(nodes, counts, data)
+
+
+def gather_kernel(nodes, counts, one_ref, two_ref, three_ref, out_ref, table, rows_ref, *, depth, rp):
+    t = pl.program_id(0)
+
+    @pl.when(t == 0)
+    def _():
+        @pl.loop(0, rp, unroll=4)
+        def _(k):
+            at = pl.ds(k, 3, stride=rp)
+            value = one_ref[at, :] + two_ref[at, :] + three_ref[at, :]
+            value = jnp.concatenate([value, jnp.zeros((5, 128), jnp.float32)], axis=0)
+            table[pl.ds(pl.multiple_of(k * 128, 128), 128), 0:8] = jnp.transpose(value)
+
+    base = t * (depth * 128)
+
+    def some(i, carry):
+        at = pl.multiple_of(i * UNROLL, UNROLL)
+        for u in range(UNROLL):
+            rows_ref[pl.ds(at + u, 1), :] = table[pl.ds(nodes[base + at + u], 1), :]
+        return carry
+
+    lax.fori_loop(0, lax.div(counts[t] + (UNROLL - 1), jnp.int32(UNROLL)), some, 0)
+    for r in range(depth):
+        turned = jnp.transpose(rows_ref[r * 128 : (r + 1) * 128, 0:8])
+        out_ref[0, pl.ds(r, 3, stride=depth), :] = turned[:3]
+
+
+def gather_call(nodes, counts, one, two, three, depth):
+    rp = one.shape[0] // 3
+    peers = counts.shape[0]
+    return pl.pallas_call(
+        functools.partial(gather_kernel, depth=depth, rp=rp),
+        out_shape=jax.ShapeDtypeStruct((peers, 3 * depth, 128), jnp.float32),
+        grid=(peers,),
+        in_specs=[SMEM_SPEC, SMEM_SPEC] + [VMEM_SPEC] * 3,
+        out_specs=pl.BlockSpec((1, 3 * depth, 128), lambda t: (t, 0, 0)),
+        scratch_shapes=[pltpu.VMEM((rp * 128 + 8, 128), jnp.float32), pltpu.VMEM((depth * 128, 128), jnp.float32)],
+        compiler_params=pltpu.CompilerParams(vmem_limit_bytes=52 * 1024 * 1024),
+        name="gather",
+    )(nodes, counts, one, two, three)
+
+
+def finish_kernel(starts, in_ref, pos_ref, noise_ref, moved_ref, drift_ref, table, *, rows, depth, stride):
+    lane = lane_index(depth)
+    first = lane_index(1)
+
+    @pl.loop(0, in_ref.shape[0])
+    def _(t):
+        at = starts[t]
+        row = lax.shift_right_logical(at, 7)
+        lead = at & 127
+        for c in range(3):
+            value = pltpu.roll(in_ref[t, c * depth : (c + 1) * depth, :], lead, 1)
+            here = pl.ds(c * stride + row, depth)
+            behind = pl.ds(c * stride + row + 1, depth)
+            edge = table[pl.ds(c * stride + row, 1), :]
+            table[behind, :] = value
+            if depth > 1:
+                body = jnp.where(lane[1:] < lead, value[:-1], value[1:])
+                table[pl.ds(c * stride + row + 1, depth - 1), :] = body
+            table[pl.ds(c * stride + row, 1), :] = jnp.where(first < lead, edge, value[:1])
+
+    step = 8
+
+    @pl.loop(0, rows // step)
+    def _(i):
+        at = pl.multiple_of(i * step, step)
+        for c in range(3):
+            drift = time_step * table[pl.ds(c * stride + at, step), :]
+            drift_ref[c, pl.ds(at, step), :] = drift
+            moved_ref[c, pl.ds(at, step), :] = pos_ref[c, pl.ds(at, step), :] + drift + noise_ref[c, pl.ds(at, step), :]
+
+
+def finish_call(starts, data, pos, noise):
+    rows = pos.shape[1]
+    depth = data.shape[1] // 3
+    stride = rows + depth + 8
+    stride += -stride % 8
+    return pl.pallas_call(
+        functools.partial(finish_kernel, rows=rows, depth=depth, stride=stride),
+        out_shape=(jax.ShapeDtypeStruct(pos.shape, jnp.float32),) * 2,
+        in_specs=[SMEM_SPEC] + [VMEM_SPEC] * 3,
+        out_specs=(VMEM_SPEC,) * 2,
+        scratch_shapes=[pltpu.VMEM((3 * stride, 128), jnp.float32)],
+        name="finish",
+    )(starts, data, pos, noise)
 
 
 ERFCX_COEF = (0.06548172872398669,
@@ -281,39 +527,39 @@
 
 
 def shards(positions, noise, route, node_perm, pair_first, pair_second, pair_count):
-    forces = bonded_forces(positions)
     n_gx = lax.axis_size("gx")
     n_gy = lax.axis_size("gy")
-    devices = n_gx * n_gy
+    both = ("gx", "gy")
+    peers = n_gx * n_gy
     slots = node_perm.shape[2]
-    per_peer = slots // devices
-    row_gx = lax.axis_index("gx")
-    own_order = node_perm[row_gx, 0]
-    stacked = jnp.concatenate([positions, forces], axis=0)
-    outgoing = (
-        jnp.zeros((6, slots), jnp.float32).at[:, route].set(stacked).reshape(6, devices, per_peer)
-    )
-    incoming = lax.all_to_all(outgoing, ("gx", "gy"), split_axis=1, concat_axis=1, tiled=True)
-    grid_data = jnp.zeros((6, slots), jnp.float32).at[:, own_order].set(incoming.reshape(6, slots))
+    depth = slots // peers // 128
+    rows = positions.shape[1] // 128
+    rp = slots // 128
+    swap = partial(lax.all_to_all, axis_name=both, split_axis=0, concat_axis=0, tiled=True)
+
+    bounds = jnp.arange(peers + 1, dtype=jnp.int32) * (slots // peers)
+    starts = jnp.sum(route[None, :] < bounds[:, None], axis=1, dtype=jnp.int32)
+    taken = swap(slots_call(starts, route.reshape(rows, 128), depth))
+    places = positions.reshape(3, rows, 128)
+    data = swap(pack_call(starts, places, depth))
+    counts = jnp.sum(taken >= 0, axis=(1, 2), dtype=jnp.int32)
+    own_order = lax.dynamic_index_in_dim(node_perm, lax.axis_index("gx"), 0, False)
+    nodes = nodes_call(taken, own_order.reshape(peers, depth, 128), slots).reshape(slots)
+    grid_data = scatter_call(nodes, counts, data, rp)
+
     beside_data = shifted(grid_data, "gx", -1)
     near_vel, far_vel = pair_call(
         pair_first[0],
         pair_second[0],
         pair_count,
-        grid_data.reshape(6, slots // 128, 128),
-        beside_data.reshape(6, slots // 128, 128),
-    )
-    wave_vel = kspace_part(grid_data[3:], n_gx, n_gy)
-    own_vel = near_vel.reshape(3, slots) + wave_vel
-    own_vel = own_vel + shifted(far_vel.reshape(3, slots), "gx", 1)
-    back_msg = own_vel[:, own_order].reshape(3, devices, per_peer)
-    arrived = lax.all_to_all(
-        back_msg, ("gx", "gy"), split_axis=1, concat_axis=1, tiled=True
-    ).reshape(3, slots)
-    velocity = arrived[:, route]
-    drift = time_step * velocity
-    moved = positions + drift + noise
-    return (moved, drift)
+        grid_data.reshape(6, rp, 128),
+        beside_data.reshape(6, rp, 128),
+    )
+    wave_vel = kspace_part(grid_data[3 * rp :], n_gx, n_gy).reshape(3 * rp, 128)
+    back_vel = shifted(far_vel.reshape(3 * rp, 128), "gx", 1)
+    back = swap(gather_call(nodes, counts, near_vel.reshape(3 * rp, 128), wave_vel, back_vel, depth))
+    moved, drift = finish_call(starts, back, places, noise.reshape(3, rows, 128))
+    return (moved.reshape(positions.shape), drift.reshape(positions.shape))
 
 
 def solution(mesh):

time: 1580 us -> 939 us (0.59)
  local copies, waits for them, and re-layouts: 927 us -> 113 us
  starting transfers between devices: 37.4 us -> 173 us
  Pallas kernels: 291 us -> 332 us
  other arithmetic: 65.2 us -> 41.5 us
  waiting for transfers between devices: 142 us -> 162 us
    gather x2 -> x0, local copies, waits for them, and re-layouts: 347 us -> none  [the longest x1 228 us: shards(): back_msg = own_vel[:, own_order].reshape(3, devices, per_peer)]
    scatter x3 -> x0, local copies, waits for them, and re-layouts: 285 us -> none  [the longest x2 191 us: shards(): jnp.zeros((6, slots), jnp.float32).at[:, own_order]]
    pallas_call x0 -> x6, Pallas kernels: none -> 165 us  [the longest x1 69.1 us: gather_call(): pl.pallas_call(functools.partial(gather_kernel, depth=depth, rp=rp), out_...]
    ppermute x2, starting transfers between devices: 4.79 us -> 133 us  [shifted(): lax.ppermute(value, axis, [(i, (i + by) % devices) for i in range(devices)])]
    pallas_call x1, Pallas kernels: 291 us -> 167 us  [pair_call(): pl.pallas_call(functools.partial(pair_kernel, rp=rp, coef=coef, unroll=un...]
    reshape x7 -> x0, local copies, waits for them, and re-layouts: 93 us -> none  [the longest x1 19.5 us: kspace_part(): force_field = force_rows.reshape(3, local_x, local_y, G)]
    unnamed x38 -> x36, local copies, waits for them, and re-layouts: 88.3 us -> 59.1 us
    ppermute x2, waiting for transfers between devices: 28.7 us -> 54.4 us  [shifted(): lax.ppermute(value, axis, [(i, (i + by) % devices) for i in range(devices)])]
  transfers between devices with their start and end apart: 7 -> 8, of which waited for: 6 -> 5; matrix products, arithmetic and copies ran while one was open for 5% -> 4% of each run, Pallas kernels for 18% -> 20%
where the time goes in v2:
time: 939 us; the launch traced here: 934 us
  Pallas kernels  332 us (35%)
  starting transfers between devices  173 us (18%)
  waiting for transfers between devices  162 us (17%)
  local copies, waits for them, and re-layouts  113 us (12%)
  matrix products  86.9 us (9%)
  other arithmetic  41.5 us (4%)
  blocking collectives  24.7 us (3%)
    pallas_call x1, Pallas kernels, pair_call(): pl.pallas_call(functools.partial(pair_kernel, rp=rp, coef=coef, unroll=un...  167 us
    ppermute x2, starting transfers between devices, shifted(): lax.ppermute(value, axis, [(i, (i + by) % devices) for i in range(devices)])  133 us
    pallas_call x1, Pallas kernels, gather_call(): pl.pallas_call(functools.partial(gather_kernel, depth=depth, rp=rp), out_...  69.1 us
    pallas_call x1, Pallas kernels, scatter_call(): pl.pallas_call(functools.partial(scatter_kernel, depth=depth, rp=rp), out...  66.6 us
    unnamed x36, local copies, waits for them, and re-layouts  59.1 us
    ppermute x2, waiting for transfers between devices, shifted(): lax.ppermute(value, axis, [(i, (i + by) % devices) for i in range(devices)])  54.4 us
    all_to_all x1, waiting for transfers between devices, kspace_part(): lax.all_to_all(spec_z[:, :, None], 'gx', split_axis=5, concat_axis=2, til...  38.7 us
    all_to_all x1, waiting for transfers between devices, shards(): data = swap(pack_call(starts, places, depth))  29.8 us
  transfers between devices with their start and end apart: 8, of which 5 were waited for; matrix products, arithmetic and copies ran while one was open for 4% of the time, Pallas kernels for 20%

profile of v2, /device:TPU:0, one launch (start us, length us, event | category | flops | bytes accessed | tf_op | source)
XLA Modules:
  0.0 934.4 jit_solution(7689561103986768353)
XLA Ops:
  6.9 7.3 all-to-all-start
  16.1 14.7 %pack.1 = f32[32,96,128]{2,1,0:T(8,128)} custom-call(s32[33]{0:T(128)} %convert_reduce_fusion.starts, f32[3,256,128]{2,1,0:T(8,128)} %bitcast.303), custom_call_target="tpu_custom_call" | custom-call | tf_op jit(solution)/shard_map/pack/pallas_call | solution.py:124
  30.8 5.9 all-to-all-start.1
  44.3 29.8 %all-to-all-done.1.in_ref = f32[32,96,128]{2,1,0:T(8,128)} async-done(((f32[32,96,128]{2,1,0:T(8,128)}), f32[32,96,128]{2,1,0:T(8,128)}, u32[]{:S(2)}, u32[]{:S(2)}) %all-to-all-start.1) | async-done | bytes 1572896 | tf_op jit(solution)/shard_map/all_to_all | solution.py:544
  75.1 66.6 %scatter.1 = f32[3072,128]{1,0:T(8,128)S(1)} custom-call(s32[65536]{0:T(1024)S(1)} %bitcast.281, s32[32]{0:T(128)S(1)} %convert_reduce_fusion.1.counts, f32[32,96,128]{2,1,0:T(8,128)} %all-to-all-done.1.in_ref), custom_call_target="tpu_custom_call" | custom-call | tf_op jit(solution)/shard_map/scatter/pallas_call | solution.py:195
  145.1 6.9 copy.41
  152.0 7.7 reshape.323
  159.7 5.9 all-to-all-start.2
  165.6 38.7 %all-to-all-done.2 = f32[8,1,49152]{2,1,0:T(1,128)} async-done(((f32[8,1,49152]{2,1,0:T(1,128)}), f32[8,1,49152]{2,1,0:T(1,128)}, u32[]{:S(2)}, u32[]{:S(2)}) %all-to-all-start.2) | async-done | bytes 1572896 | tf_op jit(solution)/shard_map/all_to_all | solution.py:500
  204.7 6.9 reduce
  211.7 6.1 reshape.324
  226.8 5.6 fusion.13
  244.1 6.9 copy.44
  251.0 5.9 reshape.325
  261.6 19.8 %all-to-all-done.3 = f32[4,1,98304]{2,1,0:T(1,128)} async-done(((f32[4,1,98304]{2,1,0:T(1,128)}), f32[4,1,98304]{2,1,0:T(1,128)}, u32[]{:S(2)}, u32[]{:S(2)}) %all-to-all-start.3) | async-done | bytes 1572896 | tf_op jit(solution)/shard_map/all_to_all | solution.py:502
  281.4 7.3 reduce.1
  288.7 6.3 reshape.326
  295.0 6.4 copy.45
  338.7 5.9 reshape.327
  344.7 24.7 %all_to_all.75 = f32[4,1,98304]{2,1,0:T(1,128)} all-to-all(f32[4,1,98304]{2,1,0:T(1,128)} %reshape.327), channel_id=1, replica_groups=mesh['gx'=8,'gy'=4] {'gy'}, dimensions={0} | all-to-all | bytes 3145728 | tf_op jit(solution)/shard_map/all_to_all | solution.py:516
  369.3 7.3 reduce.2
  376.6 6.3 reshape.328
  396.6 5.6 fusion.30
  427.5 7.7 reshape.329
  444.9 54.4 %collective-permute-done = f32[3072,128]{1,0:T(8,128)S(1)} collective-permute-done((f32[3072,128]{1,0:T(8,128)S(1)}, f32[3072,128]{1,0:T(8,128)S(1)}, u32[]{:S(2)}, u32[]{:S(2)}) %collective-permute-start) | collective-permute-done | bytes 1572896 | tf_op jit(solution)/shard_map/ppermute | solution.py:29
  499.3 166.9 %pairs.1 = (f32[3,512,128]{2,1,0:T(8,128)S(1)}, f32[3,512,128]{2,1,0:T(8,128)}) custom-call(s32[1024]{0:T(1024)S(1)} %bitcast.285, s32[1024]{0:T(1024)S(1)} %bitcast.286, s32[1]{0:T(128)S(6)} %copy.100.count, f32[6,512,128]{2,1,0:T(8,128)S(1)} %bitcast.280, f32[6,512,128]{2,1,0:T(8,128)S(1)} %bitcast.283), custom_call_target="tpu_custom_call" | custom-call | tf_op jit(solution)/shard_map/pairs/pallas_call | solution.py:419
  666.2 127.9 %collective-permute-start.1 = (f32[1536,128]{1,0:T(8,128)}, f32[1536,128]{1,0:T(8,128)}, u32[]{:S(2)}, u32[]{:S(2)}) collective-permute-start(f32[1536,128]{1,0:T(8,128)} %bitcast.98), channel_id=1, source_target_pairs={{0,4},{4,8},{8,12},{12,16},{16,20},{20,24},{24,28},{28,0},{1,5},{5... | collective-permute-start | bytes 2359304 | tf_op jit(solution)/shard_map/ppermute | solution.py:29
  794.1 5.8 reduce.3
  816.3 6.0 fusion.17
  822.3 69.1 %gather.1 = f32[32,48,128]{2,1,0:T(8,128)} custom-call(s32[65536]{0:T(1024)S(1)} %bitcast.282, s32[32]{0:T(128)S(1)} %convert_reduce_fusion.1.counts, f32[1536,128]{1,0:T(8,128)S(1)} %bitcast.284, f32[1536,128]{1,0:T(8,128)} %bitcast.305, f32[1536,128]{1,0:T(8,128)} %collective-permute-done.1.three_ref), custom_call_target="tpu_custom_call" | custom-call | tf_op jit(solution)/shard_map/gather/pallas_call | solution.py:236
  891.3 12.2 %all-to-all-start.6 = ((f32[32,48,128]{2,1,0:T(8,128)}), f32[32,48,128]{2,1,0:T(8,128)S(1)}, u32[]{:S(2)}, u32[]{:S(2)}) async-start(f32[32,48,128]{2,1,0:T(8,128)} %gather.1), calls=%async_computation.6 | async-start | bytes 1572864 | tf_op jit(solution)/shard_map/all_to_all | solution.py:560
  904.4 19.8 %all-to-all-done.6.in_ref = f32[32,48,128]{2,1,0:T(8,128)S(1)} async-done(((f32[32,48,128]{2,1,0:T(8,128)}), f32[32,48,128]{2,1,0:T(8,128)S(1)}, u32[]{:S(2)}, u32[]{:S(2)}) %all-to-all-start.6) | async-done | bytes 786464 | tf_op jit(solution)/shard_map/all_to_all | solution.py:560
  (85 shorter events, 158.2 us)
Async XLA Ops:
  0.6 36.1 %copy-start = (s32[8,1,65536]{2,1,0:T(1,128)S(1)}, s32[8,1,65536]{2,1,0:T(1,128)}, u32[]{:S(2)}) copy-start(s32[8,1,65536]{2,1,0:T(1,128)} %param.10) | copy-start | bytes 6291460
  6.9 23.8 %all-to-all-start = ((s32[32,16,128]{2,1,0:T(8,128)}), s32[32,16,128]{2,1,0:T(8,128)S(1)}, u32[]{:S(2)}, u32[]{:S(2)}) async-start(s32[32,16,128]{2,1,0:T(8,128)} %slots.1), calls=%async_computation | async-start | bytes 524288 | tf_op jit(solution)/shard_map/all_to_all | solution.py:542
  30.8 6.7 copy-start.10
  30.8 43.4 %all-to-all-start.1 = ((f32[32,96,128]{2,1,0:T(8,128)}), f32[32,96,128]{2,1,0:T(8,128)}, u32[]{:S(2)}, u32[]{:S(2)}) async-start(f32[32,96,128]{2,1,0:T(8,128)} %pack.1), calls=%async_computation.1 | async-start | bytes 3145728 | tf_op jit(solution)/shard_map/all_to_all | solution.py:544
  74.2 1.0 copy-start.2
  159.7 44.6 %all-to-all-start.2 = ((f32[8,1,49152]{2,1,0:T(1,128)}), f32[8,1,49152]{2,1,0:T(1,128)}, u32[]{:S(2)}, u32[]{:S(2)}) async-start(f32[8,1,49152]{2,1,0:T(1,128)} %reshape.323), calls=%async_computation.2 | async-start | bytes 3145728 | tf_op jit(solution)/shard_map/all_to_all | solution.py:500
  257.0 24.5 %all-to-all-start.3 = ((f32[4,1,98304]{2,1,0:T(1,128)}), f32[4,1,98304]{2,1,0:T(1,128)}, u32[]{:S(2)}, u32[]{:S(2)}) async-start(f32[4,1,98304]{2,1,0:T(1,128)} %reshape.325), calls=%async_computation.3 | async-start | bytes 3145728 | tf_op jit(solution)/shard_map/all_to_all | solution.py:502
  396.6 5.6 copy-start.7
  410.5 5.3 copy-start.6
  410.5 5.3 copy-start.8
  435.1 64.1 %copy-start.4 = (s32[1,1024]{1,0:T(1,128)S(1)}, s32[1,1024]{1,0:T(1,128)}, u32[]{:S(2)}) copy-start(s32[1,1024]{1,0:T(1,128)} %param.11) | copy-start | bytes 12292
  435.1 64.1 %copy-start.5 = (s32[1,1024]{1,0:T(1,128)S(1)}, s32[1,1024]{1,0:T(1,128)}, u32[]{:S(2)}) copy-start(s32[1,1024]{1,0:T(1,128)} %param.12) | copy-start | bytes 12292
  435.1 359.0 %all-to-all-start.5 = ((f32[8,1,49152]{2,1,0:T(1,128)}), f32[8,1,49152]{2,1,0:T(1,128)}, u32[]{:S(2)}, u32[]{:S(2)}) async-start(f32[8,1,49152]{2,1,0:T(1,128)} %reshape.329), calls=%async_computation.5 | async-start | bytes 3145728 | tf_op jit(solution)/shard_map/all_to_all | solution.py:520
  439.6 59.7 %collective-permute-start = (f32[3072,128]{1,0:T(8,128)S(1)}, f32[3072,128]{1,0:T(8,128)S(1)}, u32[]{:S(2)}, u32[]{:S(2)}) collective-permute-start(f32[3072,128]{1,0:T(8,128)S(1)} %scatter.1), channel_id=1, source_target_pairs={{0,28},{4,0},{8,4},{12,8},{16,12},{20,16},{24,20},{28,24},{1,29},{... | collective-permute-start | bytes 4718600 | tf_op jit(solution)/shard_map/ppermute | solution.py:29
  666.2 156.0 %collective-permute-start.1 = (f32[1536,128]{1,0:T(8,128)}, f32[1536,128]{1,0:T(8,128)}, u32[]{:S(2)}, u32[]{:S(2)}) collective-permute-start(f32[1536,128]{1,0:T(8,128)} %bitcast.98), channel_id=1, source_target_pairs={{0,4},{4,8},{8,12},{12,16},{16,20},{20,24},{24,28},{28,0},{1,5},{5... | collective-permute-start | bytes 2359304 | tf_op jit(solution)/shard_map/ppermute | solution.py:29
  816.2 6.0 copy-start.3
  822.2 81.3 %copy-start.11 = (f32[3,32768]{1,0:T(4,128)S(1)}, f32[3,32768]{1,0:T(4,128)}, u32[]{:S(2)}) copy-start(f32[3,32768]{1,0:T(4,128)} %param.8) | copy-start | bytes 1179652
  822.3 111.9 %copy-start.1 = (s32[8,1,65536]{2,1,0:T(1,128)S(1)}, s32[8,1,65536]{2,1,0:T(1,128)}, u32[]{:S(2)}) copy-start(s32[8,1,65536]{2,1,0:T(1,128)} %param.10) | copy-start | bytes 6291460
  891.3 32.8 %all-to-all-start.6 = ((f32[32,48,128]{2,1,0:T(8,128)}), f32[32,48,128]{2,1,0:T(8,128)S(1)}, u32[]{:S(2)}, u32[]{:S(2)}) async-start(f32[32,48,128]{2,1,0:T(8,128)} %gather.1), calls=%async_computation.6 | async-start | bytes 1572864 | tf_op jit(solution)/shard_map/all_to_all | solution.py:560
  924.2 0.9 copy-start.9

commit v3 on v2

--- a/solution.py
+++ b/solution.py
@@ -4,6 +4,7 @@
 
 import jax
 import jax.numpy as jnp
+import numpy as np
 from jax import lax
 from jax.experimental import pallas as pl
 from jax.experimental.pallas import tpu as pltpu
@@ -302,118 +303,100 @@
     7.010614160106155e-05)
 
 
-def pair_math(dx, dy, dz, coef):
-    s2 = dx*dx + dy*dy + dz*dz + 0.25
-    u = lax.rsqrt(s2)
-    r = s2*u
-    t = pl.reciprocal(1.0 + 0.2*r)
-    w = coef[0]*t + coef[1]
+def pair_math(square, coef):
+    inverse = lax.rsqrt(square)
+    ratio = pl.reciprocal(1.0 + 0.2 * (square * inverse))
+    scaled = coef[0] * ratio + coef[1]
     for k in coef[2:]:
-        w = w*t + k
-    ex = jnp.exp(-0.25*s2)
-    u2 = u*u
-    a = w*u
-    f = ex*(a*(0.375 + 0.0625*u2) + 0.125)
-    h = ex*u2*(a*(0.375 - 0.1875*u2) - 0.125)
-    return f, h
-
-def pair_kernel(first, second, count, own_ref, far_ref, vown_ref, vfar_ref, pc, xr, vc, vr, *, rp, coef, unroll):
+        scaled = scaled * ratio + k
+    decay = jnp.exp(-0.25 * square)
+    inverse_sq = inverse * inverse
+    screen = scaled * inverse
+    along = decay * (screen * (0.375 + 0.0625 * inverse_sq) + 0.125)
+    across = (decay * inverse_sq) * (screen * (0.375 - 0.1875 * inverse_sq) - 0.125)
+    return along, across
+
+def pair_kernel(first, second, count, own_ref, far_ref, vown_ref, vfar_ref, cells, sums, *, rp, coef, unroll):
     lane = lax.broadcasted_iota(jnp.int32, (8, 128), 1)
     sub = lax.broadcasted_iota(jnp.int32, (8, 128), 0)
     left = lane < 64
-    groups = rp // 4
+    unturn = (lane + sub) & 127
 
     @pl.loop(0, rp // 8)
     def _(i):
+        at = pl.ds(pl.multiple_of(i * 8, 8), 8)
         for src, off in ((own_ref, 0), (far_ref, rp)):
             for c in range(6):
-                pc[pl.ds((off + i*8)*8 + c, 8, stride=8), :] = src[c, pl.ds(pl.multiple_of(i*8, 8), 8), :]
-            for c in (6, 7):
-                pc[pl.ds((off + i*8)*8 + c, 8, stride=8), :] = jnp.zeros((8, 128), jnp.float32)
-            vc[pl.ds(pl.multiple_of((off + i*8)*8, 64), 64), :] = jnp.zeros((64, 128), jnp.float32)
-
-    lane32 = lax.broadcasted_iota(jnp.int32, (32, 128), 1)
-
-    @pl.loop(0, groups)
-    def _(g):
-        blk = pc[pl.ds(pl.multiple_of(g*32, 32), 32), :]
-        tr = jnp.transpose(blk)
-        tr = jnp.concatenate([tr[32*b:32*b + 32, :] for b in range(4)], axis=1)
-        xr[pl.ds(pl.multiple_of(g*32, 32), 32), :] = tr
-        vr[pl.ds(pl.multiple_of(g*32, 32), 32), :] = jnp.zeros((32, 128), jnp.float32)
-
-    total = count[0]
+                cells[pl.ds((off + i * 8) * 8 + c, 8, stride=8), :] = src[c, at, :]
+            sums[pl.ds(pl.multiple_of((off + i * 8) * 8, 64), 64), :] = jnp.zeros((64, 128), jnp.float32)
+
+    def both_halves(k):
+        cell = cells[pl.ds(pl.multiple_of((k >> 1) * 8, 8), 8), :]
+        return jnp.where(left == ((k & 1) == 0), cell, pltpu.roll(cell, 64, 1))
+
+    def stacked(parts):
+        out = jnp.zeros((8, 128), jnp.float32)
+        for c, part in enumerate(parts):
+            out = jnp.where(sub == c, jnp.sum(part, axis=0, keepdims=True), out)
+        return out
 
     def one(p):
         ka = first[p]
         kb = second[p]
-        jv = pc[pl.ds(pl.multiple_of((kb >> 1)*8, 8), 8), :]
-        dup = jnp.where(left == ((kb & 1) == 0), jv, pltpu.roll(jv, 64, 1))
-        xj = [jnp.broadcast_to(dup[c:c+1, :], (8, 128)) for c in range(6)]
-        base = (ka & 1)*64 + ((ka >> 1) & 3)*8
-        idx0 = base + jnp.where(left, 0, 32)
-        row0 = pl.multiple_of((ka >> 3)*32, 32)
-        facc = [jnp.zeros((8, 128), jnp.float32) for _ in range(3)]
-        near = []
-        for q in range(4):
-            row = xr[pl.ds(row0 + 8*q, 8), :]
-            xi = [jnp.take_along_axis(row, idx0 + c, axis=1) for c in range(6)]
-            d = [xi[c] - xj[c] for c in range(3)]
-            f, h = pair_math(d[0], d[1], d[2], coef)
-            dj = d[0]*xj[3] + d[1]*xj[4] + d[2]*xj[5]
-            di = d[0]*xi[3] + d[1]*xi[4] + d[2]*xi[5]
-            hj = h*dj
-            hi = h*di
-            val = jnp.zeros((8, 128), jnp.float32)
-            for c in range(3):
-                nv = f*xj[3+c] + hj*d[c]
-                lo = jnp.sum(jnp.where(left, nv, 0.0), axis=1, keepdims=True)
-                hi_ = jnp.sum(jnp.where(left, 0.0, nv), axis=1, keepdims=True)
-                val = jnp.where(lane == base + c, lo, val)
-                val = jnp.where(lane == base + 32 + c, hi_, val)
-                facc[c] = facc[c] + (f*xi[3+c] + hi*d[c])
-            near.append(val)
-        fv = jnp.zeros((8, 128), jnp.float32)
-        for c in range(3):
-            s = jnp.sum(facc[c], axis=0, keepdims=True)
-            fv = jnp.where(sub == c, s, fv)
-        fv = fv + pltpu.roll(fv, 64, 1)
-        keep = (left == ((kb & 1) == 0)) & (ka != kb)
-        fv = jnp.where(keep, fv, 0.0)
-        return row0, near, kb, fv
+        near = both_halves(ka)
+        near = jnp.where(left, near, pltpu.roll(near, 96, 1))
+        far = both_halves(kb)
+        mine = [jnp.broadcast_to(near[c : c + 1, :], (8, 128)) for c in range(6)]
+        other = [jnp.broadcast_to(far[c : c + 1, :], (8, 128)) for c in range(6)]
+        near_sum = None
+        far_sum = None
+        for q in (3, 2, 1, 0):
+            turned = [pltpu.roll(x, 8 * q, 1, stride=1, stride_axis=0) for x in other]
+            gap = [mine[c] - turned[c] for c in range(3)]
+            along, across = pair_math(gap[0] * gap[0] + gap[1] * gap[1] + gap[2] * gap[2] + 0.25, coef)
+            to_near = across * (gap[0] * turned[3] + gap[1] * turned[4] + gap[2] * turned[5])
+            to_far = across * (gap[0] * mine[3] + gap[1] * mine[4] + gap[2] * mine[5])
+            near_add = [along * turned[3 + c] + to_near * gap[c] for c in range(3)]
+            far_add = [along * mine[3 + c] + to_far * gap[c] for c in range(3)]
+            if near_sum is None:
+                near_sum, far_sum = near_add, far_add
+            else:
+                near_sum = [a + b for a, b in zip(near_sum, near_add)]
+                far_sum = [pltpu.roll(a, 120, 1) + b for a, b in zip(far_sum, far_add)]
+        far_sum = [jnp.take_along_axis(a, unturn, axis=1) for a in far_sum]
+        near_vel = stacked(near_sum)
+        half = jnp.where(left, pltpu.roll(near_vel, 64, 1), 0.0)
+        near_vel = jnp.where(left, near_vel, 0.0) + pltpu.roll(half, 32, 1)
+        near_vel = near_vel + pltpu.roll(near_vel, 64, 1)
+        far_vel = stacked(far_sum)
+        far_vel = far_vel + pltpu.roll(far_vel, 64, 1)
+        return ka, near_vel, kb, far_vel
+
+    total = count[0]
 
     def turn(i, carry):
-        outs = []
+        found = []
         for k in range(unroll):
-            outs.append((i*unroll + k, one(i*unroll + k)))
-        for p, (row0, near, kb, fv) in outs:
-            alive = (p < total).astype(jnp.float32) if unroll > 1 else None
-            if unroll > 1:
-                near = [n*alive for n in near]
-                fv = fv*alive
-            for q in range(4):
-                at = pl.ds(row0 + 8*q, 8)
-                vr[at, :] = vr[at, :] + near[q]
-            at = pl.ds(pl.multiple_of((kb >> 1)*8, 8), 8)
-            vc[at, :] = vc[at, :] + fv
+            p = i * unroll + k
+            found.append((p < total, one(p)))
+        for alive, (ka, near_vel, kb, far_vel) in found:
+            at = pl.ds(pl.multiple_of((ka >> 1) * 8, 8), 8)
+            sums[at, :] = sums[at, :] + jnp.where((left == ((ka & 1) == 0)) & alive, near_vel, 0.0)
+            at = pl.ds(pl.multiple_of((kb >> 1) * 8, 8), 8)
+            keep = (left == ((kb & 1) == 0)) & (alive & (ka != kb))
+            sums[at, :] = sums[at, :] + jnp.where(keep, far_vel, 0.0)
         return carry
 
     lax.fori_loop(0, lax.div(total + (unroll - 1), jnp.int32(unroll)), turn, 0)
 
-    @pl.loop(0, groups)
-    def _(g):
-        m = vr[pl.ds(pl.multiple_of(g*32, 32), 32), :]
-        st = jnp.concatenate([m[:, 32*b:32*b + 32] for b in range(4)], axis=0)
-        at = pl.ds(pl.multiple_of(g*32, 32), 32)
-        vc[at, :] = vc[at, :] + jnp.transpose(st)
-
     @pl.loop(0, rp // 8)
     def _(i):
+        at = pl.ds(pl.multiple_of(i * 8, 8), 8)
         for dst, off in ((vown_ref, 0), (vfar_ref, rp)):
             for c in range(3):
-                dst[c, pl.ds(pl.multiple_of(i*8, 8), 8), :] = vc[pl.ds((off + i*8)*8 + c, 8, stride=8), :]
-
-def pair_call(first, second, count, own, far, coef=ERFCX_COEF, unroll=1):
+                dst[c, at, :] = sums[pl.ds((off + i * 8) * 8 + c, 8, stride=8), :]
+
+def pair_call(first, second, count, own, far, coef=ERFCX_COEF, unroll=8):
     rp = own.shape[1]
     f32 = jnp.float32
     return pl.pallas_call(
@@ -421,8 +404,7 @@
         out_shape=(jax.ShapeDtypeStruct((3, rp, 128), f32),)*2,
         in_specs=[pl.BlockSpec(memory_space=pltpu.SMEM)]*3 + [pl.BlockSpec(memory_space=pltpu.VMEM)]*2,
         out_specs=(pl.BlockSpec(memory_space=pltpu.VMEM),)*2,
-        scratch_shapes=[pltpu.VMEM((2*rp*8, 128), f32), pltpu.VMEM((rp*8, 128), f32),
-                        pltpu.VMEM((2*rp*8, 128), f32), pltpu.VMEM((rp*8, 128), f32)],
+        scratch_shapes=[pltpu.VMEM((2*rp*8, 128), f32), pltpu.VMEM((2*rp*8, 128), f32)],
         compiler_params=pltpu.CompilerParams(vmem_limit_bytes=48*1024*1024),
         name="pairs",
     )(first, second, count, own, far)
@@ -526,6 +508,263 @@
     return (result / float(G**3)).reshape(3, local_x * local_y * G)
 
 
+matmul = functools.partial(lax.dot_general, precision=lax.Precision.HIGHEST, preferred_element_type=jnp.float32)
+PLAIN = (((1,), (0,)), ((), ()))
+TURNED = (((1,), (1,)), ((), ()))
+
+
+def wave_tables(n_gx, n_gy):
+    share = G // 2 // n_gx
+    width = G // n_gy
+    grid = np.arange(G)
+    turn = 2.0 * math.pi * (np.outer(grid, grid) % G) / G
+    cos, sin = np.cos(turn), np.sin(turn)
+    half = width // 2
+    order = np.zeros(G, np.int64)
+    for j in range(n_gy):
+        for p in range(half):
+            k = j * half + p
+            order[j * width + p] = k
+            order[j * width + half + p] = (G - k) % G if k else G // 2
+    ahead = np.zeros((G, n_gx, 2, share))
+    ahead[:, :, 0] = cos[:, : G // 2].reshape(G, n_gx, share)
+    ahead[:, :, 1] = -sin[:, : G // 2].reshape(G, n_gx, share)
+    back = 2.0 * ahead
+    ahead[:, 0, 1, 0] = cos[:, G // 2]
+    back[:, 0, 0, 0] = 1.0
+    back[:, 0, 1, 0] = cos[:, G // 2]
+    unit = 2.0 * math.pi / (G * grid_spacing)
+    signed = np.where(grid < G // 2, grid, grid - G) * unit
+    plain = np.where(grid == G // 2, 0.0, signed)
+    edge = signed - plain
+    lane = np.arange(128)
+    across = np.zeros((n_gy, 8, 128))
+    across[:, 0] = plain[order].reshape(n_gy, 1, width)[:, 0][:, lane % width]
+    across[:, 1] = edge[order].reshape(n_gy, 1, width)[:, 0][:, lane % width]
+    across[0, 2] = lane % half == 0
+    deep = np.zeros((n_gx, 8, 128))
+    per = 128 // width
+    for v in range(share // per):
+        deep[:, v] = (np.arange(n_gx)[:, None] * share + v * per + lane // width) * unit
+    down = np.stack([np.broadcast_to(t[:, None], (G, 128)) for t in (plain, edge)])
+    tables = {
+        "ahead": ahead.reshape(G, G),
+        "back": back.reshape(G, G).T,
+        "first": np.concatenate([cos[:, order], sin[:, order]], axis=1),
+        "first_back": np.concatenate([cos[:, order], sin[:, order]], axis=1),
+        "second": np.concatenate([cos, sin], axis=0),
+        "across": across,
+        "deep": deep,
+        "down": down,
+    }
+    return {name: np.asarray(table, np.float32) for name, table in tables.items()}
+
+
+def spread(tiles, at, group, tall):
+    count = 128 // group
+    lane = lax.shift_right_logical(lax.broadcasted_iota(jnp.int32, (tall, 128), 1), group.bit_length() - 1)
+    out = None
+    for g, tile in enumerate(tiles):
+        moved = pltpu.roll(tile, group * ((g - at) % count), 1) if g != at else tile
+        out = moved if out is None else jnp.where(lane == g, moved, out)
+    return out
+
+
+def depth_kernel(field_ref, table_ref, out_ref, spec, *, n_gx, tall, wide):
+    rows = tall * wide
+    for c in range(3):
+        spec[c * rows : (c + 1) * rows, :] = matmul(field_ref[c * rows : (c + 1) * rows, :], table_ref[...], PLAIN)
+    group = G // n_gx
+    count = n_gx
+
+    @pl.loop(0, 3 * wide // count)
+    def _(i):
+        c = lax.div(i, jnp.int32(wide // count))
+        b = (i - c * (wide // count)) * count
+        tiles = [spec[pl.ds(c * rows + b + g, tall, stride=wide), :] for g in range(count)]
+        for p in range(n_gx):
+            out_ref[p, :, pl.ds(pl.multiple_of(i * 128, 128), 128)] = spread(tiles, p, group, tall)
+
+
+def first_kernel(data_ref, table_ref, out_ref, turned, *, n_gy, share, wide):
+    group = G // n_gy
+    per = 128 // (2 * share)
+
+    @pl.loop(0, 3 * wide // per)
+    def _(i):
+        c = lax.div(i, jnp.int32(wide // per))
+        b = (i - c * (wide // per)) * per
+        piece = jnp.transpose(data_ref[:, pl.ds(pl.multiple_of(i * 128, 128), 128)])
+        both = matmul(piece, table_ref[...], PLAIN)
+        for g in range(per):
+            lo, mid, hi = g * 2 * share, (g * 2 + 1) * share, (g * 2 + 2) * share
+            real = both[lo:mid, :128] + both[mid:hi, 128:]
+            imag = both[mid:hi, :128] - both[lo:mid, 128:]
+            turned[pl.ds(2 * c * share * wide + b + g, share, stride=wide), :] = real
+            turned[pl.ds((2 * c + 1) * share * wide + b + g, share, stride=wide), :] = imag
+
+    count = 128 // group
+
+    @pl.loop(0, 6 * share // count)
+    def _(i):
+        at = i * (count * wide)
+        tiles = [turned[pl.ds(pl.multiple_of(at + u * wide, 8), wide), :] for u in range(count)]
+        for j in range(n_gy):
+            out_ref[j, i] = spread(tiles, j, group, wide)
+
+
+def second_kernel(ids, data_ref, table_ref, across_ref, deep_ref, down_ref, out_ref, flow, *, n_gy, views, wide):
+    lane = lax.broadcasted_iota(jnp.int32, (G, 128), 1)
+    width = G // n_gy
+    half = width // 2
+    across = across_ref[ids[1]]
+    deep = deep_ref[ids[0]]
+    alone = (lane < width) & (ids[0] == 0)
+    mirror_self = across[2:3, :] > 0.5
+    upper = (lane & half) != 0
+
+    def whole(tile):
+        return jnp.concatenate([data_ref[j, tile] for j in range(n_gy)], axis=0)
+
+    def mirrored(value):
+        other = jnp.where(upper, pltpu.roll(value, half, 1), pltpu.roll(value, 128 - half, 1))
+        return jnp.where(mirror_self, value, other)
+
+    def ahead(real, imag):
+        one = matmul(table_ref[...], real, PLAIN)
+        two = matmul(table_ref[...], imag, PLAIN)
+        return one[:G] + two[G:], two[:G] - one[G:]
+
+    def projected(spectrum, deep_plain, deep_edge):
+        plain = (across[0:1, :], down_ref[0], deep_plain)
+        edge = (across[1:2, :], down_ref[1], deep_edge)
+        waves = [p + e for p, e in zip(plain, edge)]
+        wave_sq = waves[0] * waves[0] + waves[1] * waves[1] + waves[2] * waves[2]
+        live = wave_sq > 0
+        inverse = 1.0 / jnp.where(live, wave_sq, 1.0)
+        spread_sq = wave_sq / (4.0 * split_xi**2)
+        green = (1.0 - bead_radius**2 * wave_sq / 3.0) * (1.0 + spread_sq) * jnp.exp(-spread_sq) * inverse
+        green = jnp.where(live, green / float(G**3), 0.0)
+        out = []
+        for r in range(2):
+            regular = sum(w * spectrum[c][r] for c, w in enumerate(plain)) * inverse
+            nyquist = sum(w * spectrum[c][r] for c, w in enumerate(edge)) * inverse
+            out.append([green * (spectrum[c][r] - plain[c] * regular - edge[c] * nyquist) for c in range(3)])
+        return out
+
+    zero = jnp.zeros((1, 128), jnp.float32)
+    for v in range(views):
+        spectrum = []
+        apart = []
+        for c in range(3):
+            real = whole((2 * c) * views + v)
+            imag = whole((2 * c + 1) * views + v)
+            if v == 0:
+                off_real = jnp.where(alone, 0.5 * (real - mirrored(real)), 0.0)
+                off_imag = jnp.where(alone, 0.5 * (imag + mirrored(imag)), 0.0)
+                apart.append(ahead(off_real, off_imag))
+                real, imag = real - off_real, imag - off_imag
+            spectrum.append(ahead(real, imag))
+        found = projected(spectrum, deep[v : v + 1, :], zero)
+        if v == 0:
+            extra = projected(apart, zero, zero - math.pi / grid_spacing)
+            found = [[a + b for a, b in zip(one, two)] for one, two in zip(found, extra)]
+        for c in range(3):
+            one = matmul(table_ref[...], found[0][c], PLAIN)
+            two = matmul(table_ref[...], found[1][c], PLAIN)
+            real, imag = one[:G] - two[G:], two[:G] + one[G:]
+            for j in range(n_gy):
+                out_ref[j, (2 * c) * views + v] = real[j * wide : (j + 1) * wide]
+                out_ref[j, (2 * c + 1) * views + v] = imag[j * wide : (j + 1) * wide]
+
+
+def first_back_kernel(data_ref, table_ref, out_ref, turned, *, n_gy, share, wide):
+    group = G // n_gy
+    count = n_gy
+    per = 128 // (2 * share)
+
+    @pl.loop(0, 6 * share // count)
+    def _(i):
+        tiles = [data_ref[j, i] for j in range(n_gy)]
+        for u in range(count):
+            turned[pl.ds(pl.multiple_of((i * count + u) * wide, 8), wide), :] = spread(tiles, u, group, wide)
+
+    @pl.loop(0, 3 * wide // per)
+    def _(i):
+        c = lax.div(i, jnp.int32(wide // per))
+        b = (i - c * (wide // per)) * per
+        rows = []
+        for g in range(per):
+            real = turned[pl.ds(2 * c * share * wide + b + g, share, stride=wide), :]
+            imag = turned[pl.ds((2 * c + 1) * share * wide + b + g, share, stride=wide), :]
+            rows.append(jnp.concatenate([real, -imag], axis=1))
+            rows.append(jnp.concatenate([imag, real], axis=1))
+        piece = jnp.concatenate(rows, axis=0)
+        out_ref[:, pl.ds(pl.multiple_of(i * 128, 128), 128)] = matmul(table_ref[...], piece, TURNED)
+
+
+def depth_back_kernel(data_ref, table_ref, out_ref, spec, *, n_gx, tall, wide):
+    rows = tall * wide
+    group = G // n_gx
+    count = n_gx
+
+    @pl.loop(0, 3 * wide // count)
+    def _(i):
+        c = lax.div(i, jnp.int32(wide // count))
+        b = (i - c * (wide // count)) * count
+        tiles = [data_ref[p, :, pl.ds(pl.multiple_of(i * 128, 128), 128)] for p in range(n_gx)]
+        for g in range(count):
+            spec[pl.ds(c * rows + b + g, tall, stride=wide), :] = spread(tiles, g, group, tall)
+
+    for c in range(3):
+        out_ref[c * rows : (c + 1) * rows, :] = matmul(spec[c * rows : (c + 1) * rows, :], table_ref[...], PLAIN)
+
+
+def waves(grid_data, n_gx, n_gy):
+    tall, wide, share = G // n_gx, G // n_gy, G // 2 // n_gx
+    rows = 3 * tall * wide
+    views = share * wide // 128
+    tables = wave_tables(n_gx, n_gy)
+    f32 = jnp.float32
+
+    def run(name, kernel, shape, args, scratch, specs=None, **sizes):
+        return pl.pallas_call(
+            functools.partial(kernel, **sizes),
+            out_shape=jax.ShapeDtypeStruct(shape, f32),
+            in_specs=specs or [VMEM_SPEC] * len(args),
+            out_specs=VMEM_SPEC,
+            scratch_shapes=[pltpu.VMEM(scratch, f32)],
+            compiler_params=pltpu.CompilerParams(vmem_limit_bytes=24 * 1024 * 1024),
+            name=name,
+            grid=(1,),
+        )(*args)
+
+    def swap(value, axis):
+        return lax.all_to_all(value, axis, split_axis=0, concat_axis=0, tiled=True)
+
+    def full(shape):
+        return pl.BlockSpec(shape, lambda i: (0,) * len(shape))
+
+    force = pl.BlockSpec((rows, 128), lambda i: (1, 0))
+    lanes = 6 * wide * share
+    ids = jnp.stack([lax.axis_index("gx"), lax.axis_index("gy")]).astype(jnp.int32)
+    value = run("depth", depth_kernel, (n_gx, tall, lanes), (grid_data, tables["ahead"]), (rows, 128),
+                [force, full((G, 128))], n_gx=n_gx, tall=tall, wide=wide)
+    value = swap(value, "gx").reshape(G, lanes)
+    value = run("first", first_kernel, (n_gy, 6 * views, wide, 128), (value, tables["first"]), (rows, 128),
+                n_gy=n_gy, share=share, wide=wide)
+    value = swap(value.reshape(n_gy, 6 * views * wide, 128), "gy").reshape(n_gy, 6 * views, wide, 128)
+    args = (ids, value, tables["second"], tables["across"], tables["deep"], tables["down"])
+    value = run("second", second_kernel, (n_gy, 6 * views, wide, 128), args, (8, 128),
+                [SMEM_SPEC] + [VMEM_SPEC] * 5, n_gy=n_gy, views=views, wide=wide)
+    value = swap(value.reshape(n_gy, 6 * views * wide, 128), "gy").reshape(n_gy, 6 * views, wide, 128)
+    value = run("first_back", first_back_kernel, (G, lanes), (value, tables["first_back"]), (rows, 128),
+                n_gy=n_gy, share=share, wide=wide)
+    value = swap(value.reshape(n_gx, tall, lanes), "gx")
+    return run("depth_back", depth_back_kernel, (rows, 128), (value, tables["back"]), (rows, 128),
+               n_gx=n_gx, tall=tall, wide=wide)
+
+
 def shards(positions, noise, route, node_perm, pair_first, pair_second, pair_count):
     n_gx = lax.axis_size("gx")
     n_gy = lax.axis_size("gy")
@@ -555,7 +794,11 @@
         grid_data.reshape(6, rp, 128),
         beside_data.reshape(6, rp, 128),
     )
-    wave_vel = kspace_part(grid_data[3 * rp :], n_gx, n_gy).reshape(3 * rp, 128)
+    share = G // 2 // n_gx
+    if share % 8 == 0 and share * (G // n_gy) % 128 == 0:
+        wave_vel = waves(grid_data, n_gx, n_gy)
+    else:
+        wave_vel = kspace_part(grid_data[3 * rp :], n_gx, n_gy).reshape(3 * rp, 128)
     back_vel = shifted(far_vel.reshape(3 * rp, 128), "gx", 1)
     back = swap(gather_call(nodes, counts, near_vel.reshape(3 * rp, 128), wave_vel, back_vel, depth))
     moved, drift = finish_call(starts, back, places, noise.reshape(3, rows, 128))

time: 939 us -> 456 us (0.49)
  starting transfers between devices: 173 us -> 29.7 us
  local copies, waits for them, and re-layouts: 113 us -> 13.8 us
  waiting for transfers between devices: 162 us -> 73.1 us
  matrix products: 86.9 us -> 0 us
  other arithmetic: 41.5 us -> 3.98 us
  Pallas kernels: 332 us -> 296 us
  blocking collectives: 24.7 us -> 36.6 us
    ppermute x2, starting transfers between devices: 133 us -> 4.82 us  [shifted(): lax.ppermute(value, axis, [(i, (i + by) % devices) for i in range(devices)])]
    dot_general x20 -> x0, matrix products: 86.9 us -> none  [the longest x2 9.84 us: forward_pass(): contract(form, imag_in, cos_part) - contract(form, real_in, sin_part)]
    pallas_call x1, Pallas kernels: 167 us -> 107 us  [pair_call(): pl.pallas_call(functools.partial(pair_kernel, rp=rp, coef=coef, unroll=un...]
    all_to_all x3 -> x2, waiting for transfers between devices: 58.4 us -> 8.75 us  [swap(): return lax.all_to_all(value, axis, split_axis=0, concat_axis=0, tiled=True)]
    unnamed x36 -> x44, local copies, waits for them, and re-layouts: 59.1 us -> 10.5 us
    ppermute x2, waiting for transfers between devices: 54.4 us -> 15.8 us  [shifted(): lax.ppermute(value, axis, [(i, (i + by) % devices) for i in range(devices)])]
    all_to_all x4 -> x0, other arithmetic: 27.3 us -> none  [the longest x1 7.31 us: kspace_part(): lax.all_to_all(jnp.stack([xr_part, xi_part])[:, :, None], 'gy', split_axi...]
    pallas_call x0 -> x5, Pallas kernels: none -> 22 us  [run(): pl.pallas_call(functools.partial(kernel, **sizes), out_shape=jax.ShapeDty...]
  transfers between devices with their start and end apart: 8 -> 7, of which waited for: 5 -> 4; matrix products, arithmetic and copies ran while one was open for 4% -> 1% of each run, Pallas kernels for 20% -> 31%
where the time goes in v3:
time: 456 us; the launch traced here: 455 us
  Pallas kernels  296 us (65%)
  waiting for transfers between devices  73.1 us (16%)
  blocking collectives  36.6 us (8%)
  starting transfers between devices  29.7 us (7%)
  local copies, waits for them, and re-layouts  13.8 us (3%)
    pallas_call x1, Pallas kernels, pair_call(): pl.pallas_call(functools.partial(pair_kernel, rp=rp, coef=coef, unroll=un...  107 us
    pallas_call x1, Pallas kernels, gather_call(): pl.pallas_call(functools.partial(gather_kernel, depth=depth, rp=rp), out_...  70.2 us
    pallas_call x1, Pallas kernels, scatter_call(): pl.pallas_call(functools.partial(scatter_kernel, depth=depth, rp=rp), out...  67.7 us
    all_to_all x2, blocking collectives, swap(): return lax.all_to_all(value, axis, split_axis=0, concat_axis=0, tiled=True)  36.6 us
    all_to_all x1, waiting for transfers between devices, shards(): data = swap(pack_call(starts, places, depth))  29.8 us
    pallas_call x5, Pallas kernels, run(): pl.pallas_call(functools.partial(kernel, **sizes), out_shape=jax.ShapeDty...  22 us
    all_to_all x1, waiting for transfers between devices, shards(): swap(gather_call(nodes, counts, near_vel.reshape(3 * rp, 128), wave_vel,...  18.8 us
    ppermute x2, waiting for transfers between devices, shifted(): lax.ppermute(value, axis, [(i, (i + by) % devices) for i in range(devices)])  15.8 us
  transfers between devices with their start and end apart: 7, of which 4 were waited for; matrix products, arithmetic and copies ran while one was open for 1% of the time, Pallas kernels for 31%

profile of v3, /device:TPU:0, one launch (start us, length us, event | category | flops | bytes accessed | tf_op | source)
XLA Modules:
  0.0 454.7 jit_solution(11444103651201298539)
XLA Ops:
  0.7 2.3 convert_reduce_fusion.starts
  2.9 4.0 slots.1
  6.9 7.3 %all-to-all-start = ((s32[32,16,128]{2,1,0:T(8,128)}), s32[32,16,128]{2,1,0:T(8,128)S(1)}, u32[]{:S(2)}, u32[]{:S(2)}) async-start(s32[32,16,128]{2,1,0:T(8,128)} %slots.1), calls=%async_computation | async-start | bytes 524288 | tf_op jit(solution)/shard_map/all_to_all | solution.py:781
  14.3 1.8 copy.26
  16.1 14.7 %pack.1 = f32[32,96,128]{2,1,0:T(8,128)} custom-call(s32[33]{0:T(128)} %convert_reduce_fusion.starts, f32[3,256,128]{2,1,0:T(8,128)} %bitcast.43), custom_call_target="tpu_custom_call" | custom-call | tf_op jit(solution)/shard_map/pack/pallas_call | solution.py:125
  30.8 5.9 %all-to-all-start.1 = ((f32[32,96,128]{2,1,0:T(8,128)}), f32[32,96,128]{2,1,0:T(8,128)}, u32[]{:S(2)}, u32[]{:S(2)}) async-start(f32[32,96,128]{2,1,0:T(8,128)} %pack.1), calls=%async_computation.1 | async-start | bytes 3145728 | tf_op jit(solution)/shard_map/all_to_all | solution.py:783
  37.5 5.3 %nodes.1 = s32[32,16,128]{2,1,0:T(8,128)} custom-call(s32[32,16,128]{2,1,0:T(8,128)} %copy-done.20, s32[32,16,128]{2,1,0:T(8,128)} %bitcast.46), custom_call_target="tpu_custom_call" | custom-call | tf_op jit(solution)/shard_map/nodes/pallas_call | solution.py:152
  42.7 1.6 convert_reduce_fusion.1.counts
  44.4 29.8 %all-to-all-done.1.in_ref = f32[32,96,128]{2,1,0:T(8,128)} async-done(((f32[32,96,128]{2,1,0:T(8,128)}), f32[32,96,128]{2,1,0:T(8,128)}, u32[]{:S(2)}, u32[]{:S(2)}) %all-to-all-start.1) | async-done | bytes 1572896 | tf_op jit(solution)/shard_map/all_to_all | solution.py:783
  74.1 0.9 copy-done.6
  75.1 67.7 %scatter.1.field_ref = f32[3072,128]{1,0:T(8,128)S(1)} custom-call(s32[65536]{0:T(1024)S(1)} %bitcast.38, s32[32]{0:T(128)S(1)} %convert_reduce_fusion.1.counts, f32[32,96,128]{2,1,0:T(8,128)} %all-to-all-done.1.in_ref), custom_call_target="tpu_custom_call" | custom-call | tf_op jit(solution)/shard_map/scatter/pallas_call | solution.py:196
  142.8 3.3 depth.1
  146.2 22.5 %all_to_all.35 = f32[8,16,1536]{2,1,0:T(8,128)S(1)} all-to-all(f32[8,16,1536]{2,1,0:T(8,128)S(1)} %depth.1), channel_id=1, replica_groups=mesh['gx'=8,'gy'=4] {'gx'}, dimensions={0} | all-to-all | bytes 1572864 | tf_op jit(solution)/shard_map/all_to_all | solution.py:743
  168.7 5.7 %first.1 = f32[4,12,32,128]{3,2,1,0:T(8,128)S(1)} custom-call(f32[128,1536]{1,0:T(8,128)S(1)} %bitcast.37, f32[128,256]{1,0:T(8,128)S(1)} %copy-done.10), custom_call_target="tpu_custom_call" | custom-call | tf_op jit(solution)/shard_map/first/pallas_call | solution.py:731
  175.3 3.8 all-to-all-start.3
  179.1 2.8 collective-permute-start
  182.0 8.7 %all-to-all-done.3 = f32[4,384,128]{2,1,0:T(8,128)S(1)} async-done(((f32[4,384,128]{2,1,0:T(8,128)}), f32[4,384,128]{2,1,0:T(8,128)S(1)}, u32[]{:S(2)}, u32[]{:S(2)}) %all-to-all-start.3) | async-done | bytes 786464 | tf_op jit(solution)/shard_map/all_to_all | solution.py:743
  190.7 4.8 %second.1 = f32[4,12,32,128]{3,2,1,0:T(8,128)S(1)} custom-call(s32[2]{0:T(128)S(1)} %pad_add_fusion.ids, f32[4,12,32,128]{3,2,1,0:T(8,128)S(1)} %bitcast.32, f32[256,128]{1,0:T(8,128)S(1)} %copy-done.11, f32[4,8,128]{2,1,0:T(8,128)S(1)} %copy-done.16, f32[8,8,128]{2,1,0:T(8,128)S(1)} %copy-done.15, f32[2,128,128]{2,1,0:T(8,128)S(1)} %copy-done.12), custom_call_target="tpu_custom_call" | custom-call | tf_op jit(solution)/shard_map/second/pallas_call | solution.py:731
  195.6 14.0 %all_to_all.36 = f32[4,384,128]{2,1,0:T(8,128)S(1)} all-to-all(f32[4,384,128]{2,1,0:T(8,128)S(1)} %bitcast.33), channel_id=1, replica_groups=mesh['gx'=8,'gy'=4] {'gy'}, dimensions={0} | all-to-all | bytes 1572864 | tf_op jit(solution)/shard_map/all_to_all | solution.py:743
  209.6 5.0 %first_back.1 = f32[128,1536]{1,0:T(8,128)S(1)} custom-call(f32[4,12,32,128]{3,2,1,0:T(8,128)S(1)} %bitcast.36, f32[128,256]{1,0:T(8,128)S(1)} %copy-done.10), custom_call_target="tpu_custom_call" | custom-call | tf_op jit(solution)/shard_map/first_back/pallas_call | solution.py:731
  215.5 4.1 all-to-all-start.5
  220.3 1.4 copy-done.2
  221.7 107.0 %pairs.1 = (f32[3,512,128]{2,1,0:T(8,128)S(1)}, f32[3,512,128]{2,1,0:T(8,128)}) custom-call(s32[1024]{0:T(1024)S(1)} %bitcast.41, s32[1024]{0:T(1024)S(1)} %bitcast.42, s32[1]{0:T(128)S(6)} %copy.27.count, f32[6,512,128]{2,1,0:T(8,128)S(1)} %bitcast.31, f32[6,512,128]{2,1,0:T(8,128)} %bitcast.6.far_ref), custom_call_target="tpu_custom_call" | custom-call | tf_op jit(solution)/shard_map/pairs/pallas_call | solution.py:402
  329.6 2.0 collective-permute-start.1
  331.6 3.3 depth_back.1.two_ref
  335.8 15.8 %collective-permute-done.1.three_ref = f32[1536,128]{1,0:T(8,128)} collective-permute-done((f32[1536,128]{1,0:T(8,128)}, f32[1536,128]{1,0:T(8,128)}, u32[]{:S(2)}, u32[]{:S(2)}) %collective-permute-start.1) | collective-permute-done | bytes 786464 | tf_op jit(solution)/shard_map/ppermute | solution.py:30
  351.6 70.2 %gather.1 = f32[32,48,128]{2,1,0:T(8,128)} custom-call(s32[65536]{0:T(1024)S(1)} %bitcast.39, s32[32]{0:T(128)S(1)} %convert_reduce_fusion.1.counts, f32[1536,128]{1,0:T(8,128)S(1)} %bitcast.40, f32[1536,128]{1,0:T(8,128)} %copy-done.5, f32[1536,128]{1,0:T(8,128)} %collective-permute-done.1.three_ref), custom_call_target="tpu_custom_call" | custom-call | tf_op jit(solution)/shard_map/gather/pallas_call | solution.py:237
  421.8 3.7 all-to-all-start.6
  425.6 1.8 copy.25
  427.4 18.8 %all-to-all-done.6.in_ref = f32[32,48,128]{2,1,0:T(8,128)S(1)} async-done(((f32[32,48,128]{2,1,0:T(8,128)}), f32[32,48,128]{2,1,0:T(8,128)S(1)}, u32[]{:S(2)}, u32[]{:S(2)}) %all-to-all-start.6) | async-done | bytes 786464 | tf_op jit(solution)/shard_map/all_to_all | solution.py:803
  447.0 5.0 %finish.1 = (f32[3,256,128]{2,1,0:T(8,128)}, f32[3,256,128]{2,1,0:T(8,128)}) custom-call(s32[33]{0:T(128)} %convert_reduce_fusion.starts, f32[32,48,128]{2,1,0:T(8,128)} %copy-done.19, f32[3,256,128]{2,1,0:T(8,128)} %bitcast.44, f32[3,256,128]{2,1,0:T(8,128)} %bitcast.45), custom_call_target="tpu_custom_call" | custom-call | tf_op jit(solution)/shard_map/finish/pallas_call | solution.py:285
  452.1 2.6 copy_bitcast_fusion
  (46 shorter events, 5.3 us)
Async XLA Ops:
  0.6 36.1 %copy-start = (s32[8,1,65536]{2,1,0:T(1,128)S(1)}, s32[8,1,65536]{2,1,0:T(1,128)}, u32[]{:S(2)}) copy-start(s32[8,1,65536]{2,1,0:T(1,128)} %param.18) | copy-start | bytes 6291460
  6.9 23.8 %all-to-all-start = ((s32[32,16,128]{2,1,0:T(8,128)}), s32[32,16,128]{2,1,0:T(8,128)S(1)}, u32[]{:S(2)}, u32[]{:S(2)}) async-start(s32[32,16,128]{2,1,0:T(8,128)} %slots.1), calls=%async_computation | async-start | bytes 524288 | tf_op jit(solution)/shard_map/all_to_all | solution.py:781
  30.8 6.7 %copy-start.20 = (s32[32,16,128]{2,1,0:T(8,128)}, s32[32,16,128]{2,1,0:T(8,128)S(1)}, u32[]{:S(2)}) copy-start(s32[32,16,128]{2,1,0:T(8,128)S(1)} %all-to-all-done.slots_ref) | copy-start | bytes 786436
  30.8 43.4 %all-to-all-start.1 = ((f32[32,96,128]{2,1,0:T(8,128)}), f32[32,96,128]{2,1,0:T(8,128)}, u32[]{:S(2)}, u32[]{:S(2)}) async-start(f32[32,96,128]{2,1,0:T(8,128)} %pack.1), calls=%async_computation.1 | async-start | bytes 3145728 | tf_op jit(solution)/shard_map/all_to_all | solution.py:783
  37.4 105.4 %copy-start.14 = (f32[128,128]{1,0:T(8,128)S(1)}, f32[128,128]{1,0:T(8,128)}, u32[]{:S(2)}) copy-start(f32[128,128]{1,0:T(8,128)} %constant.33.clone.table_ref) | copy-start | bytes 196612
  74.1 1.0 copy-start.6
  142.8 31.6 %copy-start.1 = (f32[3072,128]{1,0:T(8,128)}, f32[3072,128]{1,0:T(8,128)S(1)}, u32[]{:S(2)}) copy-start(f32[3072,128]{1,0:T(8,128)S(1)} %scatter.1.field_ref) | copy-start | bytes 4718596
  142.8 25.9 %copy-start.10 = (f32[128,256]{1,0:T(8,128)S(1)}, f32[128,256]{1,0:T(8,128)}, u32[]{:S(2)}) copy-start(f32[128,256]{1,0:T(8,128)} %constant.34.clone.table_ref) | copy-start | bytes 393220
  146.1 44.6 %copy-start.11 = (f32[256,128]{1,0:T(8,128)S(1)}, f32[256,128]{1,0:T(8,128)}, u32[]{:S(2)}) copy-start(f32[256,128]{1,0:T(8,128)} %constant.35.clone.table_ref) | copy-start | bytes 393220
  146.1 44.6 %copy-start.12 = (f32[2,128,128]{2,1,0:T(8,128)S(1)}, f32[2,128,128]{2,1,0:T(8,128)}, u32[]{:S(2)}) copy-start(f32[2,128,128]{2,1,0:T(8,128)} %constant.38.clone.down_ref) | copy-start | bytes 393220
  146.1 44.6 %copy-start.15 = (f32[8,8,128]{2,1,0:T(8,128)S(1)}, f32[8,8,128]{2,1,0:T(8,128)}, u32[]{:S(2)}) copy-start(f32[8,8,128]{2,1,0:T(8,128)} %constant.37.clone.deep_ref) | copy-start | bytes 98308
  146.2 44.6 %copy-start.16 = (f32[4,8,128]{2,1,0:T(8,128)S(1)}, f32[4,8,128]{2,1,0:T(8,128)}, u32[]{:S(2)}) copy-start(f32[4,8,128]{2,1,0:T(8,128)} %constant.36.clone.across_ref) | copy-start | bytes 49156
  174.4 0.9 copy-start.4
  175.3 15.4 %all-to-all-start.3 = ((f32[4,384,128]{2,1,0:T(8,128)}), f32[4,384,128]{2,1,0:T(8,128)S(1)}, u32[]{:S(2)}, u32[]{:S(2)}) async-start(f32[4,384,128]{2,1,0:T(8,128)} %bitcast.35), calls=%async_computation.3 | async-start | bytes 1572864 | tf_op jit(solution)/shard_map/all_to_all | solution.py:743
  179.1 41.2 %collective-permute-start = (f32[3072,128]{1,0:T(8,128)}, f32[3072,128]{1,0:T(8,128)}, u32[]{:S(2)}, u32[]{:S(2)}) collective-permute-start(f32[3072,128]{1,0:T(8,128)} %copy-done.1), channel_id=1, source_target_pairs={{0,28},{4,0},{8,4},{12,8},{16,12},{20,16},{24,20},{28,24},{1,29},{... | collective-permute-start | bytes 4718600 | tf_op jit(solution)/shard_map/ppermute | solution.py:30
  195.5 24.7 %copy-start.17 = (s32[1,1024]{1,0:T(1,128)S(1)}, s32[1,1024]{1,0:T(1,128)}, u32[]{:S(2)}) copy-start(s32[1,1024]{1,0:T(1,128)} %param.19) | copy-start | bytes 12292
  195.5 24.7 %copy-start.18 = (s32[1,1024]{1,0:T(1,128)S(1)}, s32[1,1024]{1,0:T(1,128)}, u32[]{:S(2)}) copy-start(s32[1,1024]{1,0:T(1,128)} %param.20) | copy-start | bytes 12292
  214.6 0.9 copy-start.3
  215.5 116.1 %copy-start.13 = (f32[128,128]{1,0:T(8,128)S(1)}, f32[128,128]{1,0:T(8,128)}, u32[]{:S(2)}) copy-start(f32[128,128]{1,0:T(8,128)} %constant.39.clone.table_ref) | copy-start | bytes 196612
  215.5 116.1 %all-to-all-start.5 = ((f32[8,16,1536]{2,1,0:T(8,128)}), f32[8,16,1536]{2,1,0:T(8,128)S(1)}, u32[]{:S(2)}, u32[]{:S(2)}) async-start(f32[8,16,1536]{2,1,0:T(8,128)} %bitcast.34), calls=%async_computation.5 | async-start | bytes 1572864 | tf_op jit(solution)/shard_map/all_to_all | solution.py:743
  220.3 1.4 copy-start.2
  221.7 129.9 %copy-start.7 = (s32[32,16,128]{2,1,0:T(8,128)S(1)}, s32[32,16,128]{2,1,0:T(8,128)}, u32[]{:S(2)}) copy-start(s32[32,16,128]{2,1,0:T(8,128)} %nodes.1) | copy-start | bytes 786436
  328.7 0.9 copy-start.8
  329.6 22.1 %collective-permute-start.1 = (f32[1536,128]{1,0:T(8,128)}, f32[1536,128]{1,0:T(8,128)}, u32[]{:S(2)}, u32[]{:S(2)}) collective-permute-start(f32[1536,128]{1,0:T(8,128)} %bitcast.16), channel_id=1, source_target_pairs={{0,4},{4,8},{8,12},{12,16},{16,20},{20,24},{24,28},{28,0},{1,5},{5... | collective-permute-start | bytes 2359304 | tf_op jit(solution)/shard_map/ppermute | solution.py:30
  331.6 20.0 %copy-start.9 = (f32[3,512,128]{2,1,0:T(8,128)S(1)}, f32[3,512,128]{2,1,0:T(8,128)}, u32[]{:S(2)}) copy-start(f32[3,512,128]{2,1,0:T(8,128)} %copy-done.8) | copy-start | bytes 2359300
  334.9 0.9 copy-start.5
  421.8 24.3 %all-to-all-start.6 = ((f32[32,48,128]{2,1,0:T(8,128)}), f32[32,48,128]{2,1,0:T(8,128)S(1)}, u32[]{:S(2)}, u32[]{:S(2)}) async-start(f32[32,48,128]{2,1,0:T(8,128)} %gather.1), calls=%async_computation.6 | async-start | bytes 1572864 | tf_op jit(solution)/shard_map/all_to_all | solution.py:803
  446.1 0.9 copy-start.19

commit v4 on v3

--- a/solution.py
+++ b/solution.py
@@ -30,10 +30,20 @@
     return lax.ppermute(value, axis, [(i, (i + by) % devices) for i in range(devices)])
 
 
-UNROLL = 16
+SPAN = 16
 
 SMEM_SPEC = pl.BlockSpec(memory_space=pltpu.SMEM)
 VMEM_SPEC = pl.BlockSpec(memory_space=pltpu.VMEM)
+
+
+ANY_SPEC = pl.BlockSpec(memory_space=pl.ANY)
+
+
+def ignoring(kernel, inputs, extra):
+    def run(*refs):
+        kernel(*refs[:inputs], *refs[inputs + extra :])
+
+    return run
 
 
 def lane_index(rows):
@@ -98,7 +108,7 @@
 
 
 def pack_kernel(starts, pos_ref, out_ref, table, *, rows, depth, stride):
-    step = 8
+    step = 32 if rows % 32 == 0 else 8
 
     @pl.loop(0, rows // step)
     def _(i):
@@ -132,118 +142,193 @@
     )(starts, pos)
 
 
-def nodes_kernel(slots_ref, perm_ref, out_ref, *, depth, spare):
-    tile = 8 if depth % 8 == 0 else 1
+def list_count(depth):
+    return 8 if depth % 8 == 0 else 1
+
+
+def nodes_kernel(slots_ref, perm_ref, node_ref, *list_refs, depth, spare):
+    tile = list_count(depth)
+    parts = depth // tile
 
     @pl.loop(0, slots_ref.shape[0])
     def _(t):
         rows = [jnp.broadcast_to(perm_ref[t, w : w + 1, :], (8, 128)) for w in range(depth)]
-        for r in range(depth // tile):
+        for r in range(parts):
             slot = jnp.broadcast_to(slots_ref[t, r * tile : (r + 1) * tile, :], (8, 128))
             place = slot & 127
             which = slot >> 7
             node = jnp.full((8, 128), spare, jnp.int32)
             for w in range(depth):
                 node = jnp.where(which == w, jnp.take_along_axis(rows[w], place, axis=1), node)
-            out_ref[t, r * tile : (r + 1) * tile, :] = node[:tile]
+            packed = ((node >> 12) << 7) | (node & 127)
+            node_ref[t, r * tile : (r + 1) * tile, :] = node[:tile]
+            for u in range(tile):
+                list_refs[u][pl.ds(t * parts + r, 1), :] = node[u : u + 1]
+                list_refs[tile + u][pl.ds(t * parts + r, 1), :] = packed[u : u + 1]
 
 
 def nodes_call(slots, perm, spare):
-    return pl.pallas_call(
-        functools.partial(nodes_kernel, depth=slots.shape[1], spare=spare),
-        out_shape=jax.ShapeDtypeStruct(slots.shape, jnp.int32),
+    peers, depth, _ = slots.shape
+    lists = list_count(depth)
+    one = jax.ShapeDtypeStruct((peers * depth // lists, 128), jnp.int32)
+    found = pl.pallas_call(
+        functools.partial(nodes_kernel, depth=depth, spare=spare),
+        out_shape=(jax.ShapeDtypeStruct(slots.shape, jnp.int32),) + (one,) * (2 * lists),
         in_specs=[VMEM_SPEC] * 2,
-        out_specs=VMEM_SPEC,
+        out_specs=(VMEM_SPEC,) * (1 + 2 * lists),
         name="nodes",
     )(slots, perm)
-
-
-def scatter_kernel(nodes, counts, in_ref, out_ref, table, rows_ref, *, depth, rp):
-    t = pl.program_id(0)
-
-    @pl.when(t == 0)
-    def _():
-        @pl.loop(0, rp)
-        def _(k):
-            table[pl.ds(pl.multiple_of(k * 128, 128), 128), :] = jnp.zeros((128, 128), jnp.float32)
-
-    for r in range(depth):
-        piece = in_ref[0, pl.ds(r, 6, stride=depth), :]
-        piece = jnp.concatenate([piece, jnp.zeros((2, 128), jnp.float32)], axis=0)
-        rows_ref[r * 128 : (r + 1) * 128, 0:8] = jnp.transpose(piece)
-
-    base = t * (depth * 128)
-
-    def some(i, carry):
-        at = pl.multiple_of(i * UNROLL, UNROLL)
-        for u in range(UNROLL):
-            table[pl.ds(nodes[base + at + u], 1), :] = rows_ref[pl.ds(at + u, 1), :]
-        return carry
-
-    lax.fori_loop(0, lax.div(counts[t] + (UNROLL - 1), jnp.int32(UNROLL)), some, 0)
-
-    @pl.when(t == pl.num_programs(0) - 1)
-    def _():
-        @pl.loop(0, rp, unroll=4)
-        def _(k):
-            turned = jnp.transpose(table[pl.ds(pl.multiple_of(k * 128, 128), 128), 0:8])
-            out_ref[pl.ds(k, 6, stride=rp), :] = turned[:6]
-
-
-def scatter_call(nodes, counts, data, rp):
-    peers, height, _ = data.shape
-    depth = height // 6
+    flat = [x.reshape(-1) for x in found[1:]]
+    return found[0], flat[:lists], flat[lists:]
+
+
+def move_rows(lists, count, t, depth, move):
+    width = len(lists)
+    parts = depth // width
+
+    def part(p, carry):
+        live = jnp.minimum(count - p * (width * 128), 128)
+        base = (t * parts + p) * 128
+        start = p * (width * 128)
+
+        def some(i, carry):
+            for k in range(SPAN):
+                at = i * SPAN + k
+                for u in range(width):
+                    move(start + at + u * 128, lists[u][base + at])
+            return carry
+
+        return lax.fori_loop(0, lax.div(live + (SPAN - 1), jnp.int32(SPAN)), some, carry)
+
+    whole = width * 128
+    lax.fori_loop(0, lax.div(count + (whole - 1), jnp.int32(whole)), part, 0)
+
+
+def scatter_kernel(counts, in_ref, *refs, depth, rp, lists):
+    nodes = refs[:lists]
+    out_ref, cells_ref, table, rows_ref = refs[lists:]
+
+    @pl.loop(0, rp)
+    def _(k):
+        table[pl.ds(pl.multiple_of(k * 128, 128), 128), :] = jnp.zeros((128, 128), jnp.float32)
+
+    together = 4 if depth % 4 == 0 else 1
+
+    @pl.loop(0, in_ref.shape[0])
+    def _(t):
+        def turn(i, carry):
+            for j in range(together):
+                r = i * together + j
+                piece = in_ref[t, pl.ds(r, 6, stride=depth), :]
+                piece = jnp.concatenate([piece, jnp.zeros((2, 128), jnp.float32)], axis=0)
+                piece = jnp.concatenate([piece] * 16, axis=0)
+                rows_ref[pl.ds(pl.multiple_of(r * 128, 128), 128), :] = jnp.transpose(piece)
+            return carry
+
+        def move(at, node):
+            table[pl.ds(node, 1), :] = rows_ref[pl.ds(at, 1), :]
+
+        count = counts[t]
+        part = together * 128
+        lax.fori_loop(0, lax.div(count + (part - 1), jnp.int32(part)), turn, 0)
+        move_rows(nodes, count, t, depth, move)
+
+    group = lane_index(8) >> 3
+
+    @pl.loop(0, rp // 16)
+    def _(g):
+        tiles = []
+        for i in range(16):
+            tile = table[pl.ds(pl.multiple_of(g * 2048, 2048) + 8 * i, 8), :]
+            for k in range(1, 16):
+                one = table[pl.ds(pl.multiple_of(g * 2048, 2048) + k * 128 + 8 * i, 8), :]
+                tile = jnp.where(group == k, one, tile)
+            tiles.append(tile)
+        at = pl.multiple_of(g * 128, 128)
+        cells_ref[pl.ds(at, 128), :] = jnp.transpose(jnp.concatenate(tiles, axis=0))
+        for c in range(6):
+            out_ref[pl.ds(pl.multiple_of(c * rp + g * 16, 16), 16), :] = cells_ref[pl.ds(at + c, 16, stride=8), :]
+
+
+def scatter_call(nodes, counts, data, rp, after=()):
+    depth = data.shape[1] // 6
     return pl.pallas_call(
-        functools.partial(scatter_kernel, depth=depth, rp=rp),
-        out_shape=jax.ShapeDtypeStruct((6 * rp, 128), jnp.float32),
-        grid=(peers,),
-        in_specs=[SMEM_SPEC, SMEM_SPEC, pl.BlockSpec((1, height, 128), lambda t: (t, 0, 0))],
-        out_specs=VMEM_SPEC,
-        scratch_shapes=[pltpu.VMEM((rp * 128 + 8, 128), jnp.float32), pltpu.VMEM((depth * 128, 128), jnp.float32)],
+        ignoring(
+            functools.partial(scatter_kernel, depth=depth, rp=rp, lists=len(nodes)), 2 + len(nodes), len(after)
+        ),
+        out_shape=(
+            jax.ShapeDtypeStruct((6 * rp, 128), jnp.float32),
+            jax.ShapeDtypeStruct((8 * rp, 128), jnp.float32),
+        ),
+        in_specs=[SMEM_SPEC, VMEM_SPEC] + [SMEM_SPEC] * len(nodes) + [ANY_SPEC] * len(after),
+        out_specs=(VMEM_SPEC,) * 2,
+        scratch_shapes=[
+            pltpu.VMEM((rp * 128 + 8, 128), jnp.float32),
+            pltpu.VMEM((depth * 128, 128), jnp.float32),
+        ],
         compiler_params=pltpu.CompilerParams(vmem_limit_bytes=52 * 1024 * 1024),
         name="scatter",
-    )(nodes, counts, data)
-
-
-def gather_kernel(nodes, counts, one_ref, two_ref, three_ref, out_ref, table, rows_ref, *, depth, rp):
-    t = pl.program_id(0)
-
-    @pl.when(t == 0)
-    def _():
-        @pl.loop(0, rp, unroll=4)
-        def _(k):
-            at = pl.ds(k, 3, stride=rp)
-            value = one_ref[at, :] + two_ref[at, :] + three_ref[at, :]
-            value = jnp.concatenate([value, jnp.zeros((5, 128), jnp.float32)], axis=0)
-            table[pl.ds(pl.multiple_of(k * 128, 128), 128), 0:8] = jnp.transpose(value)
-
-    base = t * (depth * 128)
-
-    def some(i, carry):
-        at = pl.multiple_of(i * UNROLL, UNROLL)
-        for u in range(UNROLL):
-            rows_ref[pl.ds(at + u, 1), :] = table[pl.ds(nodes[base + at + u], 1), :]
-        return carry
-
-    lax.fori_loop(0, lax.div(counts[t] + (UNROLL - 1), jnp.int32(UNROLL)), some, 0)
-    for r in range(depth):
-        turned = jnp.transpose(rows_ref[r * 128 : (r + 1) * 128, 0:8])
-        out_ref[0, pl.ds(r, 3, stride=depth), :] = turned[:3]
-
-
-def gather_call(nodes, counts, one, two, three, depth):
+    )(counts, data, *nodes, *after)
+
+
+def gather_kernel(counts, node_ref, sums_ref, one_ref, two_ref, *refs, depth, rp, lists):
+    rows = refs[:lists]
+    out_ref, table, found, comb = refs[lists:]
+    comb[...] = jnp.zeros((128, 128), jnp.float32)
+
+    @pl.loop(0, rp // 32)
+    def _(g):
+        for c in range(3):
+            at = pl.ds(pl.multiple_of(c * rp + g * 32, 32), 32)
+            comb[pl.ds(c, 32, stride=4), :] = one_ref[at, :] + two_ref[at, :]
+        for i in range(16):
+            pair = [sums_ref[pl.ds(pl.multiple_of((g * 32 + 2 * i + h) * 8, 8), 8), :] for h in range(2)]
+            both = pair[0] + pltpu.roll(pair[1], 4, 0)
+            comb[8 * i : 8 * i + 8, :] = comb[8 * i : 8 * i + 8, :] + both
+        table[pl.ds(pl.multiple_of(g * 128, 128), 128), :] = jnp.transpose(comb[...])
+
+    together = 4 if depth % 4 == 0 else 1
+
+    @pl.loop(0, out_ref.shape[0])
+    def _(t):
+        def move(at, row):
+            found[pl.ds(at, 1), :] = table[pl.ds(row, 1), :]
+
+        def turn(i, carry):
+            for j in range(together):
+                r = i * together + j
+                turned = jnp.transpose(found[pl.ds(pl.multiple_of(r * 128, 128), 128), :])
+                place = jnp.broadcast_to(node_ref[t, pl.ds(r, 1), :], (8, 128)) >> 7
+                half = (place >> 1) & 15
+                value = turned[:8]
+                for h in range(1, 16):
+                    value = jnp.where(half == h, turned[8 * h : 8 * h + 8], value)
+                value = jnp.where((place & 1) == 1, pltpu.roll(value, 4, 0), value)
+                out_ref[t, pl.ds(r, 3, stride=depth), :] = value[:3]
+            return carry
+
+        count = counts[t]
+        part = together * 128
+        move_rows(rows, count, t, depth, move)
+        lax.fori_loop(0, lax.div(count + (part - 1), jnp.int32(part)), turn, 0)
+
+
+def gather_call(rows, counts, nodes, sums, one, two):
     rp = one.shape[0] // 3
-    peers = counts.shape[0]
+    peers, depth, _ = nodes.shape
     return pl.pallas_call(
-        functools.partial(gather_kernel, depth=depth, rp=rp),
+        functools.partial(gather_kernel, depth=depth, rp=rp, lists=len(rows)),
         out_shape=jax.ShapeDtypeStruct((peers, 3 * depth, 128), jnp.float32),
-        grid=(peers,),
-        in_specs=[SMEM_SPEC, SMEM_SPEC] + [VMEM_SPEC] * 3,
-        out_specs=pl.BlockSpec((1, 3 * depth, 128), lambda t: (t, 0, 0)),
-        scratch_shapes=[pltpu.VMEM((rp * 128 + 8, 128), jnp.float32), pltpu.VMEM((depth * 128, 128), jnp.float32)],
-        compiler_params=pltpu.CompilerParams(vmem_limit_bytes=52 * 1024 * 1024),
+        in_specs=[SMEM_SPEC] + [VMEM_SPEC] * 4 + [SMEM_SPEC] * len(rows),
+        out_specs=VMEM_SPEC,
+        scratch_shapes=[
+            pltpu.VMEM((rp * 4 + 8, 128), jnp.float32),
+            pltpu.VMEM((depth * 128, 128), jnp.float32),
+            pltpu.VMEM((128, 128), jnp.float32),
+        ],
+        compiler_params=pltpu.CompilerParams(vmem_limit_bytes=32 * 1024 * 1024),
         name="gather",
-    )(nodes, counts, one, two, three)
+    )(counts, nodes, sums, one, two, *rows)
 
 
 def finish_kernel(starts, in_ref, pos_ref, noise_ref, moved_ref, drift_ref, table, *, rows, depth, stride):
@@ -316,22 +401,64 @@
     across = (decay * inverse_sq) * (screen * (0.375 - 0.1875 * inverse_sq) - 0.125)
     return along, across
 
-def pair_kernel(first, second, count, own_ref, far_ref, vown_ref, vfar_ref, cells, sums, *, rp, coef, unroll):
+def order_kernel(first, second, count, own_ref, far_ref, totals, *, blocks):
+    def step(p, sizes):
+        own, far = sizes
+        other = second[p]
+        within = other < blocks
+        both = first[p] * 65536 + other
+        own_ref[own] = both
+        far_ref[far] = both - blocks
+        inside = within.astype(jnp.int32)
+        return own + inside, far + 1 - inside
+
+    own, far = lax.fori_loop(0, count[0], step, (jnp.int32(0), jnp.int32(0)))
+    totals[0] = own
+    totals[1] = far
+
+
+def order_call(first, second, count, blocks):
+    size = first.shape[0] + 8
+    return pl.pallas_call(
+        functools.partial(order_kernel, blocks=blocks),
+        out_shape=(jax.ShapeDtypeStruct((size,), jnp.int32),) * 2 + (jax.ShapeDtypeStruct((2,), jnp.int32),),
+        in_specs=[SMEM_SPEC] * 3,
+        out_specs=(SMEM_SPEC,) * 3,
+        name="order",
+    )(first, second, count)
+
+
+def fill_cells(src_ref, cells, rp):
+    @pl.loop(0, rp // 8)
+    def _(i):
+        at = pl.multiple_of(i * 8, 8)
+        for c in range(6):
+            cells[pl.ds(at * 8 + c, 8, stride=8), :] = src_ref[pl.ds(pl.multiple_of(c * rp + at, 8), 8), :]
+
+
+def pair_kernel(pairs, bounds, cells_ref, near_in, *refs, rp, coef, unroll, beyond):
+    if beyond:
+        other_ref, far_in, near_ref, far_ref, other_cells, far_sums = refs
+        fill_cells(other_ref, other_cells, rp)
+        for c in range(3):
+            @pl.loop(0, rp // 8)
+            def _(i):
+                at = pl.ds(pl.multiple_of(c * rp + i * 8, 8), 8)
+                far_sums[pl.ds(i * 64 + c, 8, stride=8), :] = far_in[at, :]
+    else:
+        (near_ref,) = refs
+        other_cells, far_sums = cells_ref, near_ref
     lane = lax.broadcasted_iota(jnp.int32, (8, 128), 1)
     sub = lax.broadcasted_iota(jnp.int32, (8, 128), 0)
     left = lane < 64
     unturn = (lane + sub) & 127
-
-    @pl.loop(0, rp // 8)
-    def _(i):
-        at = pl.ds(pl.multiple_of(i * 8, 8), 8)
-        for src, off in ((own_ref, 0), (far_ref, rp)):
-            for c in range(6):
-                cells[pl.ds((off + i * 8) * 8 + c, 8, stride=8), :] = src[c, at, :]
-            sums[pl.ds(pl.multiple_of((off + i * 8) * 8, 64), 64), :] = jnp.zeros((64, 128), jnp.float32)
-
-    def both_halves(k):
-        cell = cells[pl.ds(pl.multiple_of((k >> 1) * 8, 8), 8), :]
+    near_ref[...] = near_in[...]
+
+    def row(k):
+        return pl.ds(pl.multiple_of((k >> 1) * 8, 8), 8)
+
+    def both_halves(table, k):
+        cell = table[row(k), :]
         return jnp.where(left == ((k & 1) == 0), cell, pltpu.roll(cell, 64, 1))
 
     def stacked(parts):
@@ -340,12 +467,10 @@
             out = jnp.where(sub == c, jnp.sum(part, axis=0, keepdims=True), out)
         return out
 
-    def one(p):
-        ka = first[p]
-        kb = second[p]
-        near = both_halves(ka)
+    def one(ka, kb):
+        near = both_halves(cells_ref, ka)
         near = jnp.where(left, near, pltpu.roll(near, 96, 1))
-        far = both_halves(kb)
+        far = both_halves(other_cells, kb)
         mine = [jnp.broadcast_to(near[c : c + 1, :], (8, 128)) for c in range(6)]
         other = [jnp.broadcast_to(far[c : c + 1, :], (8, 128)) for c in range(6)]
         near_sum = None
@@ -370,44 +495,58 @@
         near_vel = near_vel + pltpu.roll(near_vel, 64, 1)
         far_vel = stacked(far_sum)
         far_vel = far_vel + pltpu.roll(far_vel, 64, 1)
-        return ka, near_vel, kb, far_vel
-
-    total = count[0]
+        return near_vel, far_vel
+
+    low = bounds[0]
+    high = bounds[1]
 
     def turn(i, carry):
         found = []
         for k in range(unroll):
-            p = i * unroll + k
-            found.append((p < total, one(p)))
-        for alive, (ka, near_vel, kb, far_vel) in found:
-            at = pl.ds(pl.multiple_of((ka >> 1) * 8, 8), 8)
-            sums[at, :] = sums[at, :] + jnp.where((left == ((ka & 1) == 0)) & alive, near_vel, 0.0)
-            at = pl.ds(pl.multiple_of((kb >> 1) * 8, 8), 8)
-            keep = (left == ((kb & 1) == 0)) & (alive & (ka != kb))
-            sums[at, :] = sums[at, :] + jnp.where(keep, far_vel, 0.0)
+            p = low + i * unroll + k
+            alive = p < high
+            both = jnp.where(alive, pairs[p], 0)
+            ka, kb = both >> 16, both & 65535
+            found.append((alive, ka, kb, one(ka, kb)))
+        for alive, ka, kb, (near_vel, far_vel) in found:
+            near_ref[row(ka), :] += jnp.where((left == ((ka & 1) == 0)) & alive, near_vel, 0.0)
+            if not beyond:
+                alive = alive & (ka != kb)
+            far_sums[row(kb), :] += jnp.where((left == ((kb & 1) == 0)) & alive, far_vel, 0.0)
         return carry
 
-    lax.fori_loop(0, lax.div(total + (unroll - 1), jnp.int32(unroll)), turn, 0)
-
-    @pl.loop(0, rp // 8)
-    def _(i):
-        at = pl.ds(pl.multiple_of(i * 8, 8), 8)
-        for dst, off in ((vown_ref, 0), (vfar_ref, rp)):
-            for c in range(3):
-                dst[c, at, :] = sums[pl.ds((off + i * 8) * 8 + c, 8, stride=8), :]
-
-def pair_call(first, second, count, own, far, coef=ERFCX_COEF, unroll=8):
-    rp = own.shape[1]
-    f32 = jnp.float32
+    lax.fori_loop(0, lax.div(jnp.maximum(high - low, 0) + (unroll - 1), jnp.int32(unroll)), turn, 0)
+
+    if beyond:
+        for c in range(3):
+            @pl.loop(0, rp // 8)
+            def _(i):
+                at = pl.ds(pl.multiple_of(c * rp + i * 8, 8), 8)
+                far_ref[at, :] = far_sums[pl.ds(i * 64 + c, 8, stride=8), :]
+
+
+def pair_call(pairs, bounds, cells, near, beside=None, far=None, after=(), coef=ERFCX_COEF, unroll=8):
+    rp = cells.shape[0] // 8
+    beyond = beside is not None
+    extra = [beside, far] if beyond else []
+    out = [jax.ShapeDtypeStruct((8 * rp, 128), jnp.float32)]
+    scratch = []
+    if beyond:
+        out.append(jax.ShapeDtypeStruct((3 * rp, 128), jnp.float32))
+        scratch = [pltpu.VMEM((8 * rp, 128), jnp.float32)] * 2
     return pl.pallas_call(
-        functools.partial(pair_kernel, rp=rp, coef=coef, unroll=unroll),
-        out_shape=(jax.ShapeDtypeStruct((3, rp, 128), f32),)*2,
-        in_specs=[pl.BlockSpec(memory_space=pltpu.SMEM)]*3 + [pl.BlockSpec(memory_space=pltpu.VMEM)]*2,
-        out_specs=(pl.BlockSpec(memory_space=pltpu.VMEM),)*2,
-        scratch_shapes=[pltpu.VMEM((2*rp*8, 128), f32), pltpu.VMEM((2*rp*8, 128), f32)],
-        compiler_params=pltpu.CompilerParams(vmem_limit_bytes=48*1024*1024),
-        name="pairs",
-    )(first, second, count, own, far)
+        ignoring(
+            functools.partial(pair_kernel, rp=rp, coef=coef, unroll=unroll, beyond=beyond),
+            4 + len(extra),
+            len(after),
+        ),
+        out_shape=tuple(out),
+        in_specs=[SMEM_SPEC] * 2 + [VMEM_SPEC] * (2 + len(extra)) + [ANY_SPEC] * len(after),
+        out_specs=(VMEM_SPEC,) * len(out),
+        scratch_shapes=scratch,
+        compiler_params=pltpu.CompilerParams(vmem_limit_bytes=32 * 1024 * 1024),
+        name="beyond" if beyond else "within",
+    )(pairs, bounds, cells, near, *extra, *after)
 
 
 def signed_wave(grid_index):
@@ -720,24 +859,24 @@
         out_ref[c * rows : (c + 1) * rows, :] = matmul(spec[c * rows : (c + 1) * rows, :], table_ref[...], PLAIN)
 
 
-def waves(grid_data, n_gx, n_gy):
+def waves(grid_data, n_gx, n_gy, fill):
     tall, wide, share = G // n_gx, G // n_gy, G // 2 // n_gx
     rows = 3 * tall * wide
     views = share * wide // 128
     tables = wave_tables(n_gx, n_gy)
     f32 = jnp.float32
 
-    def run(name, kernel, shape, args, scratch, specs=None, **sizes):
+    def run(name, kernel, shape, args, scratch, specs=None, after=(), **sizes):
         return pl.pallas_call(
-            functools.partial(kernel, **sizes),
+            ignoring(functools.partial(kernel, **sizes), len(args), len(after)),
             out_shape=jax.ShapeDtypeStruct(shape, f32),
-            in_specs=specs or [VMEM_SPEC] * len(args),
+            in_specs=(specs or [VMEM_SPEC] * len(args)) + [ANY_SPEC] * len(after),
             out_specs=VMEM_SPEC,
             scratch_shapes=[pltpu.VMEM(scratch, f32)],
             compiler_params=pltpu.CompilerParams(vmem_limit_bytes=24 * 1024 * 1024),
             name=name,
             grid=(1,),
-        )(*args)
+        )(*args, *after)
 
     def swap(value, axis):
         return lax.all_to_all(value, axis, split_axis=0, concat_axis=0, tiled=True)
@@ -750,19 +889,23 @@
     ids = jnp.stack([lax.axis_index("gx"), lax.axis_index("gy")]).astype(jnp.int32)
     value = run("depth", depth_kernel, (n_gx, tall, lanes), (grid_data, tables["ahead"]), (rows, 128),
                 [force, full((G, 128))], n_gx=n_gx, tall=tall, wide=wide)
+    after = fill(0, value)
     value = swap(value, "gx").reshape(G, lanes)
     value = run("first", first_kernel, (n_gy, 6 * views, wide, 128), (value, tables["first"]), (rows, 128),
-                n_gy=n_gy, share=share, wide=wide)
+                after=after, n_gy=n_gy, share=share, wide=wide)
+    after = fill(1, value)
     value = swap(value.reshape(n_gy, 6 * views * wide, 128), "gy").reshape(n_gy, 6 * views, wide, 128)
     args = (ids, value, tables["second"], tables["across"], tables["deep"], tables["down"])
     value = run("second", second_kernel, (n_gy, 6 * views, wide, 128), args, (8, 128),
-                [SMEM_SPEC] + [VMEM_SPEC] * 5, n_gy=n_gy, views=views, wide=wide)
+                [SMEM_SPEC] + [VMEM_SPEC] * 5, after, n_gy=n_gy, views=views, wide=wide)
+    after = fill(2, value)
     value = swap(value.reshape(n_gy, 6 * views * wide, 128), "gy").reshape(n_gy, 6 * views, wide, 128)
     value = run("first_back", first_back_kernel, (G, lanes), (value, tables["first_back"]), (rows, 128),
-                n_gy=n_gy, share=share, wide=wide)
+                after=after, n_gy=n_gy, share=share, wide=wide)
+    after = fill(3, value)
     value = swap(value.reshape(n_gx, tall, lanes), "gx")
     return run("depth_back", depth_back_kernel, (rows, 128), (value, tables["back"]), (rows, 128),
-               n_gx=n_gx, tall=tall, wide=wide)
+               after=after, n_gx=n_gx, tall=tall, wide=wide)
 
 
 def shards(positions, noise, route, node_perm, pair_first, pair_second, pair_count):
@@ -783,24 +926,46 @@
     data = swap(pack_call(starts, places, depth))
     counts = jnp.sum(taken >= 0, axis=(1, 2), dtype=jnp.int32)
     own_order = lax.dynamic_index_in_dim(node_perm, lax.axis_index("gx"), 0, False)
-    nodes = nodes_call(taken, own_order.reshape(peers, depth, 128), slots).reshape(slots)
-    grid_data = scatter_call(nodes, counts, data, rp)
-
-    beside_data = shifted(grid_data, "gx", -1)
-    near_vel, far_vel = pair_call(
-        pair_first[0],
-        pair_second[0],
-        pair_count,
-        grid_data.reshape(6, rp, 128),
-        beside_data.reshape(6, rp, 128),
-    )
+    nodes, node_lists, row_lists = nodes_call(taken, own_order.reshape(peers, depth, 128), slots)
+    own_pairs, far_pairs, totals = order_call(pair_first[0], pair_second[0], pair_count, slots // CELL)
+    grid_data, cells = scatter_call(node_lists, counts, data, rp, after=(totals,))
+
+    beside = shifted(grid_data, "gx", -1)
+    steps = pair_first.shape[1]
+    marks = [jnp.minimum(totals[0], steps // 4), jnp.minimum(totals[0], steps * 3 // 8)]
+    half = totals[1] // 16 * 8
+    begin = jnp.int32(0)
+    state = {"sums": jnp.zeros_like(cells), "far": jnp.zeros((3 * rp, 128), jnp.float32)}
+
+    def within(low, high, after):
+        (state["sums"],) = pair_call(own_pairs, jnp.stack([low, high]), cells, state["sums"], after=after)
+
+    def beyond(low, high, after):
+        state["sums"], state["far"] = pair_call(
+            far_pairs, jnp.stack([low, high]), cells, state["sums"], beside, state["far"], after=after
+        )
+
+    def fill(n, value):
+        if n == 0:
+            within(begin, marks[0], (value,))
+        elif n == 1:
+            within(marks[0], marks[1], (value,))
+        elif n == 2:
+            beyond(begin, half, (value,))
+        else:
+            beyond(half, totals[1], (value,))
+            state["far"] = shifted(state["far"], "gx", 1)
+            within(marks[1], totals[0], ())
+        return (state["sums"],)
+
     share = G // 2 // n_gx
     if share % 8 == 0 and share * (G // n_gy) % 128 == 0:
-        wave_vel = waves(grid_data, n_gx, n_gy)
+        wave_vel = waves(grid_data, n_gx, n_gy, fill)
     else:
         wave_vel = kspace_part(grid_data[3 * rp :], n_gx, n_gy).reshape(3 * rp, 128)
-    back_vel = shifted(far_vel.reshape(3 * rp, 128), "gx", 1)
-    back = swap(gather_call(nodes, counts, near_vel.reshape(3 * rp, 128), wave_vel, back_vel, depth))
+        for n in range(4):
+            fill(n, wave_vel)
+    back = swap(gather_call(row_lists, counts, nodes, state["sums"], wave_vel, state["far"]))
     moved, drift = finish_call(starts, back, places, noise.reshape(3, rows, 128))
     return (moved.reshape(positions.shape), drift.reshape(positions.shape))
 

time: 456 us -> 413 us (0.906)
  Pallas kernels: 296 us -> 206 us
  starting transfers between devices: 29.7 us -> 85.5 us
  blocking collectives: 36.6 us -> 0 us
  local copies, waits for them, and re-layouts: 13.8 us -> 38.9 us
  waiting for transfers between devices: 73.1 us -> 68 us
    pallas_call x9 -> x14, Pallas kernels: 272 us -> 189 us  [the longest x5 64.4 us: pair_call(): pl.pallas_call(ignoring(functools.partial(pair_kernel, rp=rp, coef=coef,...]
    all_to_all x2 -> x4, starting transfers between devices: 7.93 us -> 54.7 us  [swap(): return lax.all_to_all(value, axis, split_axis=0, concat_axis=0, tiled=True)]
    all_to_all x2 -> x0, blocking collectives: 36.6 us -> none  [swap(): return lax.all_to_all(value, axis, split_axis=0, concat_axis=0, tiled=True)]
    unnamed x44 -> x104, local copies, waits for them, and re-layouts: 10.5 us -> 34.8 us
    all_to_all x1, starting transfers between devices: 3.71 us -> 13.4 us  [shards(): swap(gather_call(row_lists, counts, nodes, state['sums'], wave_vel, state...]
    pallas_call x1, Pallas kernels: 14.7 us -> 7.76 us  [pack_call(): pl.pallas_call(functools.partial(pack_kernel, rows=rows, depth=depth, str...]
    all_to_all x1, waiting for transfers between devices: 29.8 us -> 23.1 us  [shards(): data = swap(pack_call(starts, places, depth))]
  transfers between devices with their start and end apart: 7 -> 9, of which waited for: 4 -> 5; matrix products, arithmetic and copies ran while one was open for 1% -> 2% of each run, Pallas kernels for 31% -> 24%
where the time goes in v4:
time: 413 us; the launch traced here: 410 us
  Pallas kernels  206 us (50%)
  starting transfers between devices  85.5 us (21%)
  waiting for transfers between devices  68 us (16%)
  local copies, waits for them, and re-layouts  38.9 us (9%)
  other arithmetic  5.65 us (1%)
  between operations  5.57 us (1%)
    pallas_call x5, Pallas kernels, pair_call(): pl.pallas_call(ignoring(functools.partial(pair_kernel, rp=rp, coef=coef,...  64.4 us
    all_to_all x4, starting transfers between devices, swap(): return lax.all_to_all(value, axis, split_axis=0, concat_axis=0, tiled=True)  54.7 us
    pallas_call x1, Pallas kernels, scatter_call(): pl.pallas_call(ignoring(functools.partial(scatter_kernel, depth=depth, rp...  48.2 us
    pallas_call x1, Pallas kernels, gather_call(): pl.pallas_call(functools.partial(gather_kernel, depth=depth, rp=rp, lists...  39.9 us
    unnamed x104, local copies, waits for them, and re-layouts  34.8 us
    pallas_call x5, Pallas kernels, run(): pl.pallas_call(ignoring(functools.partial(kernel, **sizes), len(args), le...  25.7 us
    all_to_all x1, waiting for transfers between devices, shards(): data = swap(pack_call(starts, places, depth))  23.1 us
    all_to_all x1, waiting for transfers between devices, shards(): swap(gather_call(row_lists, counts, nodes, state['sums'], wave_vel, state...  19.8 us
  transfers between devices with their start and end apart: 9, of which 5 were waited for; matrix products, arithmetic and copies ran while one was open for 2% of the time, Pallas kernels for 24%

profile of v4, /device:TPU:0, one launch (start us, length us, event | category | flops | bytes accessed | tf_op | source)
XLA Modules:
  0.0 409.7 jit_solution(3585973544250353874)
XLA Ops:
  0.7 2.3 convert_reduce_fusion.starts
  2.9 4.0 slots.1
  6.9 7.3 %all-to-all-start = ((s32[32,16,128]{2,1,0:T(8,128)}), s32[32,16,128]{2,1,0:T(8,128)S(1)}, u32[]{:S(2)}, u32[]{:S(2)}) async-start(s32[32,16,128]{2,1,0:T(8,128)} %slots.1), calls=%async_computation | async-start | bytes 524288 | tf_op jit(solution)/shard_map/all_to_all | solution.py:924
  14.3 1.8 copy.26
  16.1 7.8 %pack.1 = f32[32,96,128]{2,1,0:T(8,128)} custom-call(s32[33]{0:T(128)} %convert_reduce_fusion.starts, f32[3,256,128]{2,1,0:T(8,128)} %bitcast.63), custom_call_target="tpu_custom_call" | custom-call | tf_op jit(solution)/shard_map/pack/pallas_call | solution.py:135
  24.8 5.0 %all-to-all-start.1 = ((f32[32,96,128]{2,1,0:T(8,128)}), f32[32,96,128]{2,1,0:T(8,128)}, u32[]{:S(2)}, u32[]{:S(2)}) async-start(f32[32,96,128]{2,1,0:T(8,128)} %pack.1), calls=%async_computation.1 | async-start | bytes 3145728 | tf_op jit(solution)/shard_map/all_to_all | solution.py:926
  31.2 5.5 %order.1 = (s32[1032]{0:T(1024)}, s32[1032]{0:T(1024)}, s32[2]{0:T(128)}) custom-call(s32[1024]{0:T(1024)} %bitcast.72, s32[1024]{0:T(1024)} %bitcast.73, s32[1]{0:T(128)S(6)} %copy.27.count), custom_call_target="tpu_custom_call" | custom-call | tf_op jit(solution)/shard_map/order/pallas_call | solution.py:422
  36.7 5.8 %nodes.1 = (s32[32,16,128]{2,1,0:T(8,128)}, s32[64,128]{1,0:T(8,128)}, s32[64,128]{1,0:T(8,128)}, s32[64,128]{1,0:T(8,128)}, s32[64,128]{1,0:T(8,128)}, /*index=...) custom-call(s32[32,16,128]{2,1,0:T(8,128)} %copy-done.49, ...), custom_call_target="tpu_custom_call" | custom-call | tf_op jit(solution)/shard_map/nodes/pallas_call | solution.py:174
  42.5 1.6 convert_reduce_fusion.1.refs_0_.counts
  44.1 23.1 %all-to-all-done.1.refs_1_ = f32[32,96,128]{2,1,0:T(8,128)} async-done(((f32[32,96,128]{2,1,0:T(8,128)}), f32[32,96,128]{2,1,0:T(8,128)}, u32[]{:S(2)}, u32[]{:S(2)}) %all-to-all-start.1) | async-done | bytes 1572896 | tf_op jit(solution)/shard_map/all_to_all | solution.py:926
  74.0 48.2 %scatter.1 = (f32[3072,128]{1,0:T(8,128)S(1)}, f32[4096,128]{1,0:T(8,128)}) custom-call(s32[32]{0:T(128)S(1)} %convert_reduce_fusion.1.refs_0_.counts, f32[32,96,128]{2,1,0:T(8,128)} %all-to-all-done.1.refs_1_, s32[8192]{0:T(1024)S(1)} %bitcast.55, s32[8192]{0:T(1024)S(1)} %bitcast.56, s32[8192]{0:T(1024)S(1)} %bitcast.57, s32[8192]{0:T(1024)S(1)} %bitcast.58, ...), custom_call_target="tpu_custom_call" | custom-call | tf_op jit(solution)/shard_map/scatter/pallas_call | solution.py:255
  122.2 4.2 %depth.1.refs_4_ = f32[8,16,1536]{2,1,0:T(8,128)} custom-call(f32[3072,128]{1,0:T(8,128)S(1)} %get-tuple-element.43.refs_0_, f32[128,128]{1,0:T(8,128)S(1)} %copy-done.26), custom_call_target="tpu_custom_call" | custom-call | tf_op jit(solution)/shard_map/depth/pallas_call | solution.py:870
  127.5 3.7 all-to-all-start.2
  131.2 4.7 %collective-permute-start = (f32[3072,128]{1,0:T(8,128)}, f32[3072,128]{1,0:T(8,128)}, u32[]{:S(2)}, u32[]{:S(2)}) collective-permute-start(f32[3072,128]{1,0:T(8,128)} %copy-done.17), channel_id=1, source_target_pairs={{0,28},{4,0},{8,4},{12,8},{16,12},{20,16},{24,20},{28,24},{1,29},{... | collective-permute-start | bytes 4718600 | tf_op jit(solution)/shard_map/ppermute | solution.py:30
  137.4 25.0 %within.3.refs_2_.refs_3_ = f32[4096,128]{1,0:T(8,128)S(1)} custom-call(s32[1032]{0:T(1024)S(1)} %copy-done.24, s32[2]{0:T(128)S(1)} %pad_add_fusion.refs_1_, f32[4096,128]{1,0:T(8,128)S(1)} %copy-done.1, f32[4096,128]{1,0:T(8,128)S(1)} %broadcast_in_dim.8.refs_3_, f32[8,16,1536]{2,1,0:T(8,128)} %depth.1.refs_4_), custom_call_target="tpu_custom_call" | custom-call | tf_op jit(solution)/shard_map/within/pallas_call | solution.py:537
  165.3 6.6 %first.1.refs_4_ = f32[4,12,32,128]{3,2,1,0:T(8,128)} custom-call(f32[128,1536]{1,0:T(8,128)S(1)} %bitcast.46, f32[128,256]{1,0:T(8,128)S(1)} %copy-done.20, f32[4096,128]{1,0:T(8,128)S(1)} %copy-done.12), custom_call_target="tpu_custom_call" | custom-call | tf_op jit(solution)/shard_map/first/pallas_call | solution.py:870
  171.8 6.1 %all-to-all-start.3 = ((f32[4,384,128]{2,1,0:T(8,128)}), f32[4,384,128]{2,1,0:T(8,128)S(1)}, u32[]{:S(2)}, u32[]{:S(2)}) async-start(f32[4,384,128]{2,1,0:T(8,128)} %bitcast.17), calls=%async_computation.3 | async-start | bytes 1572864 | tf_op jit(solution)/shard_map/all_to_all | solution.py:882
  184.0 5.5 %all-to-all-done.3 = f32[4,384,128]{2,1,0:T(8,128)S(1)} async-done(((f32[4,384,128]{2,1,0:T(8,128)}), f32[4,384,128]{2,1,0:T(8,128)S(1)}, u32[]{:S(2)}, u32[]{:S(2)}) %all-to-all-start.3) | async-done | bytes 786464 | tf_op jit(solution)/shard_map/all_to_all | solution.py:882
  191.1 5.7 %second.1.refs_6_ = f32[4,12,32,128]{3,2,1,0:T(8,128)} custom-call(s32[2]{0:T(128)S(1)} %pad_add_fusion.5.refs_0_, f32[4,12,32,128]{3,2,1,0:T(8,128)S(1)} %bitcast.44, f32[256,128]{1,0:T(8,128)S(1)} %copy-done.22, f32[4,8,128]{2,1,0:T(8,128)S(1)} %copy-done.45, f32[8,8,128]{2,1,0:T(8,128)S(1)} %copy-done.35, f32[2,128,128]{2,1,0:T(8,128)S(1)} %copy-done.23, ...), custom_call_target="tpu_custom_call" | custom-call | tf_op jit(solution)/shard_map/second/pallas_call | solution.py:870
  196.8 11.0 %all-to-all-start.4 = ((f32[4,384,128]{2,1,0:T(8,128)}), f32[4,384,128]{2,1,0:T(8,128)S(1)}, u32[]{:S(2)}, u32[]{:S(2)}) async-start(f32[4,384,128]{2,1,0:T(8,128)} %bitcast.19), calls=%async_computation.4 | async-start | bytes 1572864 | tf_op jit(solution)/shard_map/all_to_all | solution.py:882
  213.8 18.0 %beyond.2 = (f32[4096,128]{1,0:T(8,128)S(1)}, f32[1536,128]{1,0:T(8,128)S(1)}) custom-call(s32[1032]{0:T(1024)S(1)} %copy-done.44, s32[2]{0:T(128)S(1)} %pad_add_fusion.1.refs_1_, f32[4096,128]{1,0:T(8,128)S(1)} %copy-done.3, f32[4096,128]{1,0:T(8,128)S(1)} %copy-done.10, f32[3072,128]{1,0:T(8,128)} %collective-permute-done.refs_4_, ...), custom_call_target="tpu_custom_call" | custom-call | tf_op jit(solution)/shard_map/beyond/pallas_call | solution.py:537
  235.7 5.9 %first_back.1.refs_6_ = f32[128,1536]{1,0:T(8,128)} custom-call(f32[4,12,32,128]{3,2,1,0:T(8,128)S(1)} %bitcast.45, f32[128,256]{1,0:T(8,128)S(1)} %copy-done.20, f32[4096,128]{1,0:T(8,128)S(1)} %copy-done.15), custom_call_target="tpu_custom_call" | custom-call | tf_op jit(solution)/shard_map/first_back/pallas_call | solution.py:870
  241.6 33.9 %all-to-all-start.5 = ((f32[8,16,1536]{2,1,0:T(8,128)}), f32[8,16,1536]{2,1,0:T(8,128)S(1)}, u32[]{:S(2)}, u32[]{:S(2)}) async-start(f32[8,16,1536]{2,1,0:T(8,128)} %bitcast.21), calls=%async_computation.5 | async-start | bytes 1572864 | tf_op jit(solution)/shard_map/all_to_all | solution.py:882
  280.5 19.9 %beyond.3 = (f32[4096,128]{1,0:T(8,128)S(1)}, f32[1536,128]{1,0:T(8,128)}) custom-call(s32[1032]{0:T(1024)S(1)} %copy-done.44, s32[2]{0:T(128)S(1)} %pad_add_fusion.3.refs_1_, f32[4096,128]{1,0:T(8,128)S(1)} %copy-done.4, f32[4096,128]{1,0:T(8,128)S(1)} %copy-done.16, f32[3072,128]{1,0:T(8,128)} %collective-permute-done.refs_4_, f32[1536,128]{1,0:T(8,128)S(1)} %copy-done.19, ...), custom_call_target="tpu_custom_call" | custom-call | tf_op jit(solution)/shard_map/beyond/pallas_call | solution.py:537
  303.7 1.6 copy-done.6
  305.4 3.3 depth_back.1.one_ref
  308.7 18.5 %collective-permute-done.1.two_ref = f32[1536,128]{1,0:T(8,128)} collective-permute-done((f32[1536,128]{1,0:T(8,128)}, f32[1536,128]{1,0:T(8,128)}, u32[]{:S(2)}, u32[]{:S(2)}) %collective-permute-start.1) | collective-permute-done | bytes 786464 | tf_op jit(solution)/shard_map/ppermute | solution.py:30
  327.3 39.9 %gather.1 = f32[32,48,128]{2,1,0:T(8,128)} custom-call(s32[32]{0:T(128)S(1)} %convert_reduce_fusion.1.refs_0_.counts, s32[32,16,128]{2,1,0:T(8,128)S(1)} %copy-done.21, f32[4096,128]{1,0:T(8,128)S(1)} %copy-done.7, f32[1536,128]{1,0:T(8,128)S(1)} %depth_back.1.one_ref, f32[1536,128]{1,0:T(8,128)} %collective-permute-done.1.two_ref, s32[8192]{0:T(1024)S(1)} %bitcast.47, ...), custom_call_target="tpu_custom_call" | custom-call | tf_op jit(solution)/shard_map/gather/pallas_call | solution.py:319
  367.2 13.4 %all-to-all-start.6 = ((f32[32,48,128]{2,1,0:T(8,128)}), f32[32,48,128]{2,1,0:T(8,128)S(1)}, u32[]{:S(2)}, u32[]{:S(2)}) async-start(f32[32,48,128]{2,1,0:T(8,128)} %gather.1), calls=%async_computation.6 | async-start | bytes 1572864 | tf_op jit(solution)/shard_map/all_to_all | solution.py:968
  381.4 19.8 %all-to-all-done.6.in_ref = f32[32,48,128]{2,1,0:T(8,128)S(1)} async-done(((f32[32,48,128]{2,1,0:T(8,128)}), f32[32,48,128]{2,1,0:T(8,128)S(1)}, u32[]{:S(2)}, u32[]{:S(2)}) %all-to-all-start.6) | async-done | bytes 786464 | tf_op jit(solution)/shard_map/all_to_all | solution.py:968
  402.1 5.0 %finish.1 = (f32[3,256,128]{2,1,0:T(8,128)}, f32[3,256,128]{2,1,0:T(8,128)}) custom-call(s32[33]{0:T(128)} %convert_reduce_fusion.starts, f32[32,48,128]{2,1,0:T(8,128)} %copy-done.48, f32[3,256,128]{2,1,0:T(8,128)} %bitcast.64, f32[3,256,128]{2,1,0:T(8,128)} %bitcast.65), custom_call_target="tpu_custom_call" | custom-call | tf_op jit(solution)/shard_map/finish/pallas_call | solution.py:370
  407.1 2.6 copy_bitcast_fusion
  (121 shorter events, 37.6 us)
Async XLA Ops:
  0.6 29.2 %copy-start = (s32[8,1,65536]{2,1,0:T(1,128)S(1)}, s32[8,1,65536]{2,1,0:T(1,128)}, u32[]{:S(2)}) copy-start(s32[8,1,65536]{2,1,0:T(1,128)} %param.18) | copy-start | bytes 6291460
  6.9 17.9 %all-to-all-start = ((s32[32,16,128]{2,1,0:T(8,128)}), s32[32,16,128]{2,1,0:T(8,128)S(1)}, u32[]{:S(2)}, u32[]{:S(2)}) async-start(s32[32,16,128]{2,1,0:T(8,128)} %slots.1), calls=%async_computation | async-start | bytes 524288 | tf_op jit(solution)/shard_map/all_to_all | solution.py:924
  24.8 11.9 %copy-start.49 = (s32[32,16,128]{2,1,0:T(8,128)}, s32[32,16,128]{2,1,0:T(8,128)S(1)}, u32[]{:S(2)}) copy-start(s32[32,16,128]{2,1,0:T(8,128)S(1)} %all-to-all-done.slots_ref) | copy-start | bytes 786436
  24.8 42.4 %all-to-all-start.1 = ((f32[32,96,128]{2,1,0:T(8,128)}), f32[32,96,128]{2,1,0:T(8,128)}, u32[]{:S(2)}, u32[]{:S(2)}) async-start(f32[32,96,128]{2,1,0:T(8,128)} %pack.1), calls=%async_computation.1 | async-start | bytes 3145728 | tf_op jit(solution)/shard_map/all_to_all | solution.py:926
  29.8 92.3 %copy-start.26 = (f32[128,128]{1,0:T(8,128)S(1)}, f32[128,128]{1,0:T(8,128)}, u32[]{:S(2)}) copy-start(f32[128,128]{1,0:T(8,128)} %constant.60.clone.refs_1_) | copy-start | bytes 196612
  122.2 13.7 %copy-start.47 = (s32[2]{0:T(128)S(1)}, s32[2]{0:T(128)}, u32[]{:S(2)}) copy-start(s32[2]{0:T(128)} %get-tuple-element.32.refs_10_) | copy-start | bytes 28
  127.5 9.8 %copy-start.24 = (s32[1032]{0:T(1024)S(1)}, s32[1032]{0:T(1024)}, u32[]{:S(2)}) copy-start(s32[1032]{0:T(1024)} %get-tuple-element.31.refs_0_) | copy-start | bytes 12388
  127.5 36.1 %all-to-all-start.2 = ((f32[8,16,1536]{2,1,0:T(8,128)}), f32[8,16,1536]{2,1,0:T(8,128)S(1)}, u32[]{:S(2)}, u32[]{:S(2)}) async-start(f32[8,16,1536]{2,1,0:T(8,128)} %depth.1.refs_4_), calls=%async_computation.2 | async-start | bytes 1572864 | tf_op jit(solution)/shard_map/all_to_all | solution.py:882
  131.2 6.1 %copy-start.1 = (f32[4096,128]{1,0:T(8,128)S(1)}, f32[4096,128]{1,0:T(8,128)}, u32[]{:S(2)}) copy-start(f32[4096,128]{1,0:T(8,128)} %get-tuple-element.41.refs_2_) | copy-start | bytes 6291460
  131.2 79.3 %collective-permute-start = (f32[3072,128]{1,0:T(8,128)}, f32[3072,128]{1,0:T(8,128)}, u32[]{:S(2)}, u32[]{:S(2)}) collective-permute-start(f32[3072,128]{1,0:T(8,128)} %copy-done.17), channel_id=1, source_target_pairs={{0,28},{4,0},{8,4},{12,8},{16,12},{20,16},{24,20},{28,24},{1,29},{... | collective-permute-start | bytes 4718600 | tf_op jit(solution)/shard_map/ppermute | solution.py:30
  137.3 26.3 %copy-start.20 = (f32[128,256]{1,0:T(8,128)S(1)}, f32[128,256]{1,0:T(8,128)}, u32[]{:S(2)}) copy-start(f32[128,256]{1,0:T(8,128)} %constant.61.clone.refs_1_) | copy-start | bytes 393220
  171.8 17.7 %all-to-all-start.3 = ((f32[4,384,128]{2,1,0:T(8,128)}), f32[4,384,128]{2,1,0:T(8,128)S(1)}, u32[]{:S(2)}, u32[]{:S(2)}) async-start(f32[4,384,128]{2,1,0:T(8,128)} %bitcast.17), calls=%async_computation.3 | async-start | bytes 1572864 | tf_op jit(solution)/shard_map/all_to_all | solution.py:882
  181.9 7.6 %copy-start.22 = (f32[256,128]{1,0:T(8,128)S(1)}, f32[256,128]{1,0:T(8,128)}, u32[]{:S(2)}) copy-start(f32[256,128]{1,0:T(8,128)} %constant.62.clone.refs_2_) | copy-start | bytes 393220
  181.9 7.6 %copy-start.23 = (f32[2,128,128]{2,1,0:T(8,128)S(1)}, f32[2,128,128]{2,1,0:T(8,128)}, u32[]{:S(2)}) copy-start(f32[2,128,128]{2,1,0:T(8,128)} %constant.65.clone.refs_5_) | copy-start | bytes 393220
  181.9 7.6 %copy-start.35 = (f32[8,8,128]{2,1,0:T(8,128)S(1)}, f32[8,8,128]{2,1,0:T(8,128)}, u32[]{:S(2)}) copy-start(f32[8,8,128]{2,1,0:T(8,128)} %constant.64.clone.refs_4_) | copy-start | bytes 98308
  181.9 7.7 %copy-start.45 = (f32[4,8,128]{2,1,0:T(8,128)S(1)}, f32[4,8,128]{2,1,0:T(8,128)}, u32[]{:S(2)}) copy-start(f32[4,8,128]{2,1,0:T(8,128)} %constant.63.clone.refs_3_) | copy-start | bytes 49156
  196.8 13.7 %copy-start.44 = (s32[1032]{0:T(1024)S(1)}, s32[1032]{0:T(1024)}, u32[]{:S(2)}) copy-start(s32[1032]{0:T(1024)} %get-tuple-element.42.refs_0_) | copy-start | bytes 12388
  196.8 37.3 %all-to-all-start.4 = ((f32[4,384,128]{2,1,0:T(8,128)}), f32[4,384,128]{2,1,0:T(8,128)S(1)}, u32[]{:S(2)}, u32[]{:S(2)}) async-start(f32[4,384,128]{2,1,0:T(8,128)} %bitcast.19), calls=%async_computation.4 | async-start | bytes 1572864 | tf_op jit(solution)/shard_map/all_to_all | solution.py:882
  241.6 62.1 %all-to-all-start.5 = ((f32[8,16,1536]{2,1,0:T(8,128)}), f32[8,16,1536]{2,1,0:T(8,128)S(1)}, u32[]{:S(2)}, u32[]{:S(2)}) async-start(f32[8,16,1536]{2,1,0:T(8,128)} %bitcast.21), calls=%async_computation.5 | async-start | bytes 1572864 | tf_op jit(solution)/shard_map/all_to_all | solution.py:882
  300.5 26.8 %collective-permute-start.1 = (f32[1536,128]{1,0:T(8,128)}, f32[1536,128]{1,0:T(8,128)}, u32[]{:S(2)}, u32[]{:S(2)}) collective-permute-start(f32[1536,128]{1,0:T(8,128)} %get-tuple-element.47), channel_id=1, source_target_pairs={{0,4},{4,8},{8,12},{12,16},{16,20},{20,24},{24,28},{28,0},{1,5},{5... | collective-permute-start | bytes 2359304 | tf_op jit(solution)/shard_map/ppermute | solution.py:30
  305.3 21.9 %copy-start.7 = (f32[4096,128]{1,0:T(8,128)S(1)}, f32[4096,128]{1,0:T(8,128)}, u32[]{:S(2)}) copy-start(f32[4096,128]{1,0:T(8,128)} %copy-done.5) | copy-start | bytes 6291460
  305.3 21.9 %copy-start.21 = (s32[32,16,128]{2,1,0:T(8,128)S(1)}, s32[32,16,128]{2,1,0:T(8,128)}, u32[]{:S(2)}) copy-start(s32[32,16,128]{2,1,0:T(8,128)} %get-tuple-element.30.node_ref) | copy-start | bytes 786436
  305.3 21.9 %copy-start.27 = (s32[64,128]{1,0:T(8,128)S(1)}, s32[64,128]{1,0:T(8,128)}, u32[]{:S(2)}) copy-start(s32[64,128]{1,0:T(8,128)} %get-tuple-element.48) | copy-start | bytes 98308
  305.3 21.9 %copy-start.28 = (s32[64,128]{1,0:T(8,128)S(1)}, s32[64,128]{1,0:T(8,128)}, u32[]{:S(2)}) copy-start(s32[64,128]{1,0:T(8,128)} %get-tuple-element.49) | copy-start | bytes 98308
  305.3 21.9 %copy-start.29 = (s32[64,128]{1,0:T(8,128)S(1)}, s32[64,128]{1,0:T(8,128)}, u32[]{:S(2)}) copy-start(s32[64,128]{1,0:T(8,128)} %get-tuple-element.50) | copy-start | bytes 98308
  305.3 21.9 %copy-start.30 = (s32[64,128]{1,0:T(8,128)S(1)}, s32[64,128]{1,0:T(8,128)}, u32[]{:S(2)}) copy-start(s32[64,128]{1,0:T(8,128)} %get-tuple-element.51) | copy-start | bytes 98308
  305.3 21.9 %copy-start.31 = (s32[64,128]{1,0:T(8,128)S(1)}, s32[64,128]{1,0:T(8,128)}, u32[]{:S(2)}) copy-start(s32[64,128]{1,0:T(8,128)} %get-tuple-element.52) | copy-start | bytes 98308
  305.3 21.9 %copy-start.32 = (s32[64,128]{1,0:T(8,128)S(1)}, s32[64,128]{1,0:T(8,128)}, u32[]{:S(2)}) copy-start(s32[64,128]{1,0:T(8,128)} %get-tuple-element.53) | copy-start | bytes 98308
  305.4 21.9 %copy-start.33 = (s32[64,128]{1,0:T(8,128)S(1)}, s32[64,128]{1,0:T(8,128)}, u32[]{:S(2)}) copy-start(s32[64,128]{1,0:T(8,128)} %get-tuple-element.54) | copy-start | bytes 98308
  305.4 21.9 %copy-start.34 = (s32[64,128]{1,0:T(8,128)S(1)}, s32[64,128]{1,0:T(8,128)}, u32[]{:S(2)}) copy-start(s32[64,128]{1,0:T(8,128)} %get-tuple-element.55) | copy-start | bytes 98308
  327.3 53.3 %copy-start.50 = (f32[3,32768]{1,0:T(4,128)S(1)}, f32[3,32768]{1,0:T(4,128)}, u32[]{:S(2)}) copy-start(f32[3,32768]{1,0:T(4,128)} %param.16) | copy-start | bytes 1179652
  367.2 34.0 %all-to-all-start.6 = ((f32[32,48,128]{2,1,0:T(8,128)}), f32[32,48,128]{2,1,0:T(8,128)S(1)}, u32[]{:S(2)}, u32[]{:S(2)}) async-start(f32[32,48,128]{2,1,0:T(8,128)} %gather.1), calls=%async_computation.6 | async-start | bytes 1572864 | tf_op jit(solution)/shard_map/all_to_all | solution.py:968
  (28 other events, 34.3 us)

commit v5 on v4

--- a/solution.py
+++ b/solution.py
@@ -31,6 +31,7 @@
 
 
 SPAN = 16
+PARTS = (25, 37, 52)
 
 SMEM_SPEC = pl.BlockSpec(memory_space=pltpu.SMEM)
 VMEM_SPEC = pl.BlockSpec(memory_space=pltpu.VMEM)
@@ -42,6 +43,14 @@
 def ignoring(kernel, inputs, extra):
     def run(*refs):
         kernel(*refs[:inputs], *refs[inputs + extra :])
+
+    return run
+
+
+def marking(kernel, inputs):
+    def run(*refs):
+        refs[inputs + 1][...] = jnp.zeros(refs[inputs + 1].shape, jnp.float32)
+        kernel(*refs[: inputs + 1], *refs[inputs + 2 :])
 
     return run
 
@@ -79,6 +88,7 @@
         in_specs=[SMEM_SPEC, VMEM_SPEC],
         out_specs=VMEM_SPEC,
         scratch_shapes=[pltpu.VMEM((rows + depth + 8, 128), jnp.int32)],
+        compiler_params=pltpu.CompilerParams(vmem_limit_bytes=8 * 1024 * 1024),
         name="slots",
     )(starts, route)
 
@@ -138,6 +148,7 @@
         in_specs=[SMEM_SPEC, VMEM_SPEC],
         out_specs=VMEM_SPEC,
         scratch_shapes=[pltpu.VMEM((6 * stride, 128), jnp.float32)],
+        compiler_params=pltpu.CompilerParams(vmem_limit_bytes=8 * 1024 * 1024),
         name="pack",
     )(starts, pos)
 
@@ -176,6 +187,7 @@
         out_shape=(jax.ShapeDtypeStruct(slots.shape, jnp.int32),) + (one,) * (2 * lists),
         in_specs=[VMEM_SPEC] * 2,
         out_specs=(VMEM_SPEC,) * (1 + 2 * lists),
+        compiler_params=pltpu.CompilerParams(vmem_limit_bytes=8 * 1024 * 1024),
         name="nodes",
     )(slots, perm)
     flat = [x.reshape(-1) for x in found[1:]]
@@ -266,7 +278,7 @@
             pltpu.VMEM((rp * 128 + 8, 128), jnp.float32),
             pltpu.VMEM((depth * 128, 128), jnp.float32),
         ],
-        compiler_params=pltpu.CompilerParams(vmem_limit_bytes=52 * 1024 * 1024),
+        compiler_params=pltpu.CompilerParams(vmem_limit_bytes=40 * 1024 * 1024),
         name="scatter",
     )(counts, data, *nodes, *after)
 
@@ -326,7 +338,7 @@
             pltpu.VMEM((depth * 128, 128), jnp.float32),
             pltpu.VMEM((128, 128), jnp.float32),
         ],
-        compiler_params=pltpu.CompilerParams(vmem_limit_bytes=32 * 1024 * 1024),
+        compiler_params=pltpu.CompilerParams(vmem_limit_bytes=8 * 1024 * 1024),
         name="gather",
     )(counts, nodes, sums, one, two, *rows)
 
@@ -373,6 +385,7 @@
         in_specs=[SMEM_SPEC] + [VMEM_SPEC] * 3,
         out_specs=(VMEM_SPEC,) * 2,
         scratch_shapes=[pltpu.VMEM((3 * stride, 128), jnp.float32)],
+        compiler_params=pltpu.CompilerParams(vmem_limit_bytes=8 * 1024 * 1024),
         name="finish",
     )(starts, data, pos, noise)
 
@@ -424,6 +437,7 @@
         out_shape=(jax.ShapeDtypeStruct((size,), jnp.int32),) * 2 + (jax.ShapeDtypeStruct((2,), jnp.int32),),
         in_specs=[SMEM_SPEC] * 3,
         out_specs=(SMEM_SPEC,) * 3,
+        compiler_params=pltpu.CompilerParams(vmem_limit_bytes=8 * 1024 * 1024),
         name="order",
     )(first, second, count)
 
@@ -438,7 +452,7 @@
 
 def pair_kernel(pairs, bounds, cells_ref, near_in, *refs, rp, coef, unroll, beyond):
     if beyond:
-        other_ref, far_in, near_ref, far_ref, other_cells, far_sums = refs
+        other_ref, far_in, near_ref, token, far_ref, other_cells, far_sums = refs
         fill_cells(other_ref, other_cells, rp)
         for c in range(3):
             @pl.loop(0, rp // 8)
@@ -446,13 +460,14 @@
                 at = pl.ds(pl.multiple_of(c * rp + i * 8, 8), 8)
                 far_sums[pl.ds(i * 64 + c, 8, stride=8), :] = far_in[at, :]
     else:
-        (near_ref,) = refs
+        near_ref, token = refs
         other_cells, far_sums = cells_ref, near_ref
     lane = lax.broadcasted_iota(jnp.int32, (8, 128), 1)
     sub = lax.broadcasted_iota(jnp.int32, (8, 128), 0)
     left = lane < 64
     unturn = (lane + sub) & 127
     near_ref[...] = near_in[...]
+    token[...] = jnp.zeros((8, 128), jnp.float32)
 
     def row(k):
         return pl.ds(pl.multiple_of((k >> 1) * 8, 8), 8)
@@ -529,7 +544,7 @@
     rp = cells.shape[0] // 8
     beyond = beside is not None
     extra = [beside, far] if beyond else []
-    out = [jax.ShapeDtypeStruct((8 * rp, 128), jnp.float32)]
+    out = [jax.ShapeDtypeStruct((8 * rp, 128), jnp.float32), jax.ShapeDtypeStruct((8, 128), jnp.float32)]
     scratch = []
     if beyond:
         out.append(jax.ShapeDtypeStruct((3 * rp, 128), jnp.float32))
@@ -544,7 +559,7 @@
         in_specs=[SMEM_SPEC] * 2 + [VMEM_SPEC] * (2 + len(extra)) + [ANY_SPEC] * len(after),
         out_specs=(VMEM_SPEC,) * len(out),
         scratch_shapes=scratch,
-        compiler_params=pltpu.CompilerParams(vmem_limit_bytes=32 * 1024 * 1024),
+        compiler_params=pltpu.CompilerParams(vmem_limit_bytes=8 * 1024 * 1024),
         name="beyond" if beyond else "within",
     )(pairs, bounds, cells, near, *extra, *after)
 
@@ -868,12 +883,12 @@
 
     def run(name, kernel, shape, args, scratch, specs=None, after=(), **sizes):
         return pl.pallas_call(
-            ignoring(functools.partial(kernel, **sizes), len(args), len(after)),
-            out_shape=jax.ShapeDtypeStruct(shape, f32),
+            marking(ignoring(functools.partial(kernel, **sizes), len(args), len(after)), len(args) + len(after)),
+            out_shape=(jax.ShapeDtypeStruct(shape, f32), jax.ShapeDtypeStruct((8, 128), f32)),
             in_specs=(specs or [VMEM_SPEC] * len(args)) + [ANY_SPEC] * len(after),
-            out_specs=VMEM_SPEC,
+            out_specs=(VMEM_SPEC,) * 2,
             scratch_shapes=[pltpu.VMEM(scratch, f32)],
-            compiler_params=pltpu.CompilerParams(vmem_limit_bytes=24 * 1024 * 1024),
+            compiler_params=pltpu.CompilerParams(vmem_limit_bytes=8 * 1024 * 1024),
             name=name,
             grid=(1,),
         )(*args, *after)
@@ -887,25 +902,26 @@
     force = pl.BlockSpec((rows, 128), lambda i: (1, 0))
     lanes = 6 * wide * share
     ids = jnp.stack([lax.axis_index("gx"), lax.axis_index("gy")]).astype(jnp.int32)
-    value = run("depth", depth_kernel, (n_gx, tall, lanes), (grid_data, tables["ahead"]), (rows, 128),
+    value, token = run("depth", depth_kernel, (n_gx, tall, lanes), (grid_data, tables["ahead"]), (rows, 128),
                 [force, full((G, 128))], n_gx=n_gx, tall=tall, wide=wide)
-    after = fill(0, value)
+    after = fill(0, token)
     value = swap(value, "gx").reshape(G, lanes)
-    value = run("first", first_kernel, (n_gy, 6 * views, wide, 128), (value, tables["first"]), (rows, 128),
+    value, token = run("first", first_kernel, (n_gy, 6 * views, wide, 128), (value, tables["first"]), (rows, 128),
                 after=after, n_gy=n_gy, share=share, wide=wide)
-    after = fill(1, value)
+    after = fill(1, token)
     value = swap(value.reshape(n_gy, 6 * views * wide, 128), "gy").reshape(n_gy, 6 * views, wide, 128)
     args = (ids, value, tables["second"], tables["across"], tables["deep"], tables["down"])
-    value = run("second", second_kernel, (n_gy, 6 * views, wide, 128), args, (8, 128),
+    value, token = run("second", second_kernel, (n_gy, 6 * views, wide, 128), args, (8, 128),
                 [SMEM_SPEC] + [VMEM_SPEC] * 5, after, n_gy=n_gy, views=views, wide=wide)
-    after = fill(2, value)
+    after = fill(2, token)
     value = swap(value.reshape(n_gy, 6 * views * wide, 128), "gy").reshape(n_gy, 6 * views, wide, 128)
-    value = run("first_back", first_back_kernel, (G, lanes), (value, tables["first_back"]), (rows, 128),
+    value, token = run("first_back", first_back_kernel, (G, lanes), (value, tables["first_back"]), (rows, 128),
                 after=after, n_gy=n_gy, share=share, wide=wide)
-    after = fill(3, value)
+    after = fill(3, token)
     value = swap(value.reshape(n_gx, tall, lanes), "gx")
-    return run("depth_back", depth_back_kernel, (rows, 128), (value, tables["back"]), (rows, 128),
+    value, _ = run("depth_back", depth_back_kernel, (rows, 128), (value, tables["back"]), (rows, 128),
                after=after, n_gx=n_gx, tall=tall, wide=wide)
+    return value
 
 
 def shards(positions, noise, route, node_perm, pair_first, pair_second, pair_count):
@@ -930,33 +946,27 @@
     own_pairs, far_pairs, totals = order_call(pair_first[0], pair_second[0], pair_count, slots // CELL)
     grid_data, cells = scatter_call(node_lists, counts, data, rp, after=(totals,))
 
-    beside = shifted(grid_data, "gx", -1)
     steps = pair_first.shape[1]
-    marks = [jnp.minimum(totals[0], steps // 4), jnp.minimum(totals[0], steps * 3 // 8)]
-    half = totals[1] // 16 * 8
-    begin = jnp.int32(0)
-    state = {"sums": jnp.zeros_like(cells), "far": jnp.zeros((3 * rp, 128), jnp.float32)}
-
-    def within(low, high, after):
-        (state["sums"],) = pair_call(own_pairs, jnp.stack([low, high]), cells, state["sums"], after=after)
-
-    def beyond(low, high, after):
-        state["sums"], state["far"] = pair_call(
-            far_pairs, jnp.stack([low, high]), cells, state["sums"], beside, state["far"], after=after
+    marks = [jnp.int32(0)] + [jnp.minimum(totals[0], steps * part // 128) for part in PARTS] + [totals[0]]
+    state = {"sums": jnp.zeros_like(cells)}
+
+    def within(n, after):
+        state["sums"], token = pair_call(own_pairs, jnp.stack(marks[n : n + 2]), cells, state["sums"], after=after)
+        return token
+
+    def fill(n, token):
+        if n < 3:
+            if n == 1:
+                ready, _ = lax.optimization_barrier((grid_data, token))
+                state["beside"] = shifted(ready, "gx", -1)
+            return (within(n, (token,)),)
+        bounds = jnp.stack([marks[0], totals[1]])
+        none = jnp.zeros((3 * rp, 128), jnp.float32)
+        state["sums"], _, far = pair_call(
+            far_pairs, bounds, cells, state["sums"], state["beside"], none, after=(token,)
         )
-
-    def fill(n, value):
-        if n == 0:
-            within(begin, marks[0], (value,))
-        elif n == 1:
-            within(marks[0], marks[1], (value,))
-        elif n == 2:
-            beyond(begin, half, (value,))
-        else:
-            beyond(half, totals[1], (value,))
-            state["far"] = shifted(state["far"], "gx", 1)
-            within(marks[1], totals[0], ())
-        return (state["sums"],)
+        state["far"] = shifted(far, "gx", 1)
+        return (within(3, ()),)
 
     share = G // 2 // n_gx
     if share % 8 == 0 and share * (G // n_gy) % 128 == 0:

time: 413 us -> 390 us (0.944)
  starting transfers between devices: 85.5 us -> 45.8 us
  Pallas kernels: 206 us -> 243 us
  waiting for transfers between devices: 68 us -> 40.3 us
  local copies, waits for them, and re-layouts: 38.9 us -> 51.1 us
    pallas_call x5, Pallas kernels: 64.4 us -> 112 us  [pair_call(): pl.pallas_call(ignoring(functools.partial(pair_kernel, rp=rp, coef=coef,...]
    all_to_all x4, starting transfers between devices: 54.7 us -> 18.3 us  [swap(): return lax.all_to_all(value, axis, split_axis=0, concat_axis=0, tiled=True)]
    ppermute x2, waiting for transfers between devices: 18.5 us -> 1.55 us  [shifted(): lax.ppermute(value, axis, [(i, (i + by) % devices) for i in range(devices)])]
    unnamed x104 -> x126, local copies, waits for them, and re-layouts: 34.8 us -> 50.3 us
    all_to_all x4, waiting for transfers between devices: 5.54 us -> 0.01 us  [swap(): return lax.all_to_all(value, axis, split_axis=0, concat_axis=0, tiled=True)]
    all_to_all x1, waiting for transfers between devices: 23.1 us -> 17.7 us  [shards(): data = swap(pack_call(starts, places, depth))]
    all_to_all x1, starting transfers between devices: 13.4 us -> 8.22 us  [shards(): swap(gather_call(row_lists, counts, nodes, state['sums'], wave_vel, state...]
  transfers between devices with their start and end apart: 9 -> 9, of which waited for: 5 -> 4; matrix products, arithmetic and copies ran while one was open for 2% -> 2% of each run, Pallas kernels for 24% -> 37%
where the time goes in v5:
time: 390 us; the launch traced here: 389 us
  Pallas kernels  243 us (62%)
  local copies, waits for them, and re-layouts  51.1 us (13%)
  starting transfers between devices  45.8 us (12%)
  waiting for transfers between devices  40.3 us (10%)
  other arithmetic  5.17 us (1%)
    pallas_call x5, Pallas kernels, pair_call(): pl.pallas_call(ignoring(functools.partial(pair_kernel, rp=rp, coef=coef,...  112 us
    unnamed x126, local copies, waits for them, and re-layouts  50.3 us
    pallas_call x1, Pallas kernels, scatter_call(): pl.pallas_call(ignoring(functools.partial(scatter_kernel, depth=depth, rp...  45.1 us
    pallas_call x1, Pallas kernels, gather_call(): pl.pallas_call(functools.partial(gather_kernel, depth=depth, rp=rp, lists...  38.2 us
    pallas_call x5, Pallas kernels, run(): pl.pallas_call(marking(ignoring(functools.partial(kernel, **sizes), len(a...  22 us
    all_to_all x1, waiting for transfers between devices, shards(): swap(gather_call(row_lists, counts, nodes, state['sums'], wave_vel, state...  18.8 us
    all_to_all x4, starting transfers between devices, swap(): return lax.all_to_all(value, axis, split_axis=0, concat_axis=0, tiled=True)  18.3 us
    all_to_all x1, waiting for transfers between devices, shards(): data = swap(pack_call(starts, places, depth))  17.7 us
  transfers between devices with their start and end apart: 9, of which 4 were waited for; matrix products, arithmetic and copies ran while one was open for 2% of the time, Pallas kernels for 37%

profile of v5, /device:TPU:0, one launch (start us, length us, event | category | flops | bytes accessed | tf_op | source)
XLA Modules:
  0.0 389.1 jit_solution(13959209759596195591)
XLA Ops:
  0.7 1.8 convert_reduce_fusion.starts
  3.3 3.6 slots.1
  7.0 7.3 %all-to-all-start = ((s32[32,16,128]{2,1,0:T(8,128)}), s32[32,16,128]{2,1,0:T(8,128)S(1)}, u32[]{:S(2)}, u32[]{:S(2)}) async-start(s32[32,16,128]{2,1,0:T(8,128)} %slots.1), calls=%async_computation | async-start | bytes 524288 | tf_op jit(solution)/shard_map/all_to_all | solution.py:940
  15.4 6.1 %pack.1 = f32[32,96,128]{2,1,0:T(8,128)S(1)} custom-call(s32[33]{0:T(128)S(1)} %convert_reduce_fusion.starts, f32[3,256,128]{2,1,0:T(8,128)S(1)} %bitcast.44), custom_call_target="tpu_custom_call" | custom-call | tf_op jit(solution)/shard_map/pack/pallas_call | solution.py:145
  22.6 2.2 all-to-all-done.slots_ref
  24.9 3.7 all-to-all-start.1
  29.3 9.5 %order.1 = (s32[1032]{0:T(1024)S(1)}, s32[1032]{0:T(1024)S(1)}, s32[2]{0:T(128)S(1)}) custom-call(s32[1024]{0:T(1024)S(1)} %bitcast.73, s32[1024]{0:T(1024)S(1)} %bitcast.74, s32[1]{0:T(128)S(6)} %copy.29.count), custom_call_target="tpu_custom_call" | custom-call | tf_op jit(solution)/shard_map/order/pallas_call | solution.py:435
  38.8 3.8 nodes.1
  48.3 17.7 %all-to-all-done.1.refs_1_ = f32[32,96,128]{2,1,0:T(8,128)} async-done(((f32[32,96,128]{2,1,0:T(8,128)}), f32[32,96,128]{2,1,0:T(8,128)}, u32[]{:S(2)}, u32[]{:S(2)}) %all-to-all-start.1) | async-done | bytes 1572896 | tf_op jit(solution)/shard_map/all_to_all | solution.py:942
  66.0 45.1 %scatter.1 = (f32[3072,128]{1,0:T(8,128)S(1)}, f32[4096,128]{1,0:T(8,128)S(1)}) custom-call(s32[32]{0:T(128)S(1)} %convert_reduce_fusion.1.refs_0_.counts, f32[32,96,128]{2,1,0:T(8,128)} %all-to-all-done.1.refs_1_, s32[8192]{0:T(1024)S(1)} %bitcast.65, s32[8192]{0:T(1024)S(1)} %bitcast.66, s32[8192]{0:T(1024)S(1)} %bitcast.67, s32[8192]{0:T(1024)S(1)} %bitcast.68, ...), custom_call_target="tpu_custom_call" | custom-call | tf_op jit(solution)/shard_map/scatter/pallas_call | solution.py:267
  112.4 3.3 depth.1
  117.7 6.2 %all-to-all-start.2 = ((f32[8,16,1536]{2,1,0:T(8,128)}), f32[8,16,1536]{2,1,0:T(8,128)S(1)}, u32[]{:S(2)}, u32[]{:S(2)}) async-start(f32[8,16,1536]{2,1,0:T(8,128)} %copy-done.19), calls=%async_computation.2 | async-start | bytes 1572864 | tf_op jit(solution)/shard_map/all_to_all | solution.py:897
  125.6 20.9 %within.4 = (f32[4096,128]{1,0:T(8,128)S(1)}, f32[8,128]{1,0:T(8,128)S(1)}) custom-call(s32[1032]{0:T(1024)S(1)} %get-tuple-element.47.refs_0_, s32[2]{0:T(128)S(1)} %pad_add_fusion.refs_1_, f32[4096,128]{1,0:T(8,128)S(1)} %copy-done.2, f32[4096,128]{1,0:T(8,128)S(1)} %broadcast_in_dim.8.refs_3_, f32[8,128]{1,0:T(8,128)S(1)} %get-tuple-element.60.refs_4_), custom_call_target="tpu_custom_call" | custom-call | tf_op jit(solution)/shard_map/within/pallas_call | solution.py:552
  147.9 5.7 %first.1 = (f32[4,12,32,128]{3,2,1,0:T(8,128)S(1)}, f32[8,128]{1,0:T(8,128)S(1)}) custom-call(f32[128,1536]{1,0:T(8,128)S(1)} %bitcast.46, f32[128,256]{1,0:T(8,128)S(1)} %copy-done.21, f32[8,128]{1,0:T(8,128)S(1)} %get-tuple-element.63.refs_2_), custom_call_target="tpu_custom_call" | custom-call | tf_op jit(solution)/shard_map/first/pallas_call | solution.py:885
  155.1 5.0 %all-to-all-start.3 = ((f32[4,384,128]{2,1,0:T(8,128)}), f32[4,384,128]{2,1,0:T(8,128)S(1)}, u32[]{:S(2)}, u32[]{:S(2)}) async-start(f32[4,384,128]{2,1,0:T(8,128)} %bitcast.52), calls=%async_computation.3 | async-start | bytes 1572864 | tf_op jit(solution)/shard_map/all_to_all | solution.py:897
  160.1 4.7 %collective-permute-start = (f32[3072,128]{1,0:T(8,128)}, f32[3072,128]{1,0:T(8,128)}, u32[]{:S(2)}, u32[]{:S(2)}) collective-permute-start(f32[3072,128]{1,0:T(8,128)} %copy-done.15), channel_id=1, source_target_pairs={{0,28},{4,0},{8,4},{12,8},{16,12},{20,16},{24,20},{28,24},{1,29},{... | collective-permute-start | bytes 4718600 | tf_op jit(solution)/shard_map/ppermute | solution.py:30
  171.3 10.4 %within.5 = (f32[4096,128]{1,0:T(8,128)S(1)}, f32[8,128]{1,0:T(8,128)S(1)}) custom-call(s32[1032]{0:T(1024)S(1)} %get-tuple-element.47.refs_0_, s32[2]{0:T(128)S(1)} %get-tuple-element.95.refs_1_, f32[4096,128]{1,0:T(8,128)S(1)} %copy-done.3, f32[4096,128]{1,0:T(8,128)S(1)} %copy-done.8, f32[8,128]{1,0:T(8,128)S(1)} %copy-done.52), custom_call_target="tpu_custom_call" | custom-call | tf_op jit(solution)/shard_map/within/pallas_call | solution.py:552
  187.4 4.8 %second.1 = (f32[4,12,32,128]{3,2,1,0:T(8,128)S(1)}, f32[8,128]{1,0:T(8,128)S(1)}) custom-call(s32[2]{0:T(128)S(1)} %copy-done.60, f32[4,12,32,128]{3,2,1,0:T(8,128)S(1)} %bitcast.48, f32[256,128]{1,0:T(8,128)S(1)} %copy-done.25, f32[4,8,128]{2,1,0:T(8,128)S(1)} %copy-done.46, f32[8,8,128]{2,1,0:T(8,128)S(1)} %copy-done.45, f32[2,128,128]{2,1,0:T(8,128)S(1)} %copy-done.26, ...), custom_call_target="tpu_custom_call" | custom-call | tf_op jit(solution)/shard_map/second/pallas_call | solution.py:885
  193.8 3.5 all-to-all-start.4
  201.8 12.9 %within.6 = (f32[4096,128]{1,0:T(8,128)S(1)}, f32[8,128]{1,0:T(8,128)S(1)}) custom-call(s32[1032]{0:T(1024)S(1)} %get-tuple-element.47.refs_0_, s32[2]{0:T(128)S(1)} %copy-done.59, f32[4096,128]{1,0:T(8,128)S(1)} %copy-done.4, f32[4096,128]{1,0:T(8,128)S(1)} %copy-done.10, f32[8,128]{1,0:T(8,128)S(1)} %copy-done.54), custom_call_target="tpu_custom_call" | custom-call | tf_op jit(solution)/shard_map/within/pallas_call | solution.py:552
  216.0 5.0 %first_back.1 = (f32[128,1536]{1,0:T(8,128)S(1)}, f32[8,128]{1,0:T(8,128)S(1)}) custom-call(f32[4,12,32,128]{3,2,1,0:T(8,128)S(1)} %bitcast.47, f32[128,256]{1,0:T(8,128)S(1)} %copy-done.21, f32[8,128]{1,0:T(8,128)S(1)} %get-tuple-element.72.refs_2_), custom_call_target="tpu_custom_call" | custom-call | tf_op jit(solution)/shard_map/first_back/pallas_call | solution.py:885
  222.0 3.5 all-to-all-start.5
  230.2 56.1 %beyond.1 = (f32[4096,128]{1,0:T(8,128)S(1)}, f32[8,128]{1,0:T(8,128)}, f32[1536,128]{1,0:T(8,128)}) custom-call(s32[1032]{0:T(1024)S(1)} %get-tuple-element.58.refs_0_, s32[2]{0:T(128)S(1)} %get-tuple-element.92.refs_1_, f32[4096,128]{1,0:T(8,128)S(1)} %copy-done.5, f32[4096,128]{1,0:T(8,128)S(1)} %copy-done.12, f32[3072,128]{1,0:T(8,128)} %collective-permute-done.refs_4_, ...), custom_call_target="tpu_custom_call" | custom-call | tf_op jit(solution)/shard_map/beyond/pallas_call | solution.py:552
  286.3 3.5 collective-permute-start.1
  289.8 11.2 %within.7 = (f32[4096,128]{1,0:T(8,128)S(1)}, f32[8,128]{1,0:T(8,128)S(1)}) custom-call(s32[1032]{0:T(1024)S(1)} %get-tuple-element.47.refs_0_, s32[2]{0:T(128)S(1)} %get-tuple-element.93.refs_1_, f32[4096,128]{1,0:T(8,128)S(1)} %copy-done.5, f32[4096,128]{1,0:T(8,128)S(1)} %get-tuple-element.74.refs_3_), custom_call_target="tpu_custom_call" | custom-call | tf_op jit(solution)/shard_map/within/pallas_call | solution.py:552
  303.2 3.3 depth_back.1
  308.1 1.6 copy-done.14
  315.7 38.2 %gather.1 = f32[32,48,128]{2,1,0:T(8,128)} custom-call(s32[32]{0:T(128)S(1)} %copy-done.50, s32[32,16,128]{2,1,0:T(8,128)S(1)} %copy-done.24, f32[4096,128]{1,0:T(8,128)S(1)} %copy-done.14, f32[1536,128]{1,0:T(8,128)S(1)} %get-tuple-element.78.one_ref, f32[1536,128]{1,0:T(8,128)} %collective-permute-done.1.two_ref, s32[8192]{0:T(1024)S(1)} %bitcast.57, ...), custom_call_target="tpu_custom_call" | custom-call | tf_op jit(solution)/shard_map/gather/pallas_call | solution.py:331
  353.9 8.2 %all-to-all-start.6 = ((f32[32,48,128]{2,1,0:T(8,128)}), f32[32,48,128]{2,1,0:T(8,128)S(1)}, u32[]{:S(2)}, u32[]{:S(2)}) async-start(f32[32,48,128]{2,1,0:T(8,128)} %gather.1), calls=%async_computation.6 | async-start | bytes 1572864 | tf_op jit(solution)/shard_map/all_to_all | solution.py:978
  362.1 1.8 copy.27
  363.9 18.8 %all-to-all-done.6.in_ref = f32[32,48,128]{2,1,0:T(8,128)S(1)} async-done(((f32[32,48,128]{2,1,0:T(8,128)}), f32[32,48,128]{2,1,0:T(8,128)S(1)}, u32[]{:S(2)}, u32[]{:S(2)}) %all-to-all-start.6) | async-done | bytes 786464 | tf_op jit(solution)/shard_map/all_to_all | solution.py:978
  383.7 3.3 finish.1
  (140 shorter events, 52.7 us)
Async XLA Ops:
  0.6 28.0 %copy-start = (s32[8,1,65536]{2,1,0:T(1,128)S(1)}, s32[8,1,65536]{2,1,0:T(1,128)}, u32[]{:S(2)}) copy-start(s32[8,1,65536]{2,1,0:T(1,128)} %param.18) | copy-start | bytes 6291460
  2.4 22.4 %copy-start.47 = (s32[33]{0:T(128)}, s32[33]{0:T(128)S(1)}, u32[]{:S(2)}) copy-start(s32[33]{0:T(128)S(1)} %convert_reduce_fusion.starts) | copy-start | bytes 400
  7.0 17.9 %all-to-all-start = ((s32[32,16,128]{2,1,0:T(8,128)}), s32[32,16,128]{2,1,0:T(8,128)S(1)}, u32[]{:S(2)}, u32[]{:S(2)}) async-start(s32[32,16,128]{2,1,0:T(8,128)} %slots.1), calls=%async_computation | async-start | bytes 524288 | tf_op jit(solution)/shard_map/all_to_all | solution.py:940
  22.6 6.7 %copy-start.57 = (s32[1,1024]{1,0:T(1,128)S(1)}, s32[1,1024]{1,0:T(1,128)}, u32[]{:S(2)}) copy-start(s32[1,1024]{1,0:T(1,128)} %param.19) | copy-start | bytes 12292
  22.6 6.7 %copy-start.58 = (s32[1,1024]{1,0:T(1,128)S(1)}, s32[1,1024]{1,0:T(1,128)}, u32[]{:S(2)}) copy-start(s32[1,1024]{1,0:T(1,128)} %param.20) | copy-start | bytes 12292
  24.9 41.2 %all-to-all-start.1 = ((f32[32,96,128]{2,1,0:T(8,128)}), f32[32,96,128]{2,1,0:T(8,128)}, u32[]{:S(2)}, u32[]{:S(2)}) async-start(f32[32,96,128]{2,1,0:T(8,128)} %copy-done.6), calls=%async_computation.1 | async-start | bytes 3145728 | tf_op jit(solution)/shard_map/all_to_all | solution.py:942
  28.6 83.8 %copy-start.27 = (f32[128,128]{1,0:T(8,128)S(1)}, f32[128,128]{1,0:T(8,128)}, u32[]{:S(2)}) copy-start(f32[128,128]{1,0:T(8,128)} %constant.47.clone.refs_1_) | copy-start | bytes 196612
  47.6 70.1 %copy-start.43 = (s32[64,128]{1,0:T(8,128)}, s32[64,128]{1,0:T(8,128)S(1)}, u32[]{:S(2)}) copy-start(s32[64,128]{1,0:T(8,128)S(1)} %get-tuple-element.87) | copy-start | bytes 98308
  48.3 69.4 %copy-start.49 = (s32[32]{0:T(128)}, s32[32]{0:T(128)S(1)}, u32[]{:S(2)}) copy-start(s32[32]{0:T(128)S(1)} %convert_reduce_fusion.1.refs_0_.counts) | copy-start | bytes 388
  117.7 30.1 %all-to-all-start.2 = ((f32[8,16,1536]{2,1,0:T(8,128)}), f32[8,16,1536]{2,1,0:T(8,128)S(1)}, u32[]{:S(2)}, u32[]{:S(2)}) async-start(f32[8,16,1536]{2,1,0:T(8,128)} %copy-done.19), calls=%async_computation.2 | async-start | bytes 1572864 | tf_op jit(solution)/shard_map/all_to_all | solution.py:897
  124.0 1.6 copy-start.2
  125.6 22.3 %copy-start.21 = (f32[128,256]{1,0:T(8,128)S(1)}, f32[128,256]{1,0:T(8,128)}, u32[]{:S(2)}) copy-start(f32[128,256]{1,0:T(8,128)} %constant.48.clone.refs_1_) | copy-start | bytes 393220
  146.5 1.4 copy-start.7
  155.1 28.6 %all-to-all-start.3 = ((f32[4,384,128]{2,1,0:T(8,128)}), f32[4,384,128]{2,1,0:T(8,128)S(1)}, u32[]{:S(2)}, u32[]{:S(2)}) async-start(f32[4,384,128]{2,1,0:T(8,128)} %bitcast.52), calls=%async_computation.3 | async-start | bytes 1572864 | tf_op jit(solution)/shard_map/all_to_all | solution.py:897
  160.1 66.8 %collective-permute-start = (f32[3072,128]{1,0:T(8,128)}, f32[3072,128]{1,0:T(8,128)}, u32[]{:S(2)}, u32[]{:S(2)}) collective-permute-start(f32[3072,128]{1,0:T(8,128)} %copy-done.15), channel_id=1, source_target_pairs={{0,28},{4,0},{8,4},{12,8},{16,12},{20,16},{24,20},{28,24},{1,29},{... | collective-permute-start | bytes 4718600 | tf_op jit(solution)/shard_map/ppermute | solution.py:30
  167.4 1.6 copy-start.3
  169.0 1.6 copy-start.8
  171.3 12.4 %copy-start.25 = (f32[256,128]{1,0:T(8,128)S(1)}, f32[256,128]{1,0:T(8,128)}, u32[]{:S(2)}) copy-start(f32[256,128]{1,0:T(8,128)} %constant.49.clone.refs_2_) | copy-start | bytes 393220
  181.7 1.4 copy-start.9
  193.8 22.3 %all-to-all-start.4 = ((f32[4,384,128]{2,1,0:T(8,128)}), f32[4,384,128]{2,1,0:T(8,128)S(1)}, u32[]{:S(2)}, u32[]{:S(2)}) async-start(f32[4,384,128]{2,1,0:T(8,128)} %bitcast.53), calls=%async_computation.4 | async-start | bytes 1572864 | tf_op jit(solution)/shard_map/all_to_all | solution.py:897
  197.3 1.6 copy-start.4
  198.9 1.6 copy-start.10
  214.6 1.4 copy-start.11
  222.0 80.3 %all-to-all-start.5 = ((f32[8,16,1536]{2,1,0:T(8,128)}), f32[8,16,1536]{2,1,0:T(8,128)S(1)}, u32[]{:S(2)}, u32[]{:S(2)}) async-start(f32[8,16,1536]{2,1,0:T(8,128)} %bitcast.51), calls=%async_computation.5 | async-start | bytes 1572864 | tf_op jit(solution)/shard_map/all_to_all | solution.py:897
  227.0 1.6 copy-start.5
  228.6 1.6 copy-start.12
  286.3 21.8 %collective-permute-start.1 = (f32[1536,128]{1,0:T(8,128)}, f32[1536,128]{1,0:T(8,128)}, u32[]{:S(2)}, u32[]{:S(2)}) collective-permute-start(f32[1536,128]{1,0:T(8,128)} %get-tuple-element.79), channel_id=1, source_target_pairs={{0,4},{4,8},{8,12},{12,16},{16,20},{20,24},{24,28},{28,0},{1,5},{5... | collective-permute-start | bytes 2359304 | tf_op jit(solution)/shard_map/ppermute | solution.py:30
  289.8 18.3 %copy-start.24 = (s32[32,16,128]{2,1,0:T(8,128)S(1)}, s32[32,16,128]{2,1,0:T(8,128)}, u32[]{:S(2)}) copy-start(s32[32,16,128]{2,1,0:T(8,128)} %copy-done.23) | copy-start | bytes 786436
  289.8 18.3 %copy-start.50 = (s32[32]{0:T(128)S(1)}, s32[32]{0:T(128)}, u32[]{:S(2)}) copy-start(s32[32]{0:T(128)} %copy-done.49) | copy-start | bytes 388
  308.0 1.6 copy-start.14
  353.9 28.8 %copy-start.48 = (s32[33]{0:T(128)S(1)}, s32[33]{0:T(128)}, u32[]{:S(2)}) copy-start(s32[33]{0:T(128)} %copy-done.47) | copy-start | bytes 400
  353.9 28.8 %all-to-all-start.6 = ((f32[32,48,128]{2,1,0:T(8,128)}), f32[32,48,128]{2,1,0:T(8,128)S(1)}, u32[]{:S(2)}, u32[]{:S(2)}) async-start(f32[32,48,128]{2,1,0:T(8,128)} %gather.1), calls=%async_computation.6 | async-start | bytes 1572864 | tf_op jit(solution)/shard_map/all_to_all | solution.py:978
  (38 other events, 30.0 us)

commit v6 on v5

--- a/solution.py
+++ b/solution.py
@@ -34,10 +34,42 @@
 PARTS = (25, 37, 52)
 
 SMEM_SPEC = pl.BlockSpec(memory_space=pltpu.SMEM)
+LIST_SPEC = pl.BlockSpec(memory_space=pltpu.SMEM)
 VMEM_SPEC = pl.BlockSpec(memory_space=pltpu.VMEM)
+MOVED_SPEC = pl.BlockSpec(memory_space=pltpu.VMEM)
 
 
 ANY_SPEC = pl.BlockSpec(memory_space=pl.ANY)
+
+
+def launch(kernel, *, out_shape, in_specs, out_specs, **options):
+    def block(spec, value):
+        shape = value.shape
+        return pl.BlockSpec(shape, lambda i: (0,) * len(shape)) if spec is VMEM_SPEC or spec is MOVED_SPEC else spec
+
+    def placed(spec, value):
+        return spec is VMEM_SPEC or spec is LIST_SPEC or (spec is ANY_SPEC and value.dtype == jnp.float32)
+
+    def run(*args):
+        several = isinstance(out_shape, tuple)
+        shapes = out_shape if several else (out_shape,)
+        outs = out_specs if several else (out_specs,)
+        found = tuple(block(s, v) for s, v in zip(outs, shapes))
+        kept = tuple(pltpu.HBM(v.shape, v.dtype) if s is VMEM_SPEC else v for s, v in zip(outs, shapes))
+        args = [
+            pltpu.with_memory_space_constraint(jnp.asarray(v), pltpu.HBM) if placed(s, v) else v
+            for s, v in zip(in_specs, args)
+        ]
+        return pl.pallas_call(
+            kernel,
+            out_shape=kept if several else kept[0],
+            grid=(1,),
+            in_specs=[block(s, v) for s, v in zip(in_specs, args)],
+            out_specs=found if several else found[0],
+            **options,
+        )(*args)
+
+    return run
 
 
 def ignoring(kernel, inputs, extra):
@@ -82,13 +114,13 @@
 def slots_call(starts, route, depth):
     rows = route.shape[0]
     peers = starts.shape[0] - 1
-    return pl.pallas_call(
+    return launch(
         functools.partial(slots_kernel, rows=rows, depth=depth),
         out_shape=jax.ShapeDtypeStruct((peers, depth, 128), jnp.int32),
         in_specs=[SMEM_SPEC, VMEM_SPEC],
         out_specs=VMEM_SPEC,
         scratch_shapes=[pltpu.VMEM((rows + depth + 8, 128), jnp.int32)],
-        compiler_params=pltpu.CompilerParams(vmem_limit_bytes=8 * 1024 * 1024),
+        compiler_params=pltpu.CompilerParams(vmem_limit_bytes=32 * 1024 * 1024),
         name="slots",
     )(starts, route)
 
@@ -142,13 +174,13 @@
     peers = starts.shape[0] - 1
     stride = rows + depth + 8
     stride += -stride % 8
-    return pl.pallas_call(
+    return launch(
         functools.partial(pack_kernel, rows=rows, depth=depth, stride=stride),
         out_shape=jax.ShapeDtypeStruct((peers, 6 * depth, 128), jnp.float32),
         in_specs=[SMEM_SPEC, VMEM_SPEC],
         out_specs=VMEM_SPEC,
         scratch_shapes=[pltpu.VMEM((6 * stride, 128), jnp.float32)],
-        compiler_params=pltpu.CompilerParams(vmem_limit_bytes=8 * 1024 * 1024),
+        compiler_params=pltpu.CompilerParams(vmem_limit_bytes=32 * 1024 * 1024),
         name="pack",
     )(starts, pos)
 
@@ -182,12 +214,12 @@
     peers, depth, _ = slots.shape
     lists = list_count(depth)
     one = jax.ShapeDtypeStruct((peers * depth // lists, 128), jnp.int32)
-    found = pl.pallas_call(
+    found = launch(
         functools.partial(nodes_kernel, depth=depth, spare=spare),
         out_shape=(jax.ShapeDtypeStruct(slots.shape, jnp.int32),) + (one,) * (2 * lists),
-        in_specs=[VMEM_SPEC] * 2,
+        in_specs=[MOVED_SPEC, VMEM_SPEC],
         out_specs=(VMEM_SPEC,) * (1 + 2 * lists),
-        compiler_params=pltpu.CompilerParams(vmem_limit_bytes=8 * 1024 * 1024),
+        compiler_params=pltpu.CompilerParams(vmem_limit_bytes=32 * 1024 * 1024),
         name="nodes",
     )(slots, perm)
     flat = [x.reshape(-1) for x in found[1:]]
@@ -264,7 +296,7 @@
 
 def scatter_call(nodes, counts, data, rp, after=()):
     depth = data.shape[1] // 6
-    return pl.pallas_call(
+    return launch(
         ignoring(
             functools.partial(scatter_kernel, depth=depth, rp=rp, lists=len(nodes)), 2 + len(nodes), len(after)
         ),
@@ -272,13 +304,13 @@
             jax.ShapeDtypeStruct((6 * rp, 128), jnp.float32),
             jax.ShapeDtypeStruct((8 * rp, 128), jnp.float32),
         ),
-        in_specs=[SMEM_SPEC, VMEM_SPEC] + [SMEM_SPEC] * len(nodes) + [ANY_SPEC] * len(after),
+        in_specs=[SMEM_SPEC, MOVED_SPEC] + [LIST_SPEC] * len(nodes) + [ANY_SPEC] * len(after),
         out_specs=(VMEM_SPEC,) * 2,
         scratch_shapes=[
             pltpu.VMEM((rp * 128 + 8, 128), jnp.float32),
             pltpu.VMEM((depth * 128, 128), jnp.float32),
         ],
-        compiler_params=pltpu.CompilerParams(vmem_limit_bytes=40 * 1024 * 1024),
+        compiler_params=pltpu.CompilerParams(vmem_limit_bytes=52 * 1024 * 1024),
         name="scatter",
     )(counts, data, *nodes, *after)
 
@@ -328,17 +360,17 @@
 def gather_call(rows, counts, nodes, sums, one, two):
     rp = one.shape[0] // 3
     peers, depth, _ = nodes.shape
-    return pl.pallas_call(
+    return launch(
         functools.partial(gather_kernel, depth=depth, rp=rp, lists=len(rows)),
         out_shape=jax.ShapeDtypeStruct((peers, 3 * depth, 128), jnp.float32),
-        in_specs=[SMEM_SPEC] + [VMEM_SPEC] * 4 + [SMEM_SPEC] * len(rows),
+        in_specs=[SMEM_SPEC] + [VMEM_SPEC] * 4 + [LIST_SPEC] * len(rows),
         out_specs=VMEM_SPEC,
         scratch_shapes=[
             pltpu.VMEM((rp * 4 + 8, 128), jnp.float32),
             pltpu.VMEM((depth * 128, 128), jnp.float32),
             pltpu.VMEM((128, 128), jnp.float32),
         ],
-        compiler_params=pltpu.CompilerParams(vmem_limit_bytes=8 * 1024 * 1024),
+        compiler_params=pltpu.CompilerParams(vmem_limit_bytes=32 * 1024 * 1024),
         name="gather",
     )(counts, nodes, sums, one, two, *rows)
 
@@ -379,13 +411,13 @@
     depth = data.shape[1] // 3
     stride = rows + depth + 8
     stride += -stride % 8
-    return pl.pallas_call(
+    return launch(
         functools.partial(finish_kernel, rows=rows, depth=depth, stride=stride),
         out_shape=(jax.ShapeDtypeStruct(pos.shape, jnp.float32),) * 2,
-        in_specs=[SMEM_SPEC] + [VMEM_SPEC] * 3,
+        in_specs=[SMEM_SPEC, MOVED_SPEC] + [VMEM_SPEC] * 2,
         out_specs=(VMEM_SPEC,) * 2,
         scratch_shapes=[pltpu.VMEM((3 * stride, 128), jnp.float32)],
-        compiler_params=pltpu.CompilerParams(vmem_limit_bytes=8 * 1024 * 1024),
+        compiler_params=pltpu.CompilerParams(vmem_limit_bytes=32 * 1024 * 1024),
         name="finish",
     )(starts, data, pos, noise)
 
@@ -426,18 +458,23 @@
         return own + inside, far + 1 - inside
 
     own, far = lax.fori_loop(0, count[0], step, (jnp.int32(0), jnp.int32(0)))
-    totals[0] = own
-    totals[1] = far
+    steps = first.shape[0]
+    totals[0] = 0
+    for n, part in enumerate(PARTS):
+        totals[n + 1] = jnp.minimum(own, steps * part // 128)
+    totals[len(PARTS) + 1] = own
+    totals[len(PARTS) + 2] = 0
+    totals[len(PARTS) + 3] = far
 
 
 def order_call(first, second, count, blocks):
     size = first.shape[0] + 8
-    return pl.pallas_call(
+    return launch(
         functools.partial(order_kernel, blocks=blocks),
-        out_shape=(jax.ShapeDtypeStruct((size,), jnp.int32),) * 2 + (jax.ShapeDtypeStruct((2,), jnp.int32),),
+        out_shape=(jax.ShapeDtypeStruct((size,), jnp.int32),) * 2 + (jax.ShapeDtypeStruct((len(PARTS) + 4,), jnp.int32),),
         in_specs=[SMEM_SPEC] * 3,
         out_specs=(SMEM_SPEC,) * 3,
-        compiler_params=pltpu.CompilerParams(vmem_limit_bytes=8 * 1024 * 1024),
+        compiler_params=pltpu.CompilerParams(vmem_limit_bytes=32 * 1024 * 1024),
         name="order",
     )(first, second, count)
 
@@ -450,15 +487,13 @@
             cells[pl.ds(at * 8 + c, 8, stride=8), :] = src_ref[pl.ds(pl.multiple_of(c * rp + at, 8), 8), :]
 
 
-def pair_kernel(pairs, bounds, cells_ref, near_in, *refs, rp, coef, unroll, beyond):
+def pair_kernel(pairs, bounds, cells_ref, *refs, rp, coef, unroll, beyond, part, fresh):
+    if not fresh:
+        near_in, *refs = refs
     if beyond:
-        other_ref, far_in, near_ref, token, far_ref, other_cells, far_sums = refs
+        other_ref, near_ref, token, far_ref, other_cells, far_sums = refs
         fill_cells(other_ref, other_cells, rp)
-        for c in range(3):
-            @pl.loop(0, rp // 8)
-            def _(i):
-                at = pl.ds(pl.multiple_of(c * rp + i * 8, 8), 8)
-                far_sums[pl.ds(i * 64 + c, 8, stride=8), :] = far_in[at, :]
+        far_sums[...] = jnp.zeros(far_sums.shape, jnp.float32)
     else:
         near_ref, token = refs
         other_cells, far_sums = cells_ref, near_ref
@@ -466,7 +501,7 @@
     sub = lax.broadcasted_iota(jnp.int32, (8, 128), 0)
     left = lane < 64
     unturn = (lane + sub) & 127
-    near_ref[...] = near_in[...]
+    near_ref[...] = jnp.zeros(near_ref.shape, jnp.float32) if fresh else near_in[...]
     token[...] = jnp.zeros((8, 128), jnp.float32)
 
     def row(k):
@@ -512,8 +547,8 @@
         far_vel = far_vel + pltpu.roll(far_vel, 64, 1)
         return near_vel, far_vel
 
-    low = bounds[0]
-    high = bounds[1]
+    low = bounds[part]
+    high = bounds[part + 1]
 
     def turn(i, carry):
         found = []
@@ -540,28 +575,31 @@
                 far_ref[at, :] = far_sums[pl.ds(i * 64 + c, 8, stride=8), :]
 
 
-def pair_call(pairs, bounds, cells, near, beside=None, far=None, after=(), coef=ERFCX_COEF, unroll=8):
+def pair_call(pairs, bounds, part, cells, near=None, beside=None, after=(), coef=ERFCX_COEF, unroll=8):
     rp = cells.shape[0] // 8
     beyond = beside is not None
-    extra = [beside, far] if beyond else []
+    fresh = near is None
+    extra = [cells] + ([] if fresh else [near]) + ([beside] if beyond else [])
     out = [jax.ShapeDtypeStruct((8 * rp, 128), jnp.float32), jax.ShapeDtypeStruct((8, 128), jnp.float32)]
     scratch = []
     if beyond:
         out.append(jax.ShapeDtypeStruct((3 * rp, 128), jnp.float32))
         scratch = [pltpu.VMEM((8 * rp, 128), jnp.float32)] * 2
-    return pl.pallas_call(
+    return launch(
         ignoring(
-            functools.partial(pair_kernel, rp=rp, coef=coef, unroll=unroll, beyond=beyond),
-            4 + len(extra),
+            functools.partial(
+                pair_kernel, rp=rp, coef=coef, unroll=unroll, beyond=beyond, part=part, fresh=fresh
+            ),
+            2 + len(extra),
             len(after),
         ),
         out_shape=tuple(out),
-        in_specs=[SMEM_SPEC] * 2 + [VMEM_SPEC] * (2 + len(extra)) + [ANY_SPEC] * len(after),
+        in_specs=[SMEM_SPEC] * 2 + [VMEM_SPEC] * (len(extra) - beyond) + [MOVED_SPEC] * beyond + [ANY_SPEC] * len(after),
         out_specs=(VMEM_SPEC,) * len(out),
         scratch_shapes=scratch,
-        compiler_params=pltpu.CompilerParams(vmem_limit_bytes=8 * 1024 * 1024),
+        compiler_params=pltpu.CompilerParams(vmem_limit_bytes=32 * 1024 * 1024),
         name="beyond" if beyond else "within",
-    )(pairs, bounds, cells, near, *extra, *after)
+    )(pairs, bounds, *extra, *after)
 
 
 def signed_wave(grid_index):
@@ -882,28 +920,24 @@
     f32 = jnp.float32
 
     def run(name, kernel, shape, args, scratch, specs=None, after=(), **sizes):
-        return pl.pallas_call(
+        return launch(
             marking(ignoring(functools.partial(kernel, **sizes), len(args), len(after)), len(args) + len(after)),
             out_shape=(jax.ShapeDtypeStruct(shape, f32), jax.ShapeDtypeStruct((8, 128), f32)),
-            in_specs=(specs or [VMEM_SPEC] * len(args)) + [ANY_SPEC] * len(after),
+            in_specs=(specs or [MOVED_SPEC] + [VMEM_SPEC] * (len(args) - 1)) + [ANY_SPEC] * len(after),
             out_specs=(VMEM_SPEC,) * 2,
             scratch_shapes=[pltpu.VMEM(scratch, f32)],
-            compiler_params=pltpu.CompilerParams(vmem_limit_bytes=8 * 1024 * 1024),
+            compiler_params=pltpu.CompilerParams(vmem_limit_bytes=32 * 1024 * 1024),
             name=name,
-            grid=(1,),
         )(*args, *after)
 
     def swap(value, axis):
         return lax.all_to_all(value, axis, split_axis=0, concat_axis=0, tiled=True)
-
-    def full(shape):
-        return pl.BlockSpec(shape, lambda i: (0,) * len(shape))
 
     force = pl.BlockSpec((rows, 128), lambda i: (1, 0))
     lanes = 6 * wide * share
     ids = jnp.stack([lax.axis_index("gx"), lax.axis_index("gy")]).astype(jnp.int32)
-    value, token = run("depth", depth_kernel, (n_gx, tall, lanes), (grid_data, tables["ahead"]), (rows, 128),
-                [force, full((G, 128))], n_gx=n_gx, tall=tall, wide=wide)
+    value, token = run("depth", depth_kernel, (n_gx, tall, lanes), (pltpu.with_memory_space_constraint(grid_data, pltpu.HBM), tables["ahead"]), (rows, 128),
+                [force, VMEM_SPEC], n_gx=n_gx, tall=tall, wide=wide)
     after = fill(0, token)
     value = swap(value, "gx").reshape(G, lanes)
     value, token = run("first", first_kernel, (n_gy, 6 * views, wide, 128), (value, tables["first"]), (rows, 128),
@@ -912,7 +946,7 @@
     value = swap(value.reshape(n_gy, 6 * views * wide, 128), "gy").reshape(n_gy, 6 * views, wide, 128)
     args = (ids, value, tables["second"], tables["across"], tables["deep"], tables["down"])
     value, token = run("second", second_kernel, (n_gy, 6 * views, wide, 128), args, (8, 128),
-                [SMEM_SPEC] + [VMEM_SPEC] * 5, after, n_gy=n_gy, views=views, wide=wide)
+                [SMEM_SPEC, MOVED_SPEC] + [VMEM_SPEC] * 4, after, n_gy=n_gy, views=views, wide=wide)
     after = fill(2, token)
     value = swap(value.reshape(n_gy, 6 * views * wide, 128), "gy").reshape(n_gy, 6 * views, wide, 128)
     value, token = run("first_back", first_back_kernel, (G, lanes), (value, tables["first_back"]), (rows, 128),
@@ -946,12 +980,10 @@
     own_pairs, far_pairs, totals = order_call(pair_first[0], pair_second[0], pair_count, slots // CELL)
     grid_data, cells = scatter_call(node_lists, counts, data, rp, after=(totals,))
 
-    steps = pair_first.shape[1]
-    marks = [jnp.int32(0)] + [jnp.minimum(totals[0], steps * part // 128) for part in PARTS] + [totals[0]]
-    state = {"sums": jnp.zeros_like(cells)}
+    state = {"sums": None}
 
     def within(n, after):
-        state["sums"], token = pair_call(own_pairs, jnp.stack(marks[n : n + 2]), cells, state["sums"], after=after)
+        state["sums"], token = pair_call(own_pairs, totals, n, cells, state["sums"], after=after)
         return token
 
     def fill(n, token):
@@ -960,10 +992,8 @@
                 ready, _ = lax.optimization_barrier((grid_data, token))
                 state["beside"] = shifted(ready, "gx", -1)
             return (within(n, (token,)),)
-        bounds = jnp.stack([marks[0], totals[1]])
-        none = jnp.zeros((3 * rp, 128), jnp.float32)
         state["sums"], _, far = pair_call(
-            far_pairs, bounds, cells, state["sums"], state["beside"], none, after=(token,)
+            far_pairs, totals, len(PARTS) + 2, cells, state["sums"], state["beside"], after=(token,)
         )
         state["far"] = shifted(far, "gx", 1)
         return (within(3, ()),)

time: 390 us -> 365 us (0.936)
  local copies, waits for them, and re-layouts: 51.1 us -> 5.96 us
  Pallas kernels: 243 us -> 274 us
  starting transfers between devices: 45.8 us -> 34 us
  waiting for transfers between devices: 40.3 us -> 46.1 us
    unnamed x126 -> x10, local copies, waits for them, and re-layouts: 50.3 us -> 2.61 us
    pallas_call x17, Pallas kernels: 243 us -> 274 us  [run(): pl.pallas_call(kernel, out_shape=kept if several else kept[0], grid=(1,),...]
    all_to_all x1, starting transfers between devices: 8.22 us -> 2.62 us  [shards(): swap(gather_call(row_lists, counts, nodes, state['sums'], wave_vel, state...]
    all_to_all x4, starting transfers between devices: 18.3 us -> 14.1 us  [swap(): return lax.all_to_all(value, axis, split_axis=0, concat_axis=0, tiled=True)]
  transfers between devices with their start and end apart: 9 -> 9, of which waited for: 4 -> 4; matrix products, arithmetic and copies ran while one was open for 2% -> 1% of each run, Pallas kernels for 37% -> 45%
where the time goes in v6:
time: 365 us; the launch traced here: 364 us
  Pallas kernels  274 us (75%)
  waiting for transfers between devices  46.1 us (13%)
  starting transfers between devices  34 us (9%)
  local copies, waits for them, and re-layouts  5.96 us (2%)
    pallas_call x17, Pallas kernels, run(): pl.pallas_call(kernel, out_shape=kept if several else kept[0], grid=(1,),...  274 us
    all_to_all x1, waiting for transfers between devices, shards(): data = swap(pack_call(starts, places, depth))  20.1 us
    all_to_all x1, waiting for transfers between devices, shards(): swap(gather_call(row_lists, counts, nodes, state['sums'], wave_vel, state...  19.8 us
    all_to_all x4, starting transfers between devices, swap(): return lax.all_to_all(value, axis, split_axis=0, concat_axis=0, tiled=True)  14.1 us
    all_to_all x1, starting transfers between devices, shards(): taken = swap(slots_call(starts, route.reshape(rows, 128), depth))  7.33 us
  transfers between devices with their start and end apart: 9, of which 4 were waited for; matrix products, arithmetic and copies ran while one was open for 1% of the time, Pallas kernels for 45%

profile of v6, /device:TPU:0, one launch (start us, length us, event | category | flops | bytes accessed | tf_op | source)
XLA Modules:
  0.0 364.2 jit_solution(1928161933995978355)
XLA Ops:
  0.7 1.8 convert_reduce_fusion.starts
  2.4 4.0 %slots.1 = s32[32,16,128]{2,1,0:T(8,128)} custom-call(s32[33]{0:T(128)S(1)} %convert_reduce_fusion.starts, s32[256,128]{1,0:T(8,128)} %bitcast.56), custom_call_target="tpu_custom_call" | custom-call | tf_op jit(solution)/shard_map/slots/pallas_call | solution.py:63
  6.4 7.3 %all-to-all-start = ((s32[32,16,128]{2,1,0:T(8,128)}), s32[32,16,128]{2,1,0:T(8,128)S(1)}, u32[]{:S(2)}, u32[]{:S(2)}) async-start(s32[32,16,128]{2,1,0:T(8,128)} %slots.1), calls=%async_computation | async-start | bytes 524288 | tf_op jit(solution)/shard_map/all_to_all | solution.py:974
  13.8 1.8 copy.26
  15.6 7.8 %pack.1 = f32[32,96,128]{2,1,0:T(8,128)} custom-call(s32[33]{0:T(128)S(1)} %convert_reduce_fusion.starts, f32[3,256,128]{2,1,0:T(8,128)} %bitcast.47), custom_call_target="tpu_custom_call" | custom-call | tf_op jit(solution)/shard_map/pack/pallas_call | solution.py:63
  23.3 1.0 all-to-all-done.slots_ref
  24.3 5.0 %all-to-all-start.1 = ((f32[32,96,128]{2,1,0:T(8,128)}), f32[32,96,128]{2,1,0:T(8,128)}, u32[]{:S(2)}, u32[]{:S(2)}) async-start(f32[32,96,128]{2,1,0:T(8,128)} %pack.1), calls=%async_computation.1 | async-start | bytes 3145728 | tf_op jit(solution)/shard_map/all_to_all | solution.py:976
  30.7 9.5 %order.1 = (s32[1032]{0:T(1024)S(1)}, s32[1032]{0:T(1024)S(1)}, s32[7]{0:T(128)S(1)}) custom-call(s32[1024]{0:T(1024)S(1)} %bitcast.45, s32[1024]{0:T(1024)S(1)} %bitcast.46, s32[1]{0:T(128)S(6)} %copy.27.count), custom_call_target="tpu_custom_call" | custom-call | tf_op jit(solution)/shard_map/order/pallas_call | solution.py:63
  40.2 5.8 %nodes.1 = (s32[32,16,128]{2,1,0:T(8,128)}, s32[64,128]{1,0:T(8,128)}, s32[64,128]{1,0:T(8,128)}, s32[64,128]{1,0:T(8,128)}, s32[64,128]{1,0:T(8,128)}, /*index=...) custom-call(s32[32,16,128]{2,1,0:T(8,128)S(1)} %all-to-all-done.slot, ...), custom_call_target="tpu_custom_call" | custom-call | tf_op jit(solution)/shard_map/nodes/pallas_call | solution.py:63
  46.7 20.1 %all-to-all-done.1.refs_1_ = f32[32,96,128]{2,1,0:T(8,128)} async-done(((f32[32,96,128]{2,1,0:T(8,128)}), f32[32,96,128]{2,1,0:T(8,128)}, u32[]{:S(2)}, u32[]{:S(2)}) %all-to-all-start.1) | async-done | bytes 1572896 | tf_op jit(solution)/shard_map/all_to_all | solution.py:976
  66.7 48.7 %scatter.1 = (f32[3072,128]{1,0:T(8,128)}, f32[4096,128]{1,0:T(8,128)}) custom-call(s32[32]{0:T(128)S(1)} %convert_reduce_fusion.1.refs_0_.counts, f32[32,96,128]{2,1,0:T(8,128)} %all-to-all-done.1.refs_1_, s32[8192]{0:T(1024)} %bitcast.67, s32[8192]{0:T(1024)} %bitcast.68, s32[8192]{0:T(1024)} %bitcast.69, s32[8192]{0:T(1024)} %bitcast.70, s32[8192]{0:T(1024)} %bitcast.71, ...), custom_call_target="tpu_custom_call" | custom-call | tf_op jit(solution)/shard_map/scatter/pallas_call | solution.py:63
  115.4 5.3 %depth.1 = (f32[8,16,1536]{2,1,0:T(8,128)}, f32[8,128]{1,0:T(8,128)}) custom-call(f32[3072,128]{1,0:T(8,128)} %get-tuple-element.70.refs_0_, f32[128,128]{1,0:T(8,128)} %constant.33.clone.refs_1_), custom_call_target="tpu_custom_call" | custom-call | tf_op jit(solution)/shard_map/depth/pallas_call | solution.py:63
  120.7 3.5 all-to-all-start.2
  124.3 23.2 %within.4 = (f32[4096,128]{1,0:T(8,128)}, f32[8,128]{1,0:T(8,128)}) custom-call(s32[1032]{0:T(1024)S(1)} %get-tuple-element.47.refs_0_, s32[7]{0:T(128)S(1)} %get-tuple-element.48.refs_10_.refs_1_, f32[4096,128]{1,0:T(8,128)} %get-tuple-element.57.refs_2_, f32[8,128]{1,0:T(8,128)} %get-tuple-element.60.refs_3_), custom_call_target="tpu_custom_call" | custom-call | tf_op jit(solution)/shard_map/within/pallas_call | solution.py:63
  147.5 7.4 %first.1 = (f32[4,12,32,128]{3,2,1,0:T(8,128)}, f32[8,128]{1,0:T(8,128)}) custom-call(f32[128,1536]{1,0:T(8,128)S(1)} %bitcast.43, f32[128,256]{1,0:T(8,128)} %constant.34.clone.refs_1_, f32[8,128]{1,0:T(8,128)} %get-tuple-element.63.refs_2_), custom_call_target="tpu_custom_call" | custom-call | tf_op jit(solution)/shard_map/first/pallas_call | solution.py:63
  155.0 3.5 all-to-all-start.3
  158.5 4.7 %collective-permute-start = (f32[3072,128]{1,0:T(8,128)}, f32[3072,128]{1,0:T(8,128)}, u32[]{:S(2)}, u32[]{:S(2)}) collective-permute-start(f32[3072,128]{1,0:T(8,128)} %get-tuple-element.70.refs_0_), channel_id=1, source_target_pairs={{0,28},{4,0},{8,4},{12,8},{16,12},{20,16},{24,20},{28,24},{1,29},{... | collective-permute-start | bytes 4718600 | tf_op jit(solution)/shard_map/ppermute | solution.py:30
  163.2 13.4 %within.5 = (f32[4096,128]{1,0:T(8,128)}, f32[8,128]{1,0:T(8,128)}) custom-call(s32[1032]{0:T(1024)S(1)} %get-tuple-element.47.refs_0_, s32[7]{0:T(128)S(1)} %get-tuple-element.48.refs_10_.refs_1_, f32[4096,128]{1,0:T(8,128)} %get-tuple-element.57.refs_2_, f32[4096,128]{1,0:T(8,128)} %get-tuple-element.61.refs_3_, f32[8,128]{1,0:T(8,128)} %get-tuple-element.64.refs_4_), custom_call_target="tpu_custom_call" | custom-call | tf_op jit(solution)/shard_map/within/pallas_call | solution.py:63
  176.7 6.1 %second.1 = (f32[4,12,32,128]{3,2,1,0:T(8,128)}, f32[8,128]{1,0:T(8,128)}) custom-call(s32[2]{0:T(128)S(1)} %pad_add_fusion.refs_0_, f32[4,12,32,128]{3,2,1,0:T(8,128)S(1)} %bitcast.44, f32[256,128]{1,0:T(8,128)} %constant.35.clone.refs_2_, f32[4,8,128]{2,1,0:T(8,128)} %constant.36.clone.refs_3_, f32[8,8,128]{2,1,0:T(8,128)} %constant.37.clone.refs_4_, ...), custom_call_target="tpu_custom_call" | custom-call | tf_op jit(solution)/shard_map/second/pallas_call | solution.py:63
  182.8 3.5 all-to-all-start.4
  186.3 15.8 %within.6 = (f32[4096,128]{1,0:T(8,128)}, f32[8,128]{1,0:T(8,128)}) custom-call(s32[1032]{0:T(1024)S(1)} %get-tuple-element.47.refs_0_, s32[7]{0:T(128)S(1)} %get-tuple-element.48.refs_10_.refs_1_, f32[4096,128]{1,0:T(8,128)} %get-tuple-element.57.refs_2_, f32[4096,128]{1,0:T(8,128)} %get-tuple-element.65.refs_3_, f32[8,128]{1,0:T(8,128)} %get-tuple-element.68.refs_4_), custom_call_target="tpu_custom_call" | custom-call | tf_op jit(solution)/shard_map/within/pallas_call | solution.py:63
  202.1 6.8 %first_back.1 = (f32[128,1536]{1,0:T(8,128)}, f32[8,128]{1,0:T(8,128)}) custom-call(f32[4,12,32,128]{3,2,1,0:T(8,128)S(1)} %bitcast.42, f32[128,256]{1,0:T(8,128)} %constant.34.clone.refs_1_, f32[8,128]{1,0:T(8,128)} %get-tuple-element.72.refs_2_), custom_call_target="tpu_custom_call" | custom-call | tf_op jit(solution)/shard_map/first_back/pallas_call | solution.py:63
  208.8 3.5 all-to-all-start.5
  212.4 58.2 %beyond.1 = (f32[4096,128]{1,0:T(8,128)}, f32[8,128]{1,0:T(8,128)}, f32[1536,128]{1,0:T(8,128)}) custom-call(s32[1032]{0:T(1024)S(1)} %get-tuple-element.58.refs_0_, s32[7]{0:T(128)S(1)} %get-tuple-element.48.refs_10_.refs_1_, f32[4096,128]{1,0:T(8,128)} %get-tuple-element.57.refs_2_, f32[4096,128]{1,0:T(8,128)} %get-tuple-element.69.refs_3_, ...), custom_call_target="tpu_custom_call" | custom-call | tf_op jit(solution)/shard_map/beyond/pallas_call | solution.py:63
  271.0 12.5 %within.7 = (f32[4096,128]{1,0:T(8,128)}, f32[8,128]{1,0:T(8,128)}) custom-call(s32[1032]{0:T(1024)S(1)} %get-tuple-element.47.refs_0_, s32[7]{0:T(128)S(1)} %get-tuple-element.48.refs_10_.refs_1_, f32[4096,128]{1,0:T(8,128)} %get-tuple-element.57.refs_2_, f32[4096,128]{1,0:T(8,128)} %get-tuple-element.74.refs_3_), custom_call_target="tpu_custom_call" | custom-call | tf_op jit(solution)/shard_map/within/pallas_call | solution.py:63
  283.5 5.1 %depth_back.1 = (f32[1536,128]{1,0:T(8,128)}, f32[8,128]{1,0:T(8,128)}) custom-call(f32[8,16,1536]{2,1,0:T(8,128)S(1)} %all-to-all-done.5.refs_0_, f32[128,128]{1,0:T(8,128)} %constant.39.clone.refs_1_, f32[8,128]{1,0:T(8,128)} %get-tuple-element.77.refs_2_), custom_call_target="tpu_custom_call" | custom-call | tf_op jit(solution)/shard_map/depth_back/pallas_call | solution.py:63
  288.6 5.2 %collective-permute-done.1.two_ref = f32[1536,128]{1,0:T(8,128)} collective-permute-done((f32[1536,128]{1,0:T(8,128)}, f32[1536,128]{1,0:T(8,128)}, u32[]{:S(2)}, u32[]{:S(2)}) %collective-permute-start.1) | collective-permute-done | bytes 786464 | tf_op jit(solution)/shard_map/ppermute | solution.py:30
  293.8 39.9 %gather.1 = f32[32,48,128]{2,1,0:T(8,128)} custom-call(s32[32]{0:T(128)S(1)} %convert_reduce_fusion.1.refs_0_.counts, s32[32,16,128]{2,1,0:T(8,128)} %get-tuple-element.46.node_ref, f32[4096,128]{1,0:T(8,128)} %get-tuple-element.75.sums_ref, f32[1536,128]{1,0:T(8,128)} %get-tuple-element.78.one_ref, f32[1536,128]{1,0:T(8,128)} %collective-permute-done.1.two_ref, ...), custom_call_target="tpu_custom_call" | custom-call | tf_op jit(solution)/shard_map/gather/pallas_call | solution.py:63
  333.6 2.6 all-to-all-start.6
  337.1 19.8 %all-to-all-done.6.in_ref = f32[32,48,128]{2,1,0:T(8,128)S(1)} async-done(((f32[32,48,128]{2,1,0:T(8,128)}), f32[32,48,128]{2,1,0:T(8,128)S(1)}, u32[]{:S(2)}, u32[]{:S(2)}) %all-to-all-start.6) | async-done | bytes 786464 | tf_op jit(solution)/shard_map/all_to_all | solution.py:1008
  356.8 4.8 %finish.1 = (f32[3,256,128]{2,1,0:T(8,128)}, f32[3,256,128]{2,1,0:T(8,128)}) custom-call(s32[33]{0:T(128)S(1)} %convert_reduce_fusion.starts, f32[32,48,128]{2,1,0:T(8,128)S(1)} %all-to-all-done.6.in_ref, f32[3,256,128]{2,1,0:T(8,128)} %bitcast.48, f32[3,256,128]{2,1,0:T(8,128)} %bitcast.49), custom_call_target="tpu_custom_call" | custom-call | tf_op jit(solution)/shard_map/finish/pallas_call | solution.py:63
  361.6 2.6 copy_bitcast_fusion
  (19 shorter events, 2.6 us)
Async XLA Ops:
  0.6 28.7 %copy-start = (s32[8,1,65536]{2,1,0:T(1,128)S(1)}, s32[8,1,65536]{2,1,0:T(1,128)}, u32[]{:S(2)}) copy-start(s32[8,1,65536]{2,1,0:T(1,128)} %param.18) | copy-start | bytes 6291460
  6.4 17.9 %all-to-all-start = ((s32[32,16,128]{2,1,0:T(8,128)}), s32[32,16,128]{2,1,0:T(8,128)S(1)}, u32[]{:S(2)}, u32[]{:S(2)}) async-start(s32[32,16,128]{2,1,0:T(8,128)} %slots.1), calls=%async_computation | async-start | bytes 524288 | tf_op jit(solution)/shard_map/all_to_all | solution.py:974
  23.3 7.4 %copy-start.1 = (s32[1,1024]{1,0:T(1,128)S(1)}, s32[1,1024]{1,0:T(1,128)}, u32[]{:S(2)}) copy-start(s32[1,1024]{1,0:T(1,128)} %param.19) | copy-start | bytes 12292
  23.3 7.4 %copy-start.2 = (s32[1,1024]{1,0:T(1,128)S(1)}, s32[1,1024]{1,0:T(1,128)}, u32[]{:S(2)}) copy-start(s32[1,1024]{1,0:T(1,128)} %param.20) | copy-start | bytes 12292
  24.3 42.4 %all-to-all-start.1 = ((f32[32,96,128]{2,1,0:T(8,128)}), f32[32,96,128]{2,1,0:T(8,128)}, u32[]{:S(2)}, u32[]{:S(2)}) async-start(f32[32,96,128]{2,1,0:T(8,128)} %pack.1), calls=%async_computation.1 | async-start | bytes 3145728 | tf_op jit(solution)/shard_map/all_to_all | solution.py:976
  120.7 26.8 %all-to-all-start.2 = ((f32[8,16,1536]{2,1,0:T(8,128)}), f32[8,16,1536]{2,1,0:T(8,128)S(1)}, u32[]{:S(2)}, u32[]{:S(2)}) async-start(f32[8,16,1536]{2,1,0:T(8,128)} %get-tuple-element.62), calls=%async_computation.2 | async-start | bytes 1572864 | tf_op jit(solution)/shard_map/all_to_all | solution.py:934
  155.0 21.7 %all-to-all-start.3 = ((f32[4,384,128]{2,1,0:T(8,128)}), f32[4,384,128]{2,1,0:T(8,128)S(1)}, u32[]{:S(2)}, u32[]{:S(2)}) async-start(f32[4,384,128]{2,1,0:T(8,128)} %bitcast.52), calls=%async_computation.3 | async-start | bytes 1572864 | tf_op jit(solution)/shard_map/all_to_all | solution.py:934
  158.5 53.9 %collective-permute-start = (f32[3072,128]{1,0:T(8,128)}, f32[3072,128]{1,0:T(8,128)}, u32[]{:S(2)}, u32[]{:S(2)}) collective-permute-start(f32[3072,128]{1,0:T(8,128)} %get-tuple-element.70.refs_0_), channel_id=1, source_target_pairs={{0,28},{4,0},{8,4},{12,8},{16,12},{20,16},{24,20},{28,24},{1,29},{... | collective-permute-start | bytes 4718600 | tf_op jit(solution)/shard_map/ppermute | solution.py:30
  182.8 19.3 %all-to-all-start.4 = ((f32[4,384,128]{2,1,0:T(8,128)}), f32[4,384,128]{2,1,0:T(8,128)S(1)}, u32[]{:S(2)}, u32[]{:S(2)}) async-start(f32[4,384,128]{2,1,0:T(8,128)} %bitcast.53), calls=%async_computation.4 | async-start | bytes 1572864 | tf_op jit(solution)/shard_map/all_to_all | solution.py:934
  208.8 74.7 %all-to-all-start.5 = ((f32[8,16,1536]{2,1,0:T(8,128)}), f32[8,16,1536]{2,1,0:T(8,128)S(1)}, u32[]{:S(2)}, u32[]{:S(2)}) async-start(f32[8,16,1536]{2,1,0:T(8,128)} %bitcast.51), calls=%async_computation.5 | async-start | bytes 1572864 | tf_op jit(solution)/shard_map/all_to_all | solution.py:934
  270.6 23.1 %collective-permute-start.1 = (f32[1536,128]{1,0:T(8,128)}, f32[1536,128]{1,0:T(8,128)}, u32[]{:S(2)}, u32[]{:S(2)}) collective-permute-start(f32[1536,128]{1,0:T(8,128)} %get-tuple-element.79), channel_id=1, source_target_pairs={{0,4},{4,8},{8,12},{12,16},{16,20},{20,24},{24,28},{28,0},{1,5},{5... | collective-permute-start | bytes 2359304 | tf_op jit(solution)/shard_map/ppermute | solution.py:30
  293.8 42.5 %copy-start.3 = (f32[3,32768]{1,0:T(4,128)S(1)}, f32[3,32768]{1,0:T(4,128)}, u32[]{:S(2)}) copy-start(f32[3,32768]{1,0:T(4,128)} %param.16) | copy-start | bytes 1179652
  333.6 23.2 %all-to-all-start.6 = ((f32[32,48,128]{2,1,0:T(8,128)}), f32[32,48,128]{2,1,0:T(8,128)S(1)}, u32[]{:S(2)}, u32[]{:S(2)}) async-start(f32[32,48,128]{2,1,0:T(8,128)} %gather.1), calls=%async_computation.6 | async-start | bytes 1572864 | tf_op jit(solution)/shard_map/all_to_all | solution.py:1008

commit v7 on v6

--- a/solution.py
+++ b/solution.py
@@ -34,7 +34,7 @@
 PARTS = (25, 37, 52)
 
 SMEM_SPEC = pl.BlockSpec(memory_space=pltpu.SMEM)
-LIST_SPEC = pl.BlockSpec(memory_space=pltpu.SMEM)
+LIST_SPEC = pl.BlockSpec(memory_space=pl.ANY)
 VMEM_SPEC = pl.BlockSpec(memory_space=pltpu.VMEM)
 MOVED_SPEC = pl.BlockSpec(memory_space=pltpu.VMEM)
 
@@ -248,13 +248,28 @@
     lax.fori_loop(0, lax.div(count + (whole - 1), jnp.int32(whole)), part, 0)
 
 
+def fetching(lists, kept, arrived):
+    copies = [pltpu.make_async_copy(a, b, arrived.at[k]) for k, (a, b) in enumerate(zip(lists, kept))]
+    for copy in copies:
+        copy.start()
+    return copies
+
+
+def list_scratch(lists):
+    kept = [pltpu.SMEM(x.shape, jnp.int32) for x in lists]
+    return kept + [pltpu.SemaphoreType.DMA((len(lists),))]
+
+
 def scatter_kernel(counts, in_ref, *refs, depth, rp, lists):
-    nodes = refs[:lists]
-    out_ref, cells_ref, table, rows_ref = refs[lists:]
+    out_ref, cells_ref, table, rows_ref, *nodes, arrived = refs[lists:]
+    copies = fetching(refs[:lists], nodes, arrived)
 
     @pl.loop(0, rp)
     def _(k):
         table[pl.ds(pl.multiple_of(k * 128, 128), 128), :] = jnp.zeros((128, 128), jnp.float32)
+
+    for copy in copies:
+        copy.wait()
 
     together = 4 if depth % 4 == 0 else 1
 
@@ -309,15 +324,16 @@
         scratch_shapes=[
             pltpu.VMEM((rp * 128 + 8, 128), jnp.float32),
             pltpu.VMEM((depth * 128, 128), jnp.float32),
-        ],
+        ]
+        + list_scratch(nodes),
         compiler_params=pltpu.CompilerParams(vmem_limit_bytes=52 * 1024 * 1024),
         name="scatter",
     )(counts, data, *nodes, *after)
 
 
 def gather_kernel(counts, node_ref, sums_ref, one_ref, two_ref, *refs, depth, rp, lists):
-    rows = refs[:lists]
-    out_ref, table, found, comb = refs[lists:]
+    out_ref, table, found, comb, *rows, arrived = refs[lists:]
+    copies = fetching(refs[:lists], rows, arrived)
     comb[...] = jnp.zeros((128, 128), jnp.float32)
 
     @pl.loop(0, rp // 32)
@@ -331,6 +347,8 @@
             comb[8 * i : 8 * i + 8, :] = comb[8 * i : 8 * i + 8, :] + both
         table[pl.ds(pl.multiple_of(g * 128, 128), 128), :] = jnp.transpose(comb[...])
 
+    for copy in copies:
+        copy.wait()
     together = 4 if depth % 4 == 0 else 1
 
     @pl.loop(0, out_ref.shape[0])
@@ -369,7 +387,8 @@
             pltpu.VMEM((rp * 4 + 8, 128), jnp.float32),
             pltpu.VMEM((depth * 128, 128), jnp.float32),
             pltpu.VMEM((128, 128), jnp.float32),
-        ],
+        ]
+        + list_scratch(rows),
         compiler_params=pltpu.CompilerParams(vmem_limit_bytes=32 * 1024 * 1024),
         name="gather",
     )(counts, nodes, sums, one, two, *rows)

time: 365 us -> 369 us (1.011)
  starting transfers between devices: 34 us -> 39.7 us
  waiting for transfers between devices: 46.1 us -> 40.9 us
  Pallas kernels: 274 us -> 279 us
    ppermute x2, waiting for transfers between devices: 5.21 us -> 0.01 us  [shifted(): lax.ppermute(value, axis, [(i, (i + by) % devices) for i in range(devices)])]
    pallas_call x17, Pallas kernels: 274 us -> 279 us  [run(): pl.pallas_call(kernel, out_shape=kept if several else kept[0], grid=(1,),...]
    ppermute x2, starting transfers between devices: 5.04 us -> 9.04 us  [shifted(): lax.ppermute(value, axis, [(i, (i + by) % devices) for i in range(devices)])]
  transfers between devices with their start and end apart: 9 -> 9, of which waited for: 4 -> 3; matrix products, arithmetic and copies ran while one was open for 1% -> 1% of each run, Pallas kernels for 45% -> 44%
where the time goes in v7:
time: 369 us; the launch traced here: 370 us
  Pallas kernels  279 us (76%)
  waiting for transfers between devices  40.9 us (11%)
  starting transfers between devices  39.7 us (11%)
  local copies, waits for them, and re-layouts  5.96 us (2%)
    pallas_call x17, Pallas kernels, run(): pl.pallas_call(kernel, out_shape=kept if several else kept[0], grid=(1,),...  279 us
    all_to_all x1, waiting for transfers between devices, shards(): data = swap(pack_call(starts, places, depth))  20.1 us
    all_to_all x1, waiting for transfers between devices, shards(): swap(gather_call(row_lists, counts, nodes, state['sums'], wave_vel, state...  19.8 us
    all_to_all x4, starting transfers between devices, swap(): return lax.all_to_all(value, axis, split_axis=0, concat_axis=0, tiled=True)  14.2 us
    ppermute x2, starting transfers between devices, shifted(): lax.ppermute(value, axis, [(i, (i + by) % devices) for i in range(devices)])  9.04 us
  transfers between devices with their start and end apart: 9, of which 3 were waited for; matrix products, arithmetic and copies ran while one was open for 1% of the time, Pallas kernels for 44%

profile of v7, /device:TPU:0, one launch (start us, length us, event | category | flops | bytes accessed | tf_op | source)
XLA Modules:
  0.0 369.8 jit_solution(16148432441087681282)
XLA Ops:
  0.7 1.8 convert_reduce_fusion.starts
  2.4 4.0 %slots.1 = s32[32,16,128]{2,1,0:T(8,128)} custom-call(s32[33]{0:T(128)S(1)} %convert_reduce_fusion.starts, s32[256,128]{1,0:T(8,128)} %bitcast.56), custom_call_target="tpu_custom_call" | custom-call | tf_op jit(solution)/shard_map/slots/pallas_call | solution.py:63
  6.4 7.3 %all-to-all-start = ((s32[32,16,128]{2,1,0:T(8,128)}), s32[32,16,128]{2,1,0:T(8,128)S(1)}, u32[]{:S(2)}, u32[]{:S(2)}) async-start(s32[32,16,128]{2,1,0:T(8,128)} %slots.1), calls=%async_computation | async-start | bytes 524288 | tf_op jit(solution)/shard_map/all_to_all | solution.py:993
  13.8 1.8 copy.26
  15.6 7.8 %pack.1 = f32[32,96,128]{2,1,0:T(8,128)} custom-call(s32[33]{0:T(128)S(1)} %convert_reduce_fusion.starts, f32[3,256,128]{2,1,0:T(8,128)} %bitcast.47), custom_call_target="tpu_custom_call" | custom-call | tf_op jit(solution)/shard_map/pack/pallas_call | solution.py:63
  23.3 1.0 all-to-all-done.slots_ref
  24.3 5.0 %all-to-all-start.1 = ((f32[32,96,128]{2,1,0:T(8,128)}), f32[32,96,128]{2,1,0:T(8,128)}, u32[]{:S(2)}, u32[]{:S(2)}) async-start(f32[32,96,128]{2,1,0:T(8,128)} %pack.1), calls=%async_computation.1 | async-start | bytes 3145728 | tf_op jit(solution)/shard_map/all_to_all | solution.py:995
  30.7 9.5 %order.1 = (s32[1032]{0:T(1024)S(1)}, s32[1032]{0:T(1024)S(1)}, s32[7]{0:T(128)S(1)}) custom-call(s32[1024]{0:T(1024)S(1)} %bitcast.45, s32[1024]{0:T(1024)S(1)} %bitcast.46, s32[1]{0:T(128)S(6)} %copy.27.count), custom_call_target="tpu_custom_call" | custom-call | tf_op jit(solution)/shard_map/order/pallas_call | solution.py:63
  40.2 5.8 %nodes.1 = (s32[32,16,128]{2,1,0:T(8,128)}, s32[64,128]{1,0:T(8,128)}, s32[64,128]{1,0:T(8,128)}, s32[64,128]{1,0:T(8,128)}, s32[64,128]{1,0:T(8,128)}, /*index=...) custom-call(s32[32,16,128]{2,1,0:T(8,128)S(1)} %all-to-all-done.slot, ...), custom_call_target="tpu_custom_call" | custom-call | tf_op jit(solution)/shard_map/nodes/pallas_call | solution.py:63
  46.7 20.1 %all-to-all-done.1.refs_1_ = f32[32,96,128]{2,1,0:T(8,128)} async-done(((f32[32,96,128]{2,1,0:T(8,128)}), f32[32,96,128]{2,1,0:T(8,128)}, u32[]{:S(2)}, u32[]{:S(2)}) %all-to-all-start.1) | async-done | bytes 1572896 | tf_op jit(solution)/shard_map/all_to_all | solution.py:995
  66.7 51.9 %scatter.1 = (f32[3072,128]{1,0:T(8,128)}, f32[4096,128]{1,0:T(8,128)}) custom-call(s32[32]{0:T(128)S(1)} %convert_reduce_fusion.1.refs_0_.counts, f32[32,96,128]{2,1,0:T(8,128)} %all-to-all-done.1.refs_1_, s32[8192]{0:T(1024)} %bitcast.67, s32[8192]{0:T(1024)} %bitcast.68, s32[8192]{0:T(1024)} %bitcast.69, s32[8192]{0:T(1024)} %bitcast.70, s32[8192]{0:T(1024)} %bitcast.71, ...), custom_call_target="tpu_custom_call" | custom-call | tf_op jit(solution)/shard_map/scatter/pallas_call | solution.py:63
  118.6 5.3 %depth.1 = (f32[8,16,1536]{2,1,0:T(8,128)}, f32[8,128]{1,0:T(8,128)}) custom-call(f32[3072,128]{1,0:T(8,128)} %get-tuple-element.70.refs_0_, f32[128,128]{1,0:T(8,128)} %constant.33.clone.refs_1_), custom_call_target="tpu_custom_call" | custom-call | tf_op jit(solution)/shard_map/depth/pallas_call | solution.py:63
  123.9 3.7 all-to-all-start.2
  127.6 23.2 %within.4 = (f32[4096,128]{1,0:T(8,128)}, f32[8,128]{1,0:T(8,128)}) custom-call(s32[1032]{0:T(1024)S(1)} %get-tuple-element.47.refs_0_, s32[7]{0:T(128)S(1)} %get-tuple-element.48.refs_10_.refs_1_, f32[4096,128]{1,0:T(8,128)} %get-tuple-element.57.refs_2_, f32[8,128]{1,0:T(8,128)} %get-tuple-element.60.refs_3_), custom_call_target="tpu_custom_call" | custom-call | tf_op jit(solution)/shard_map/within/pallas_call | solution.py:63
  150.9 7.4 %first.1 = (f32[4,12,32,128]{3,2,1,0:T(8,128)}, f32[8,128]{1,0:T(8,128)}) custom-call(f32[128,1536]{1,0:T(8,128)S(1)} %bitcast.43, f32[128,256]{1,0:T(8,128)} %constant.34.clone.refs_1_, f32[8,128]{1,0:T(8,128)} %get-tuple-element.63.refs_2_), custom_call_target="tpu_custom_call" | custom-call | tf_op jit(solution)/shard_map/first/pallas_call | solution.py:63
  158.3 3.5 all-to-all-start.3
  161.8 4.8 %collective-permute-start = (f32[3072,128]{1,0:T(8,128)}, f32[3072,128]{1,0:T(8,128)}, u32[]{:S(2)}, u32[]{:S(2)}) collective-permute-start(f32[3072,128]{1,0:T(8,128)} %get-tuple-element.70.refs_0_), channel_id=1, source_target_pairs={{0,28},{4,0},{8,4},{12,8},{16,12},{20,16},{24,20},{28,24},{1,29},{... | collective-permute-start | bytes 4718600 | tf_op jit(solution)/shard_map/ppermute | solution.py:30
  166.7 13.4 %within.5 = (f32[4096,128]{1,0:T(8,128)}, f32[8,128]{1,0:T(8,128)}) custom-call(s32[1032]{0:T(1024)S(1)} %get-tuple-element.47.refs_0_, s32[7]{0:T(128)S(1)} %get-tuple-element.48.refs_10_.refs_1_, f32[4096,128]{1,0:T(8,128)} %get-tuple-element.57.refs_2_, f32[4096,128]{1,0:T(8,128)} %get-tuple-element.61.refs_3_, f32[8,128]{1,0:T(8,128)} %get-tuple-element.64.refs_4_), custom_call_target="tpu_custom_call" | custom-call | tf_op jit(solution)/shard_map/within/pallas_call | solution.py:63
  180.1 6.1 %second.1 = (f32[4,12,32,128]{3,2,1,0:T(8,128)}, f32[8,128]{1,0:T(8,128)}) custom-call(s32[2]{0:T(128)S(1)} %pad_add_fusion.refs_0_, f32[4,12,32,128]{3,2,1,0:T(8,128)S(1)} %bitcast.44, f32[256,128]{1,0:T(8,128)} %constant.35.clone.refs_2_, f32[4,8,128]{2,1,0:T(8,128)} %constant.36.clone.refs_3_, f32[8,8,128]{2,1,0:T(8,128)} %constant.37.clone.refs_4_, ...), custom_call_target="tpu_custom_call" | custom-call | tf_op jit(solution)/shard_map/second/pallas_call | solution.py:63
  186.2 3.5 all-to-all-start.4
  189.7 15.8 %within.6 = (f32[4096,128]{1,0:T(8,128)}, f32[8,128]{1,0:T(8,128)}) custom-call(s32[1032]{0:T(1024)S(1)} %get-tuple-element.47.refs_0_, s32[7]{0:T(128)S(1)} %get-tuple-element.48.refs_10_.refs_1_, f32[4096,128]{1,0:T(8,128)} %get-tuple-element.57.refs_2_, f32[4096,128]{1,0:T(8,128)} %get-tuple-element.65.refs_3_, f32[8,128]{1,0:T(8,128)} %get-tuple-element.68.refs_4_), custom_call_target="tpu_custom_call" | custom-call | tf_op jit(solution)/shard_map/within/pallas_call | solution.py:63
  205.5 6.8 %first_back.1 = (f32[128,1536]{1,0:T(8,128)}, f32[8,128]{1,0:T(8,128)}) custom-call(f32[4,12,32,128]{3,2,1,0:T(8,128)S(1)} %bitcast.42, f32[128,256]{1,0:T(8,128)} %constant.34.clone.refs_1_, f32[8,128]{1,0:T(8,128)} %get-tuple-element.72.refs_2_), custom_call_target="tpu_custom_call" | custom-call | tf_op jit(solution)/shard_map/first_back/pallas_call | solution.py:63
  212.2 3.5 all-to-all-start.5
  215.8 55.9 %beyond.1 = (f32[4096,128]{1,0:T(8,128)}, f32[8,128]{1,0:T(8,128)}, f32[1536,128]{1,0:T(8,128)}) custom-call(s32[1032]{0:T(1024)S(1)} %get-tuple-element.58.refs_0_, s32[7]{0:T(128)S(1)} %get-tuple-element.48.refs_10_.refs_1_, f32[4096,128]{1,0:T(8,128)} %get-tuple-element.57.refs_2_, f32[4096,128]{1,0:T(8,128)} %get-tuple-element.69.refs_3_, ...), custom_call_target="tpu_custom_call" | custom-call | tf_op jit(solution)/shard_map/beyond/pallas_call | solution.py:63
  271.7 4.3 %collective-permute-start.1 = (f32[1536,128]{1,0:T(8,128)}, f32[1536,128]{1,0:T(8,128)}, u32[]{:S(2)}, u32[]{:S(2)}) collective-permute-start(f32[1536,128]{1,0:T(8,128)} %get-tuple-element.79), channel_id=1, source_target_pairs={{0,4},{4,8},{8,12},{12,16},{16,20},{20,24},{24,28},{28,0},{1,5},{5... | collective-permute-start | bytes 2359304 | tf_op jit(solution)/shard_map/ppermute | solution.py:30
  275.9 15.0 %within.7 = (f32[4096,128]{1,0:T(8,128)}, f32[8,128]{1,0:T(8,128)}) custom-call(s32[1032]{0:T(1024)S(1)} %get-tuple-element.47.refs_0_, s32[7]{0:T(128)S(1)} %get-tuple-element.48.refs_10_.refs_1_, f32[4096,128]{1,0:T(8,128)} %get-tuple-element.57.refs_2_, f32[4096,128]{1,0:T(8,128)} %get-tuple-element.74.refs_3_), custom_call_target="tpu_custom_call" | custom-call | tf_op jit(solution)/shard_map/within/pallas_call | solution.py:63
  290.9 5.1 %depth_back.1 = (f32[1536,128]{1,0:T(8,128)}, f32[8,128]{1,0:T(8,128)}) custom-call(f32[8,16,1536]{2,1,0:T(8,128)S(1)} %all-to-all-done.5.refs_0_, f32[128,128]{1,0:T(8,128)} %constant.39.clone.refs_1_, f32[8,128]{1,0:T(8,128)} %get-tuple-element.77.refs_2_), custom_call_target="tpu_custom_call" | custom-call | tf_op jit(solution)/shard_map/depth_back/pallas_call | solution.py:63
  296.0 41.8 %gather.1 = f32[32,48,128]{2,1,0:T(8,128)} custom-call(s32[32]{0:T(128)S(1)} %convert_reduce_fusion.1.refs_0_.counts, s32[32,16,128]{2,1,0:T(8,128)} %get-tuple-element.46.node_ref, f32[4096,128]{1,0:T(8,128)} %get-tuple-element.75.sums_ref, f32[1536,128]{1,0:T(8,128)} %get-tuple-element.78.one_ref, f32[1536,128]{1,0:T(8,128)} %collective-permute-done.1.two_ref, ...), custom_call_target="tpu_custom_call" | custom-call | tf_op jit(solution)/shard_map/gather/pallas_call | solution.py:63
  337.8 4.1 %all-to-all-start.6 = ((f32[32,48,128]{2,1,0:T(8,128)}), f32[32,48,128]{2,1,0:T(8,128)S(1)}, u32[]{:S(2)}, u32[]{:S(2)}) async-start(f32[32,48,128]{2,1,0:T(8,128)} %gather.1), calls=%async_computation.6 | async-start | bytes 1572864 | tf_op jit(solution)/shard_map/all_to_all | solution.py:1027
  342.7 19.8 %all-to-all-done.6.in_ref = f32[32,48,128]{2,1,0:T(8,128)S(1)} async-done(((f32[32,48,128]{2,1,0:T(8,128)}), f32[32,48,128]{2,1,0:T(8,128)S(1)}, u32[]{:S(2)}, u32[]{:S(2)}) %all-to-all-start.6) | async-done | bytes 786464 | tf_op jit(solution)/shard_map/all_to_all | solution.py:1027
  362.5 4.8 %finish.1 = (f32[3,256,128]{2,1,0:T(8,128)}, f32[3,256,128]{2,1,0:T(8,128)}) custom-call(s32[33]{0:T(128)S(1)} %convert_reduce_fusion.starts, f32[32,48,128]{2,1,0:T(8,128)S(1)} %all-to-all-done.6.in_ref, f32[3,256,128]{2,1,0:T(8,128)} %bitcast.48, f32[3,256,128]{2,1,0:T(8,128)} %bitcast.49), custom_call_target="tpu_custom_call" | custom-call | tf_op jit(solution)/shard_map/finish/pallas_call | solution.py:63
  367.2 2.6 copy_bitcast_fusion
  (19 shorter events, 2.3 us)
Async XLA Ops:
  0.6 28.7 %copy-start = (s32[8,1,65536]{2,1,0:T(1,128)S(1)}, s32[8,1,65536]{2,1,0:T(1,128)}, u32[]{:S(2)}) copy-start(s32[8,1,65536]{2,1,0:T(1,128)} %param.18) | copy-start | bytes 6291460
  6.4 17.9 %all-to-all-start = ((s32[32,16,128]{2,1,0:T(8,128)}), s32[32,16,128]{2,1,0:T(8,128)S(1)}, u32[]{:S(2)}, u32[]{:S(2)}) async-start(s32[32,16,128]{2,1,0:T(8,128)} %slots.1), calls=%async_computation | async-start | bytes 524288 | tf_op jit(solution)/shard_map/all_to_all | solution.py:993
  23.3 7.4 %copy-start.1 = (s32[1,1024]{1,0:T(1,128)S(1)}, s32[1,1024]{1,0:T(1,128)}, u32[]{:S(2)}) copy-start(s32[1,1024]{1,0:T(1,128)} %param.19) | copy-start | bytes 12292
  23.3 7.4 %copy-start.2 = (s32[1,1024]{1,0:T(1,128)S(1)}, s32[1,1024]{1,0:T(1,128)}, u32[]{:S(2)}) copy-start(s32[1,1024]{1,0:T(1,128)} %param.20) | copy-start | bytes 12292
  24.3 42.4 %all-to-all-start.1 = ((f32[32,96,128]{2,1,0:T(8,128)}), f32[32,96,128]{2,1,0:T(8,128)}, u32[]{:S(2)}, u32[]{:S(2)}) async-start(f32[32,96,128]{2,1,0:T(8,128)} %pack.1), calls=%async_computation.1 | async-start | bytes 3145728 | tf_op jit(solution)/shard_map/all_to_all | solution.py:995
  123.9 26.9 %all-to-all-start.2 = ((f32[8,16,1536]{2,1,0:T(8,128)}), f32[8,16,1536]{2,1,0:T(8,128)S(1)}, u32[]{:S(2)}, u32[]{:S(2)}) async-start(f32[8,16,1536]{2,1,0:T(8,128)} %get-tuple-element.62), calls=%async_computation.2 | async-start | bytes 1572864 | tf_op jit(solution)/shard_map/all_to_all | solution.py:953
  158.3 21.8 %all-to-all-start.3 = ((f32[4,384,128]{2,1,0:T(8,128)}), f32[4,384,128]{2,1,0:T(8,128)S(1)}, u32[]{:S(2)}, u32[]{:S(2)}) async-start(f32[4,384,128]{2,1,0:T(8,128)} %bitcast.52), calls=%async_computation.3 | async-start | bytes 1572864 | tf_op jit(solution)/shard_map/all_to_all | solution.py:953
  161.8 54.0 %collective-permute-start = (f32[3072,128]{1,0:T(8,128)}, f32[3072,128]{1,0:T(8,128)}, u32[]{:S(2)}, u32[]{:S(2)}) collective-permute-start(f32[3072,128]{1,0:T(8,128)} %get-tuple-element.70.refs_0_), channel_id=1, source_target_pairs={{0,28},{4,0},{8,4},{12,8},{16,12},{20,16},{24,20},{28,24},{1,29},{... | collective-permute-start | bytes 4718600 | tf_op jit(solution)/shard_map/ppermute | solution.py:30
  186.2 19.3 %all-to-all-start.4 = ((f32[4,384,128]{2,1,0:T(8,128)}), f32[4,384,128]{2,1,0:T(8,128)S(1)}, u32[]{:S(2)}, u32[]{:S(2)}) async-start(f32[4,384,128]{2,1,0:T(8,128)} %bitcast.53), calls=%async_computation.4 | async-start | bytes 1572864 | tf_op jit(solution)/shard_map/all_to_all | solution.py:953
  212.2 78.7 %all-to-all-start.5 = ((f32[8,16,1536]{2,1,0:T(8,128)}), f32[8,16,1536]{2,1,0:T(8,128)S(1)}, u32[]{:S(2)}, u32[]{:S(2)}) async-start(f32[8,16,1536]{2,1,0:T(8,128)} %bitcast.51), calls=%async_computation.5 | async-start | bytes 1572864 | tf_op jit(solution)/shard_map/all_to_all | solution.py:953
  271.7 24.3 %collective-permute-start.1 = (f32[1536,128]{1,0:T(8,128)}, f32[1536,128]{1,0:T(8,128)}, u32[]{:S(2)}, u32[]{:S(2)}) collective-permute-start(f32[1536,128]{1,0:T(8,128)} %get-tuple-element.79), channel_id=1, source_target_pairs={{0,4},{4,8},{8,12},{12,16},{16,20},{20,24},{24,28},{28,0},{1,5},{5... | collective-permute-start | bytes 2359304 | tf_op jit(solution)/shard_map/ppermute | solution.py:30
  296.0 45.9 %copy-start.3 = (f32[3,32768]{1,0:T(4,128)S(1)}, f32[3,32768]{1,0:T(4,128)}, u32[]{:S(2)}) copy-start(f32[3,32768]{1,0:T(4,128)} %param.16) | copy-start | bytes 1179652
  337.8 24.7 %all-to-all-start.6 = ((f32[32,48,128]{2,1,0:T(8,128)}), f32[32,48,128]{2,1,0:T(8,128)S(1)}, u32[]{:S(2)}, u32[]{:S(2)}) async-start(f32[32,48,128]{2,1,0:T(8,128)} %gather.1), calls=%async_computation.6 | async-start | bytes 1572864 | tf_op jit(solution)/shard_map/all_to_all | solution.py:1027

commit v8 on v6

--- a/solution.py
+++ b/solution.py
@@ -30,7 +30,7 @@
     return lax.ppermute(value, axis, [(i, (i + by) % devices) for i in range(devices)])
 
 
-SPAN = 16
+SPAN = 32
 PARTS = (25, 37, 52)
 
 SMEM_SPEC = pl.BlockSpec(memory_space=pltpu.SMEM)
@@ -256,7 +256,7 @@
     def _(k):
         table[pl.ds(pl.multiple_of(k * 128, 128), 128), :] = jnp.zeros((128, 128), jnp.float32)
 
-    together = 4 if depth % 4 == 0 else 1
+    together = 8 if depth % 8 == 0 else 1
 
     @pl.loop(0, in_ref.shape[0])
     def _(t):
@@ -331,7 +331,7 @@
             comb[8 * i : 8 * i + 8, :] = comb[8 * i : 8 * i + 8, :] + both
         table[pl.ds(pl.multiple_of(g * 128, 128), 128), :] = jnp.transpose(comb[...])
 
-    together = 4 if depth % 4 == 0 else 1
+    together = 8 if depth % 8 == 0 else 1
 
     @pl.loop(0, out_ref.shape[0])
     def _(t):

time: 365 us -> 359 us (0.984)
  Pallas kernels: 274 us -> 212 us
  starting transfers between devices: 34 us -> 78.4 us
  waiting for transfers between devices: 46.1 us -> 57.9 us
    pallas_call x17, Pallas kernels: 274 us -> 212 us  [run(): pl.pallas_call(kernel, out_shape=kept if several else kept[0], grid=(1,),...]
    ppermute x2, starting transfers between devices: 5.04 us -> 35.9 us  [shifted(): lax.ppermute(value, axis, [(i, (i + by) % devices) for i in range(devices)])]
    all_to_all x1, starting transfers between devices: 2.62 us -> 11.5 us  [shards(): swap(gather_call(row_lists, counts, nodes, state['sums'], wave_vel, state...]
    all_to_all x4, waiting for transfers between devices: 0.01 us -> 7.95 us  [swap(): return lax.all_to_all(value, axis, split_axis=0, concat_axis=0, tiled=True)]
    all_to_all x4, starting transfers between devices: 14.1 us -> 18.7 us  [swap(): return lax.all_to_all(value, axis, split_axis=0, concat_axis=0, tiled=True)]
    all_to_all x1, waiting for transfers between devices: 20.1 us -> 24.1 us  [shards(): data = swap(pack_call(starts, places, depth))]
  transfers between devices with their start and end apart: 9 -> 9, of which waited for: 4 -> 5; matrix products, arithmetic and copies ran while one was open for 1% -> 1% of each run, Pallas kernels for 45% -> 31%
where the time goes in v8:
time: 359 us; the launch traced here: 358 us
  Pallas kernels  212 us (59%)
  starting transfers between devices  78.4 us (22%)
  waiting for transfers between devices  57.9 us (16%)
  local copies, waits for them, and re-layouts  5.96 us (2%)
    pallas_call x17, Pallas kernels, run(): pl.pallas_call(kernel, out_shape=kept if several else kept[0], grid=(1,),...  212 us
    ppermute x2, starting transfers between devices, shifted(): lax.ppermute(value, axis, [(i, (i + by) % devices) for i in range(devices)])  35.9 us
    all_to_all x1, waiting for transfers between devices, shards(): data = swap(pack_call(starts, places, depth))  24.1 us
    all_to_all x1, waiting for transfers between devices, shards(): swap(gather_call(row_lists, counts, nodes, state['sums'], wave_vel, state...  19.8 us
    all_to_all x4, starting transfers between devices, swap(): return lax.all_to_all(value, axis, split_axis=0, concat_axis=0, tiled=True)  18.7 us
    all_to_all x1, starting transfers between devices, shards(): swap(gather_call(row_lists, counts, nodes, state['sums'], wave_vel, state...  11.5 us
    all_to_all x4, waiting for transfers between devices, swap(): return lax.all_to_all(value, axis, split_axis=0, concat_axis=0, tiled=True)  7.95 us
    all_to_all x1, starting transfers between devices, shards(): taken = swap(slots_call(starts, route.reshape(rows, 128), depth))  7.33 us
  transfers between devices with their start and end apart: 9, of which 5 were waited for; matrix products, arithmetic and copies ran while one was open for 1% of the time, Pallas kernels for 31%

profile of v8, /device:TPU:0, one launch (start us, length us, event | category | flops | bytes accessed | tf_op | source)
XLA Modules:
  0.0 358.0 jit_solution(7542093259735767140)
XLA Ops:
  2.4 4.0 %slots.1 = s32[32,16,128]{2,1,0:T(8,128)} custom-call(s32[33]{0:T(128)S(1)} %convert_reduce_fusion.starts, s32[256,128]{1,0:T(8,128)} %bitcast.56), custom_call_target="tpu_custom_call" | custom-call | tf_op jit(solution)/shard_map/slots/pallas_call | solution.py:63
  6.4 7.3 %all-to-all-start = ((s32[32,16,128]{2,1,0:T(8,128)}), s32[32,16,128]{2,1,0:T(8,128)S(1)}, u32[]{:S(2)}, u32[]{:S(2)}) async-start(s32[32,16,128]{2,1,0:T(8,128)} %slots.1), calls=%async_computation | async-start | bytes 524288 | tf_op jit(solution)/shard_map/all_to_all | solution.py:974
  13.8 1.8 copy.26
  15.6 7.8 %pack.1 = f32[32,96,128]{2,1,0:T(8,128)} custom-call(s32[33]{0:T(128)S(1)} %convert_reduce_fusion.starts, f32[3,256,128]{2,1,0:T(8,128)} %bitcast.47), custom_call_target="tpu_custom_call" | custom-call | tf_op jit(solution)/shard_map/pack/pallas_call | solution.py:63
  24.3 5.0 %all-to-all-start.1 = ((f32[32,96,128]{2,1,0:T(8,128)}), f32[32,96,128]{2,1,0:T(8,128)}, u32[]{:S(2)}, u32[]{:S(2)}) async-start(f32[32,96,128]{2,1,0:T(8,128)} %pack.1), calls=%async_computation.1 | async-start | bytes 3145728 | tf_op jit(solution)/shard_map/all_to_all | solution.py:976
  30.7 5.5 %order.1 = (s32[1032]{0:T(1024)S(1)}, s32[1032]{0:T(1024)S(1)}, s32[7]{0:T(128)S(1)}) custom-call(s32[1024]{0:T(1024)S(1)} %bitcast.45, s32[1024]{0:T(1024)S(1)} %bitcast.46, s32[1]{0:T(128)S(6)} %copy.27.count), custom_call_target="tpu_custom_call" | custom-call | tf_op jit(solution)/shard_map/order/pallas_call | solution.py:63
  36.2 5.8 %nodes.1 = (s32[32,16,128]{2,1,0:T(8,128)}, s32[64,128]{1,0:T(8,128)}, s32[64,128]{1,0:T(8,128)}, s32[64,128]{1,0:T(8,128)}, s32[64,128]{1,0:T(8,128)}, /*index=...) custom-call(s32[32,16,128]{2,1,0:T(8,128)S(1)} %all-to-all-done.slot, ...), custom_call_target="tpu_custom_call" | custom-call | tf_op jit(solution)/shard_map/nodes/pallas_call | solution.py:63
  42.6 24.1 %all-to-all-done.1.refs_1_ = f32[32,96,128]{2,1,0:T(8,128)} async-done(((f32[32,96,128]{2,1,0:T(8,128)}), f32[32,96,128]{2,1,0:T(8,128)}, u32[]{:S(2)}, u32[]{:S(2)}) %all-to-all-start.1) | async-done | bytes 1572896 | tf_op jit(solution)/shard_map/all_to_all | solution.py:976
  66.7 43.2 %scatter.1 = (f32[3072,128]{1,0:T(8,128)}, f32[4096,128]{1,0:T(8,128)}) custom-call(s32[32]{0:T(128)S(1)} %convert_reduce_fusion.1.refs_0_.counts, f32[32,96,128]{2,1,0:T(8,128)} %all-to-all-done.1.refs_1_, s32[8192]{0:T(1024)} %bitcast.67, s32[8192]{0:T(1024)} %bitcast.68, s32[8192]{0:T(1024)} %bitcast.69, s32[8192]{0:T(1024)} %bitcast.70, s32[8192]{0:T(1024)} %bitcast.71, ...), custom_call_target="tpu_custom_call" | custom-call | tf_op jit(solution)/shard_map/scatter/pallas_call | solution.py:63
  110.0 5.3 %depth.1 = (f32[8,16,1536]{2,1,0:T(8,128)}, f32[8,128]{1,0:T(8,128)}) custom-call(f32[3072,128]{1,0:T(8,128)} %get-tuple-element.70.refs_0_, f32[128,128]{1,0:T(8,128)} %constant.33.clone.refs_1_), custom_call_target="tpu_custom_call" | custom-call | tf_op jit(solution)/shard_map/depth/pallas_call | solution.py:63
  115.3 4.1 %all-to-all-start.2 = ((f32[8,16,1536]{2,1,0:T(8,128)}), f32[8,16,1536]{2,1,0:T(8,128)S(1)}, u32[]{:S(2)}, u32[]{:S(2)}) async-start(f32[8,16,1536]{2,1,0:T(8,128)} %get-tuple-element.62), calls=%async_computation.2 | async-start | bytes 1572864 | tf_op jit(solution)/shard_map/all_to_all | solution.py:934
  119.4 23.2 %within.4 = (f32[4096,128]{1,0:T(8,128)}, f32[8,128]{1,0:T(8,128)}) custom-call(s32[1032]{0:T(1024)S(1)} %get-tuple-element.47.refs_0_, s32[7]{0:T(128)S(1)} %get-tuple-element.48.refs_10_.refs_1_, f32[4096,128]{1,0:T(8,128)} %get-tuple-element.57.refs_2_, f32[8,128]{1,0:T(8,128)} %get-tuple-element.60.refs_3_), custom_call_target="tpu_custom_call" | custom-call | tf_op jit(solution)/shard_map/within/pallas_call | solution.py:63
  142.6 7.4 %first.1 = (f32[4,12,32,128]{3,2,1,0:T(8,128)}, f32[8,128]{1,0:T(8,128)}) custom-call(f32[128,1536]{1,0:T(8,128)S(1)} %bitcast.43, f32[128,256]{1,0:T(8,128)} %constant.34.clone.refs_1_, f32[8,128]{1,0:T(8,128)} %get-tuple-element.63.refs_2_), custom_call_target="tpu_custom_call" | custom-call | tf_op jit(solution)/shard_map/first/pallas_call | solution.py:63
  150.1 3.5 all-to-all-start.3
  153.6 4.8 %collective-permute-start = (f32[3072,128]{1,0:T(8,128)}, f32[3072,128]{1,0:T(8,128)}, u32[]{:S(2)}, u32[]{:S(2)}) collective-permute-start(f32[3072,128]{1,0:T(8,128)} %get-tuple-element.70.refs_0_), channel_id=1, source_target_pairs={{0,28},{4,0},{8,4},{12,8},{16,12},{20,16},{24,20},{28,24},{1,29},{... | collective-permute-start | bytes 4718600 | tf_op jit(solution)/shard_map/ppermute | solution.py:30
  158.4 11.8 %within.5 = (f32[4096,128]{1,0:T(8,128)}, f32[8,128]{1,0:T(8,128)}) custom-call(s32[1032]{0:T(1024)S(1)} %get-tuple-element.47.refs_0_, s32[7]{0:T(128)S(1)} %get-tuple-element.48.refs_10_.refs_1_, f32[4096,128]{1,0:T(8,128)} %get-tuple-element.57.refs_2_, f32[4096,128]{1,0:T(8,128)} %get-tuple-element.61.refs_3_, f32[8,128]{1,0:T(8,128)} %get-tuple-element.64.refs_4_), custom_call_target="tpu_custom_call" | custom-call | tf_op jit(solution)/shard_map/within/pallas_call | solution.py:63
  170.2 6.1 %second.1 = (f32[4,12,32,128]{3,2,1,0:T(8,128)}, f32[8,128]{1,0:T(8,128)}) custom-call(s32[2]{0:T(128)S(1)} %pad_add_fusion.refs_0_, f32[4,12,32,128]{3,2,1,0:T(8,128)S(1)} %bitcast.44, f32[256,128]{1,0:T(8,128)} %constant.35.clone.refs_2_, f32[4,8,128]{2,1,0:T(8,128)} %constant.36.clone.refs_3_, f32[8,8,128]{2,1,0:T(8,128)} %constant.37.clone.refs_4_, ...), custom_call_target="tpu_custom_call" | custom-call | tf_op jit(solution)/shard_map/second/pallas_call | solution.py:63
  176.4 4.8 %all-to-all-start.4 = ((f32[4,384,128]{2,1,0:T(8,128)}), f32[4,384,128]{2,1,0:T(8,128)S(1)}, u32[]{:S(2)}, u32[]{:S(2)}) async-start(f32[4,384,128]{2,1,0:T(8,128)} %bitcast.53), calls=%async_computation.4 | async-start | bytes 1572864 | tf_op jit(solution)/shard_map/all_to_all | solution.py:934
  181.2 3.7 %within.6 = (f32[4096,128]{1,0:T(8,128)}, f32[8,128]{1,0:T(8,128)}) custom-call(s32[1032]{0:T(1024)S(1)} %get-tuple-element.47.refs_0_, s32[7]{0:T(128)S(1)} %get-tuple-element.48.refs_10_.refs_1_, f32[4096,128]{1,0:T(8,128)} %get-tuple-element.57.refs_2_, f32[4096,128]{1,0:T(8,128)} %get-tuple-element.65.refs_3_, f32[8,128]{1,0:T(8,128)} %get-tuple-element.68.refs_4_), custom_call_target="tpu_custom_call" | custom-call | tf_op jit(solution)/shard_map/within/pallas_call | solution.py:63
  184.9 7.9 %all-to-all-done.4 = f32[4,384,128]{2,1,0:T(8,128)S(1)} async-done(((f32[4,384,128]{2,1,0:T(8,128)}), f32[4,384,128]{2,1,0:T(8,128)S(1)}, u32[]{:S(2)}, u32[]{:S(2)}) %all-to-all-start.4) | async-done | bytes 786464 | tf_op jit(solution)/shard_map/all_to_all | solution.py:934
  192.8 6.8 %first_back.1 = (f32[128,1536]{1,0:T(8,128)}, f32[8,128]{1,0:T(8,128)}) custom-call(f32[4,12,32,128]{3,2,1,0:T(8,128)S(1)} %bitcast.42, f32[128,256]{1,0:T(8,128)} %constant.34.clone.refs_1_, f32[8,128]{1,0:T(8,128)} %get-tuple-element.72.refs_2_), custom_call_target="tpu_custom_call" | custom-call | tf_op jit(solution)/shard_map/first_back/pallas_call | solution.py:63
  199.6 6.3 %all-to-all-start.5 = ((f32[8,16,1536]{2,1,0:T(8,128)}), f32[8,16,1536]{2,1,0:T(8,128)S(1)}, u32[]{:S(2)}, u32[]{:S(2)}) async-start(f32[8,16,1536]{2,1,0:T(8,128)} %bitcast.51), calls=%async_computation.5 | async-start | bytes 1572864 | tf_op jit(solution)/shard_map/all_to_all | solution.py:934
  205.9 30.1 %beyond.1 = (f32[4096,128]{1,0:T(8,128)}, f32[8,128]{1,0:T(8,128)}, f32[1536,128]{1,0:T(8,128)}) custom-call(s32[1032]{0:T(1024)S(1)} %get-tuple-element.58.refs_0_, s32[7]{0:T(128)S(1)} %get-tuple-element.48.refs_10_.refs_1_, f32[4096,128]{1,0:T(8,128)} %get-tuple-element.57.refs_2_, f32[4096,128]{1,0:T(8,128)} %get-tuple-element.69.refs_3_, ...), custom_call_target="tpu_custom_call" | custom-call | tf_op jit(solution)/shard_map/beyond/pallas_call | solution.py:63
  236.0 31.1 %collective-permute-start.1 = (f32[1536,128]{1,0:T(8,128)}, f32[1536,128]{1,0:T(8,128)}, u32[]{:S(2)}, u32[]{:S(2)}) collective-permute-start(f32[1536,128]{1,0:T(8,128)} %get-tuple-element.79), channel_id=1, source_target_pairs={{0,4},{4,8},{8,12},{12,16},{16,20},{20,24},{24,28},{28,0},{1,5},{5... | collective-permute-start | bytes 2359304 | tf_op jit(solution)/shard_map/ppermute | solution.py:30
  267.1 3.7 %within.7 = (f32[4096,128]{1,0:T(8,128)}, f32[8,128]{1,0:T(8,128)}) custom-call(s32[1032]{0:T(1024)S(1)} %get-tuple-element.47.refs_0_, s32[7]{0:T(128)S(1)} %get-tuple-element.48.refs_10_.refs_1_, f32[4096,128]{1,0:T(8,128)} %get-tuple-element.57.refs_2_, f32[4096,128]{1,0:T(8,128)} %get-tuple-element.74.refs_3_), custom_call_target="tpu_custom_call" | custom-call | tf_op jit(solution)/shard_map/within/pallas_call | solution.py:63
  270.8 5.1 %depth_back.1 = (f32[1536,128]{1,0:T(8,128)}, f32[8,128]{1,0:T(8,128)}) custom-call(f32[8,16,1536]{2,1,0:T(8,128)S(1)} %all-to-all-done.5.refs_0_, f32[128,128]{1,0:T(8,128)} %constant.39.clone.refs_1_, f32[8,128]{1,0:T(8,128)} %get-tuple-element.77.refs_2_), custom_call_target="tpu_custom_call" | custom-call | tf_op jit(solution)/shard_map/depth_back/pallas_call | solution.py:63
  275.8 5.0 %collective-permute-done.1.two_ref = f32[1536,128]{1,0:T(8,128)} collective-permute-done((f32[1536,128]{1,0:T(8,128)}, f32[1536,128]{1,0:T(8,128)}, u32[]{:S(2)}, u32[]{:S(2)}) %collective-permute-start.1) | collective-permute-done | bytes 786464 | tf_op jit(solution)/shard_map/ppermute | solution.py:30
  280.9 37.6 %gather.1 = f32[32,48,128]{2,1,0:T(8,128)} custom-call(s32[32]{0:T(128)S(1)} %convert_reduce_fusion.1.refs_0_.counts, s32[32,16,128]{2,1,0:T(8,128)} %get-tuple-element.46.node_ref, f32[4096,128]{1,0:T(8,128)} %get-tuple-element.75.sums_ref, f32[1536,128]{1,0:T(8,128)} %get-tuple-element.78.one_ref, f32[1536,128]{1,0:T(8,128)} %collective-permute-done.1.two_ref, ...), custom_call_target="tpu_custom_call" | custom-call | tf_op jit(solution)/shard_map/gather/pallas_call | solution.py:63
  318.5 11.5 %all-to-all-start.6 = ((f32[32,48,128]{2,1,0:T(8,128)}), f32[32,48,128]{2,1,0:T(8,128)S(1)}, u32[]{:S(2)}, u32[]{:S(2)}) async-start(f32[32,48,128]{2,1,0:T(8,128)} %gather.1), calls=%async_computation.6 | async-start | bytes 1572864 | tf_op jit(solution)/shard_map/all_to_all | solution.py:1008
  330.8 19.8 %all-to-all-done.6.in_ref = f32[32,48,128]{2,1,0:T(8,128)S(1)} async-done(((f32[32,48,128]{2,1,0:T(8,128)}), f32[32,48,128]{2,1,0:T(8,128)S(1)}, u32[]{:S(2)}, u32[]{:S(2)}) %all-to-all-start.6) | async-done | bytes 786464 | tf_op jit(solution)/shard_map/all_to_all | solution.py:1008
  350.6 4.8 %finish.1 = (f32[3,256,128]{2,1,0:T(8,128)}, f32[3,256,128]{2,1,0:T(8,128)}) custom-call(s32[33]{0:T(128)S(1)} %convert_reduce_fusion.starts, f32[32,48,128]{2,1,0:T(8,128)S(1)} %all-to-all-done.6.in_ref, f32[3,256,128]{2,1,0:T(8,128)} %bitcast.48, f32[3,256,128]{2,1,0:T(8,128)} %bitcast.49), custom_call_target="tpu_custom_call" | custom-call | tf_op jit(solution)/shard_map/finish/pallas_call | solution.py:63
  355.3 2.6 copy_bitcast_fusion
  (19 shorter events, 5.0 us)
Async XLA Ops:
  0.6 28.7 %copy-start = (s32[8,1,65536]{2,1,0:T(1,128)S(1)}, s32[8,1,65536]{2,1,0:T(1,128)}, u32[]{:S(2)}) copy-start(s32[8,1,65536]{2,1,0:T(1,128)} %param.18) | copy-start | bytes 6291460
  6.4 17.9 %all-to-all-start = ((s32[32,16,128]{2,1,0:T(8,128)}), s32[32,16,128]{2,1,0:T(8,128)S(1)}, u32[]{:S(2)}, u32[]{:S(2)}) async-start(s32[32,16,128]{2,1,0:T(8,128)} %slots.1), calls=%async_computation | async-start | bytes 524288 | tf_op jit(solution)/shard_map/all_to_all | solution.py:974
  23.3 7.4 %copy-start.1 = (s32[1,1024]{1,0:T(1,128)S(1)}, s32[1,1024]{1,0:T(1,128)}, u32[]{:S(2)}) copy-start(s32[1,1024]{1,0:T(1,128)} %param.19) | copy-start | bytes 12292
  23.3 7.4 %copy-start.2 = (s32[1,1024]{1,0:T(1,128)S(1)}, s32[1,1024]{1,0:T(1,128)}, u32[]{:S(2)}) copy-start(s32[1,1024]{1,0:T(1,128)} %param.20) | copy-start | bytes 12292
  24.3 42.4 %all-to-all-start.1 = ((f32[32,96,128]{2,1,0:T(8,128)}), f32[32,96,128]{2,1,0:T(8,128)}, u32[]{:S(2)}, u32[]{:S(2)}) async-start(f32[32,96,128]{2,1,0:T(8,128)} %pack.1), calls=%async_computation.1 | async-start | bytes 3145728 | tf_op jit(solution)/shard_map/all_to_all | solution.py:976
  115.3 27.4 %all-to-all-start.2 = ((f32[8,16,1536]{2,1,0:T(8,128)}), f32[8,16,1536]{2,1,0:T(8,128)S(1)}, u32[]{:S(2)}, u32[]{:S(2)}) async-start(f32[8,16,1536]{2,1,0:T(8,128)} %get-tuple-element.62), calls=%async_computation.2 | async-start | bytes 1572864 | tf_op jit(solution)/shard_map/all_to_all | solution.py:934
  150.1 20.1 %all-to-all-start.3 = ((f32[4,384,128]{2,1,0:T(8,128)}), f32[4,384,128]{2,1,0:T(8,128)S(1)}, u32[]{:S(2)}, u32[]{:S(2)}) async-start(f32[4,384,128]{2,1,0:T(8,128)} %bitcast.52), calls=%async_computation.3 | async-start | bytes 1572864 | tf_op jit(solution)/shard_map/all_to_all | solution.py:934
  153.6 52.3 %collective-permute-start = (f32[3072,128]{1,0:T(8,128)}, f32[3072,128]{1,0:T(8,128)}, u32[]{:S(2)}, u32[]{:S(2)}) collective-permute-start(f32[3072,128]{1,0:T(8,128)} %get-tuple-element.70.refs_0_), channel_id=1, source_target_pairs={{0,28},{4,0},{8,4},{12,8},{16,12},{20,16},{24,20},{28,24},{1,29},{... | collective-permute-start | bytes 4718600 | tf_op jit(solution)/shard_map/ppermute | solution.py:30
  176.4 16.4 %all-to-all-start.4 = ((f32[4,384,128]{2,1,0:T(8,128)}), f32[4,384,128]{2,1,0:T(8,128)S(1)}, u32[]{:S(2)}, u32[]{:S(2)}) async-start(f32[4,384,128]{2,1,0:T(8,128)} %bitcast.53), calls=%async_computation.4 | async-start | bytes 1572864 | tf_op jit(solution)/shard_map/all_to_all | solution.py:934
  199.6 71.2 %all-to-all-start.5 = ((f32[8,16,1536]{2,1,0:T(8,128)}), f32[8,16,1536]{2,1,0:T(8,128)S(1)}, u32[]{:S(2)}, u32[]{:S(2)}) async-start(f32[8,16,1536]{2,1,0:T(8,128)} %bitcast.51), calls=%async_computation.5 | async-start | bytes 1572864 | tf_op jit(solution)/shard_map/all_to_all | solution.py:934
  236.0 44.9 %collective-permute-start.1 = (f32[1536,128]{1,0:T(8,128)}, f32[1536,128]{1,0:T(8,128)}, u32[]{:S(2)}, u32[]{:S(2)}) collective-permute-start(f32[1536,128]{1,0:T(8,128)} %get-tuple-element.79), channel_id=1, source_target_pairs={{0,4},{4,8},{8,12},{12,16},{16,20},{20,24},{24,28},{28,0},{1,5},{5... | collective-permute-start | bytes 2359304 | tf_op jit(solution)/shard_map/ppermute | solution.py:30
  280.9 49.1 %copy-start.3 = (f32[3,32768]{1,0:T(4,128)S(1)}, f32[3,32768]{1,0:T(4,128)}, u32[]{:S(2)}) copy-start(f32[3,32768]{1,0:T(4,128)} %param.16) | copy-start | bytes 1179652
  318.5 32.1 %all-to-all-start.6 = ((f32[32,48,128]{2,1,0:T(8,128)}), f32[32,48,128]{2,1,0:T(8,128)S(1)}, u32[]{:S(2)}, u32[]{:S(2)}) async-start(f32[32,48,128]{2,1,0:T(8,128)} %gather.1), calls=%async_computation.6 | async-start | bytes 1572864 | tf_op jit(solution)/shard_map/all_to_all | solution.py:1008

commit v9 on v8

--- a/solution.py
+++ b/solution.py
@@ -30,7 +30,7 @@
     return lax.ppermute(value, axis, [(i, (i + by) % devices) for i in range(devices)])
 
 
-SPAN = 32
+SPAN = 64
 PARTS = (25, 37, 52)
 
 SMEM_SPEC = pl.BlockSpec(memory_space=pltpu.SMEM)

time: 359 us -> 355 us (0.989)
  waiting for transfers between devices: 57.9 us -> 66.2 us
  starting transfers between devices: 78.4 us -> 70.7 us
  Pallas kernels: 212 us -> 208 us
    ppermute x2, waiting for transfers between devices: 5.05 us -> 13.4 us  [shifted(): lax.ppermute(value, axis, [(i, (i + by) % devices) for i in range(devices)])]
    all_to_all x1, starting transfers between devices: 11.5 us -> 6.62 us  [shards(): swap(gather_call(row_lists, counts, nodes, state['sums'], wave_vel, state...]
where the time goes in v9:
time: 355 us
  Pallas kernels  208 us (59%)
  starting transfers between devices  70.7 us (20%)
  waiting for transfers between devices  66.2 us (19%)
  local copies, waits for them, and re-layouts  5.96 us (2%)
    pallas_call x17, Pallas kernels, run(): pl.pallas_call(kernel, out_shape=kept if several else kept[0], grid=(1,),...  208 us
    ppermute x2, starting transfers between devices, shifted(): lax.ppermute(value, axis, [(i, (i + by) % devices) for i in range(devices)])  32.6 us
    all_to_all x1, waiting for transfers between devices, shards(): data = swap(pack_call(starts, places, depth))  24.1 us
    all_to_all x1, waiting for transfers between devices, shards(): swap(gather_call(row_lists, counts, nodes, state['sums'], wave_vel, state...  19.8 us
    all_to_all x4, starting transfers between devices, swap(): return lax.all_to_all(value, axis, split_axis=0, concat_axis=0, tiled=True)  19.2 us
    ppermute x2, waiting for transfers between devices, shifted(): lax.ppermute(value, axis, [(i, (i + by) % devices) for i in range(devices)])  13.4 us
    all_to_all x4, waiting for transfers between devices, swap(): return lax.all_to_all(value, axis, split_axis=0, concat_axis=0, tiled=True)  7.91 us
    all_to_all x1, starting transfers between devices, shards(): taken = swap(slots_call(starts, route.reshape(rows, 128), depth))  7.33 us
  transfers between devices with their start and end apart: 9, of which 5 were waited for; matrix products, arithmetic and copies ran while one was open for 1% of the time, Pallas kernels for 31%

profile of v9, /device:TPU:0, one launch (start us, length us, event | category | flops | bytes accessed | tf_op | source)
XLA Modules:
  0.0 355.3 jit_solution(1044535177413187014)
XLA Ops:
  2.4 4.0 %slots.1 = s32[32,16,128]{2,1,0:T(8,128)} custom-call(s32[33]{0:T(128)S(1)} %convert_reduce_fusion.starts, s32[256,128]{1,0:T(8,128)} %bitcast.56), custom_call_target="tpu_custom_call" | custom-call | tf_op jit(solution)/shard_map/slots/pallas_call | solution.py:63
  6.4 7.3 %all-to-all-start = ((s32[32,16,128]{2,1,0:T(8,128)}), s32[32,16,128]{2,1,0:T(8,128)S(1)}, u32[]{:S(2)}, u32[]{:S(2)}) async-start(s32[32,16,128]{2,1,0:T(8,128)} %slots.1), calls=%async_computation | async-start | bytes 524288 | tf_op jit(solution)/shard_map/all_to_all | solution.py:974
  13.8 1.8 copy.26
  15.6 7.8 %pack.1 = f32[32,96,128]{2,1,0:T(8,128)} custom-call(s32[33]{0:T(128)S(1)} %convert_reduce_fusion.starts, f32[3,256,128]{2,1,0:T(8,128)} %bitcast.47), custom_call_target="tpu_custom_call" | custom-call | tf_op jit(solution)/shard_map/pack/pallas_call | solution.py:63
  24.3 5.0 %all-to-all-start.1 = ((f32[32,96,128]{2,1,0:T(8,128)}), f32[32,96,128]{2,1,0:T(8,128)}, u32[]{:S(2)}, u32[]{:S(2)}) async-start(f32[32,96,128]{2,1,0:T(8,128)} %pack.1), calls=%async_computation.1 | async-start | bytes 3145728 | tf_op jit(solution)/shard_map/all_to_all | solution.py:976
  30.7 5.5 %order.1 = (s32[1032]{0:T(1024)S(1)}, s32[1032]{0:T(1024)S(1)}, s32[7]{0:T(128)S(1)}) custom-call(s32[1024]{0:T(1024)S(1)} %bitcast.45, s32[1024]{0:T(1024)S(1)} %bitcast.46, s32[1]{0:T(128)S(6)} %copy.27.count), custom_call_target="tpu_custom_call" | custom-call | tf_op jit(solution)/shard_map/order/pallas_call | solution.py:63
  36.2 5.8 %nodes.1 = (s32[32,16,128]{2,1,0:T(8,128)}, s32[64,128]{1,0:T(8,128)}, s32[64,128]{1,0:T(8,128)}, s32[64,128]{1,0:T(8,128)}, s32[64,128]{1,0:T(8,128)}, /*index=...) custom-call(s32[32,16,128]{2,1,0:T(8,128)S(1)} %all-to-all-done.slot, ...), custom_call_target="tpu_custom_call" | custom-call | tf_op jit(solution)/shard_map/nodes/pallas_call | solution.py:63
  42.6 24.1 %all-to-all-done.1.refs_1_ = f32[32,96,128]{2,1,0:T(8,128)} async-done(((f32[32,96,128]{2,1,0:T(8,128)}), f32[32,96,128]{2,1,0:T(8,128)}, u32[]{:S(2)}, u32[]{:S(2)}) %all-to-all-start.1) | async-done | bytes 1572896 | tf_op jit(solution)/shard_map/all_to_all | solution.py:976
  66.7 42.1 %scatter.1 = (f32[3072,128]{1,0:T(8,128)}, f32[4096,128]{1,0:T(8,128)}) custom-call(s32[32]{0:T(128)S(1)} %convert_reduce_fusion.1.refs_0_.counts, f32[32,96,128]{2,1,0:T(8,128)} %all-to-all-done.1.refs_1_, s32[8192]{0:T(1024)} %bitcast.67, s32[8192]{0:T(1024)} %bitcast.68, s32[8192]{0:T(1024)} %bitcast.69, s32[8192]{0:T(1024)} %bitcast.70, s32[8192]{0:T(1024)} %bitcast.71, ...), custom_call_target="tpu_custom_call" | custom-call | tf_op jit(solution)/shard_map/scatter/pallas_call | solution.py:63
  108.8 5.3 %depth.1 = (f32[8,16,1536]{2,1,0:T(8,128)}, f32[8,128]{1,0:T(8,128)}) custom-call(f32[3072,128]{1,0:T(8,128)} %get-tuple-element.70.refs_0_, f32[128,128]{1,0:T(8,128)} %constant.33.clone.refs_1_), custom_call_target="tpu_custom_call" | custom-call | tf_op jit(solution)/shard_map/depth/pallas_call | solution.py:63
  114.1 4.3 %all-to-all-start.2 = ((f32[8,16,1536]{2,1,0:T(8,128)}), f32[8,16,1536]{2,1,0:T(8,128)S(1)}, u32[]{:S(2)}, u32[]{:S(2)}) async-start(f32[8,16,1536]{2,1,0:T(8,128)} %get-tuple-element.62), calls=%async_computation.2 | async-start | bytes 1572864 | tf_op jit(solution)/shard_map/all_to_all | solution.py:934
  118.5 23.2 %within.4 = (f32[4096,128]{1,0:T(8,128)}, f32[8,128]{1,0:T(8,128)}) custom-call(s32[1032]{0:T(1024)S(1)} %get-tuple-element.47.refs_0_, s32[7]{0:T(128)S(1)} %get-tuple-element.48.refs_10_.refs_1_, f32[4096,128]{1,0:T(8,128)} %get-tuple-element.57.refs_2_, f32[8,128]{1,0:T(8,128)} %get-tuple-element.60.refs_3_), custom_call_target="tpu_custom_call" | custom-call | tf_op jit(solution)/shard_map/within/pallas_call | solution.py:63
  141.7 7.4 %first.1 = (f32[4,12,32,128]{3,2,1,0:T(8,128)}, f32[8,128]{1,0:T(8,128)}) custom-call(f32[128,1536]{1,0:T(8,128)S(1)} %bitcast.43, f32[128,256]{1,0:T(8,128)} %constant.34.clone.refs_1_, f32[8,128]{1,0:T(8,128)} %get-tuple-element.63.refs_2_), custom_call_target="tpu_custom_call" | custom-call | tf_op jit(solution)/shard_map/first/pallas_call | solution.py:63
  149.1 4.5 %all-to-all-start.3 = ((f32[4,384,128]{2,1,0:T(8,128)}), f32[4,384,128]{2,1,0:T(8,128)S(1)}, u32[]{:S(2)}, u32[]{:S(2)}) async-start(f32[4,384,128]{2,1,0:T(8,128)} %bitcast.52), calls=%async_computation.3 | async-start | bytes 1572864 | tf_op jit(solution)/shard_map/all_to_all | solution.py:934
  153.6 4.7 %collective-permute-start = (f32[3072,128]{1,0:T(8,128)}, f32[3072,128]{1,0:T(8,128)}, u32[]{:S(2)}, u32[]{:S(2)}) collective-permute-start(f32[3072,128]{1,0:T(8,128)} %get-tuple-element.70.refs_0_), channel_id=1, source_target_pairs={{0,28},{4,0},{8,4},{12,8},{16,12},{20,16},{24,20},{28,24},{1,29},{... | collective-permute-start | bytes 4718600 | tf_op jit(solution)/shard_map/ppermute | solution.py:30
  158.4 12.6 %within.5 = (f32[4096,128]{1,0:T(8,128)}, f32[8,128]{1,0:T(8,128)}) custom-call(s32[1032]{0:T(1024)S(1)} %get-tuple-element.47.refs_0_, s32[7]{0:T(128)S(1)} %get-tuple-element.48.refs_10_.refs_1_, f32[4096,128]{1,0:T(8,128)} %get-tuple-element.57.refs_2_, f32[4096,128]{1,0:T(8,128)} %get-tuple-element.61.refs_3_, f32[8,128]{1,0:T(8,128)} %get-tuple-element.64.refs_4_), custom_call_target="tpu_custom_call" | custom-call | tf_op jit(solution)/shard_map/within/pallas_call | solution.py:63
  171.0 6.1 %second.1 = (f32[4,12,32,128]{3,2,1,0:T(8,128)}, f32[8,128]{1,0:T(8,128)}) custom-call(s32[2]{0:T(128)S(1)} %pad_add_fusion.refs_0_, f32[4,12,32,128]{3,2,1,0:T(8,128)S(1)} %bitcast.44, f32[256,128]{1,0:T(8,128)} %constant.35.clone.refs_2_, f32[4,8,128]{2,1,0:T(8,128)} %constant.36.clone.refs_3_, f32[8,8,128]{2,1,0:T(8,128)} %constant.37.clone.refs_4_, ...), custom_call_target="tpu_custom_call" | custom-call | tf_op jit(solution)/shard_map/second/pallas_call | solution.py:63
  177.1 3.5 all-to-all-start.4
  180.6 3.7 %within.6 = (f32[4096,128]{1,0:T(8,128)}, f32[8,128]{1,0:T(8,128)}) custom-call(s32[1032]{0:T(1024)S(1)} %get-tuple-element.47.refs_0_, s32[7]{0:T(128)S(1)} %get-tuple-element.48.refs_10_.refs_1_, f32[4096,128]{1,0:T(8,128)} %get-tuple-element.57.refs_2_, f32[4096,128]{1,0:T(8,128)} %get-tuple-element.65.refs_3_, f32[8,128]{1,0:T(8,128)} %get-tuple-element.68.refs_4_), custom_call_target="tpu_custom_call" | custom-call | tf_op jit(solution)/shard_map/within/pallas_call | solution.py:63
  184.3 7.9 %all-to-all-done.4 = f32[4,384,128]{2,1,0:T(8,128)S(1)} async-done(((f32[4,384,128]{2,1,0:T(8,128)}), f32[4,384,128]{2,1,0:T(8,128)S(1)}, u32[]{:S(2)}, u32[]{:S(2)}) %all-to-all-start.4) | async-done | bytes 786464 | tf_op jit(solution)/shard_map/all_to_all | solution.py:934
  192.2 6.8 %first_back.1 = (f32[128,1536]{1,0:T(8,128)}, f32[8,128]{1,0:T(8,128)}) custom-call(f32[4,12,32,128]{3,2,1,0:T(8,128)S(1)} %bitcast.42, f32[128,256]{1,0:T(8,128)} %constant.34.clone.refs_1_, f32[8,128]{1,0:T(8,128)} %get-tuple-element.72.refs_2_), custom_call_target="tpu_custom_call" | custom-call | tf_op jit(solution)/shard_map/first_back/pallas_call | solution.py:63
  198.9 6.9 %all-to-all-start.5 = ((f32[8,16,1536]{2,1,0:T(8,128)}), f32[8,16,1536]{2,1,0:T(8,128)S(1)}, u32[]{:S(2)}, u32[]{:S(2)}) async-start(f32[8,16,1536]{2,1,0:T(8,128)} %bitcast.51), calls=%async_computation.5 | async-start | bytes 1572864 | tf_op jit(solution)/shard_map/all_to_all | solution.py:934
  205.8 28.5 %beyond.1 = (f32[4096,128]{1,0:T(8,128)}, f32[8,128]{1,0:T(8,128)}, f32[1536,128]{1,0:T(8,128)}) custom-call(s32[1032]{0:T(1024)S(1)} %get-tuple-element.58.refs_0_, s32[7]{0:T(128)S(1)} %get-tuple-element.48.refs_10_.refs_1_, f32[4096,128]{1,0:T(8,128)} %get-tuple-element.57.refs_2_, f32[4096,128]{1,0:T(8,128)} %get-tuple-element.69.refs_3_, ...), custom_call_target="tpu_custom_call" | custom-call | tf_op jit(solution)/shard_map/beyond/pallas_call | solution.py:63
  234.3 28.0 %collective-permute-start.1 = (f32[1536,128]{1,0:T(8,128)}, f32[1536,128]{1,0:T(8,128)}, u32[]{:S(2)}, u32[]{:S(2)}) collective-permute-start(f32[1536,128]{1,0:T(8,128)} %get-tuple-element.79), channel_id=1, source_target_pairs={{0,4},{4,8},{8,12},{12,16},{16,20},{20,24},{24,28},{28,0},{1,5},{5... | collective-permute-start | bytes 2359304 | tf_op jit(solution)/shard_map/ppermute | solution.py:30
  262.3 3.7 %within.7 = (f32[4096,128]{1,0:T(8,128)}, f32[8,128]{1,0:T(8,128)}) custom-call(s32[1032]{0:T(1024)S(1)} %get-tuple-element.47.refs_0_, s32[7]{0:T(128)S(1)} %get-tuple-element.48.refs_10_.refs_1_, f32[4096,128]{1,0:T(8,128)} %get-tuple-element.57.refs_2_, f32[4096,128]{1,0:T(8,128)} %get-tuple-element.74.refs_3_), custom_call_target="tpu_custom_call" | custom-call | tf_op jit(solution)/shard_map/within/pallas_call | solution.py:63
  266.0 5.1 %depth_back.1 = (f32[1536,128]{1,0:T(8,128)}, f32[8,128]{1,0:T(8,128)}) custom-call(f32[8,16,1536]{2,1,0:T(8,128)S(1)} %all-to-all-done.5.refs_0_, f32[128,128]{1,0:T(8,128)} %constant.39.clone.refs_1_, f32[8,128]{1,0:T(8,128)} %get-tuple-element.77.refs_2_), custom_call_target="tpu_custom_call" | custom-call | tf_op jit(solution)/shard_map/depth_back/pallas_call | solution.py:63
  271.0 13.4 %collective-permute-done.1.two_ref = f32[1536,128]{1,0:T(8,128)} collective-permute-done((f32[1536,128]{1,0:T(8,128)}, f32[1536,128]{1,0:T(8,128)}, u32[]{:S(2)}, u32[]{:S(2)}) %collective-permute-start.1) | collective-permute-done | bytes 786464 | tf_op jit(solution)/shard_map/ppermute | solution.py:30
  284.4 36.2 %gather.1 = f32[32,48,128]{2,1,0:T(8,128)} custom-call(s32[32]{0:T(128)S(1)} %convert_reduce_fusion.1.refs_0_.counts, s32[32,16,128]{2,1,0:T(8,128)} %get-tuple-element.46.node_ref, f32[4096,128]{1,0:T(8,128)} %get-tuple-element.75.sums_ref, f32[1536,128]{1,0:T(8,128)} %get-tuple-element.78.one_ref, f32[1536,128]{1,0:T(8,128)} %collective-permute-done.1.two_ref, ...), custom_call_target="tpu_custom_call" | custom-call | tf_op jit(solution)/shard_map/gather/pallas_call | solution.py:63
  320.7 6.6 %all-to-all-start.6 = ((f32[32,48,128]{2,1,0:T(8,128)}), f32[32,48,128]{2,1,0:T(8,128)S(1)}, u32[]{:S(2)}, u32[]{:S(2)}) async-start(f32[32,48,128]{2,1,0:T(8,128)} %gather.1), calls=%async_computation.6 | async-start | bytes 1572864 | tf_op jit(solution)/shard_map/all_to_all | solution.py:1008
  328.1 19.8 %all-to-all-done.6.in_ref = f32[32,48,128]{2,1,0:T(8,128)S(1)} async-done(((f32[32,48,128]{2,1,0:T(8,128)}), f32[32,48,128]{2,1,0:T(8,128)S(1)}, u32[]{:S(2)}, u32[]{:S(2)}) %all-to-all-start.6) | async-done | bytes 786464 | tf_op jit(solution)/shard_map/all_to_all | solution.py:1008
  347.9 4.8 %finish.1 = (f32[3,256,128]{2,1,0:T(8,128)}, f32[3,256,128]{2,1,0:T(8,128)}) custom-call(s32[33]{0:T(128)S(1)} %convert_reduce_fusion.starts, f32[32,48,128]{2,1,0:T(8,128)S(1)} %all-to-all-done.6.in_ref, f32[3,256,128]{2,1,0:T(8,128)} %bitcast.48, f32[3,256,128]{2,1,0:T(8,128)} %bitcast.49), custom_call_target="tpu_custom_call" | custom-call | tf_op jit(solution)/shard_map/finish/pallas_call | solution.py:63
  352.7 2.6 copy_bitcast_fusion
  (19 shorter events, 5.0 us)
Async XLA Ops:
  0.6 28.7 %copy-start = (s32[8,1,65536]{2,1,0:T(1,128)S(1)}, s32[8,1,65536]{2,1,0:T(1,128)}, u32[]{:S(2)}) copy-start(s32[8,1,65536]{2,1,0:T(1,128)} %param.18) | copy-start | bytes 6291460
  6.4 17.9 %all-to-all-start = ((s32[32,16,128]{2,1,0:T(8,128)}), s32[32,16,128]{2,1,0:T(8,128)S(1)}, u32[]{:S(2)}, u32[]{:S(2)}) async-start(s32[32,16,128]{2,1,0:T(8,128)} %slots.1), calls=%async_computation | async-start | bytes 524288 | tf_op jit(solution)/shard_map/all_to_all | solution.py:974
  23.3 7.4 %copy-start.1 = (s32[1,1024]{1,0:T(1,128)S(1)}, s32[1,1024]{1,0:T(1,128)}, u32[]{:S(2)}) copy-start(s32[1,1024]{1,0:T(1,128)} %param.19) | copy-start | bytes 12292
  23.3 7.4 %copy-start.2 = (s32[1,1024]{1,0:T(1,128)S(1)}, s32[1,1024]{1,0:T(1,128)}, u32[]{:S(2)}) copy-start(s32[1,1024]{1,0:T(1,128)} %param.20) | copy-start | bytes 12292
  24.3 42.4 %all-to-all-start.1 = ((f32[32,96,128]{2,1,0:T(8,128)}), f32[32,96,128]{2,1,0:T(8,128)}, u32[]{:S(2)}, u32[]{:S(2)}) async-start(f32[32,96,128]{2,1,0:T(8,128)} %pack.1), calls=%async_computation.1 | async-start | bytes 3145728 | tf_op jit(solution)/shard_map/all_to_all | solution.py:976
  114.1 27.6 %all-to-all-start.2 = ((f32[8,16,1536]{2,1,0:T(8,128)}), f32[8,16,1536]{2,1,0:T(8,128)S(1)}, u32[]{:S(2)}, u32[]{:S(2)}) async-start(f32[8,16,1536]{2,1,0:T(8,128)} %get-tuple-element.62), calls=%async_computation.2 | async-start | bytes 1572864 | tf_op jit(solution)/shard_map/all_to_all | solution.py:934
  149.1 21.8 %all-to-all-start.3 = ((f32[4,384,128]{2,1,0:T(8,128)}), f32[4,384,128]{2,1,0:T(8,128)S(1)}, u32[]{:S(2)}, u32[]{:S(2)}) async-start(f32[4,384,128]{2,1,0:T(8,128)} %bitcast.52), calls=%async_computation.3 | async-start | bytes 1572864 | tf_op jit(solution)/shard_map/all_to_all | solution.py:934
  153.6 52.2 %collective-permute-start = (f32[3072,128]{1,0:T(8,128)}, f32[3072,128]{1,0:T(8,128)}, u32[]{:S(2)}, u32[]{:S(2)}) collective-permute-start(f32[3072,128]{1,0:T(8,128)} %get-tuple-element.70.refs_0_), channel_id=1, source_target_pairs={{0,28},{4,0},{8,4},{12,8},{16,12},{20,16},{24,20},{28,24},{1,29},{... | collective-permute-start | bytes 4718600 | tf_op jit(solution)/shard_map/ppermute | solution.py:30
  177.1 15.1 %all-to-all-start.4 = ((f32[4,384,128]{2,1,0:T(8,128)}), f32[4,384,128]{2,1,0:T(8,128)S(1)}, u32[]{:S(2)}, u32[]{:S(2)}) async-start(f32[4,384,128]{2,1,0:T(8,128)} %bitcast.53), calls=%async_computation.4 | async-start | bytes 1572864 | tf_op jit(solution)/shard_map/all_to_all | solution.py:934
  198.9 67.0 %all-to-all-start.5 = ((f32[8,16,1536]{2,1,0:T(8,128)}), f32[8,16,1536]{2,1,0:T(8,128)S(1)}, u32[]{:S(2)}, u32[]{:S(2)}) async-start(f32[8,16,1536]{2,1,0:T(8,128)} %bitcast.51), calls=%async_computation.5 | async-start | bytes 1572864 | tf_op jit(solution)/shard_map/all_to_all | solution.py:934
  234.3 50.1 %collective-permute-start.1 = (f32[1536,128]{1,0:T(8,128)}, f32[1536,128]{1,0:T(8,128)}, u32[]{:S(2)}, u32[]{:S(2)}) collective-permute-start(f32[1536,128]{1,0:T(8,128)} %get-tuple-element.79), channel_id=1, source_target_pairs={{0,4},{4,8},{8,12},{12,16},{16,20},{20,24},{24,28},{28,0},{1,5},{5... | collective-permute-start | bytes 2359304 | tf_op jit(solution)/shard_map/ppermute | solution.py:30
  284.4 42.9 %copy-start.3 = (f32[3,32768]{1,0:T(4,128)S(1)}, f32[3,32768]{1,0:T(4,128)}, u32[]{:S(2)}) copy-start(f32[3,32768]{1,0:T(4,128)} %param.16) | copy-start | bytes 1179652
  320.7 27.2 %all-to-all-start.6 = ((f32[32,48,128]{2,1,0:T(8,128)}), f32[32,48,128]{2,1,0:T(8,128)S(1)}, u32[]{:S(2)}, u32[]{:S(2)}) async-start(f32[32,48,128]{2,1,0:T(8,128)} %gather.1), calls=%async_computation.6 | async-start | bytes 1572864 | tf_op jit(solution)/shard_map/all_to_all | solution.py:1008
